TPU v7x, 32 devices: a whole 2x2x4 slice. The times are simulated.
32 devices in a mesh: rep: 2 (over x), dp: 16 (over z, y, core).
Axes of the slice: x: 2, y: 2, z: 4, core: 2. Of those that a mesh axis runs over, the one named last changes fastest.
Arguments:
- hidden: bfloat16 [2, 2, 1, 1024, 768], P('rep', None, None, 'dp')
- bounds: int32 [2, 2, 1, 65], P('rep'), may hold values from 0 to 1024, as said below
- cotangent: bfloat16 [2, 2, 1, 1024, 768], P('rep', None, None, 'dp'), may hold values from -6 to 6
- weights: float32 [2, 9216, 768], P(None, 'dp')
- small_params: float32 [2, 9612], replicated
- first_big: float32 [2, 2, 9216, 768], P('rep', None, 'dp')
- second_big: float32 [2, 2, 9216, 768], P('rep', None, 'dp')
- first_small: float32 [2, 2, 9612], P('rep')
- second_small: float32 [2, 2, 9612], P('rep')
- outer_big: float32 [2, 9216, 768], P(None, 'dp'), may hold values from -0.012 to 0.012
- outer_small: float32 [2, 9612], replicated, may hold values from -0.06 to 0.06
Outputs:
- outputs: float32 [2, 2, 1, 1024, 768], P('rep', None, None, 'dp')
- input_grads: float32 [2, 2, 1, 1024, 768], P('rep', None, None, 'dp')
- first_big_new: float32 [2, 2, 9216, 768], P('rep', None, 'dp')
- second_big_new: float32 [2, 2, 9216, 768], P('rep', None, 'dp')
- first_small_new: float32 [2, 2, 9612], P('rep')
- second_small_new: float32 [2, 2, 9612], P('rep')
- outer_big_new: float32 [2, 9216, 768], P(None, 'dp')
- outer_small_new: float32 [2, 9612], replicated
- weights_new: float32 [2, 9216, 768], P(None, 'dp')
- small_new: float32 [2, 9612], replicated
- weights_low: bfloat16 [2, 9216, 768], P(None, 'dp')
Inputs may be any that keep to these rules, and one draw needn't show every extreme that they name: For each sequence bounds[..., 0] = 0, the entries rise strictly, every segment holds 2 or more positions, and bounds[..., 64] is the sequence's length, 256 or more; bounds[0, 0, 0, 64] = 1024.
All inputs are finite; a program needn't handle non-finite values.
Results may differ from a plain program's by a relative error of at most 0.025.
Values may be sent and summed in bfloat16 or wider, within the bound.
A program may use at most 512 MiB of HBM per device.

v0:
```python
import jax
import jax.numpy as jnp
from jax import lax
from jax.sharding import PartitionSpec as P

D = 768
HEADS = 12
FF = 3072
TAPS = 33
NS_ITERS = 6
LAYERS = 2
MICRO = 2
STEP_COUNT = 5


PRECISE = lax.Precision.HIGHEST
ADAM_ONE = 0.9
ADAM_TWO = 0.95
ADAM_EPSILON = 1e-08
WEIGHT_DECAY = 0.1
LR_INNER = 0.04
LR_SMALL = 0.2
LR_OUTER = 0.7
MOMENTUM = 0.9


def combined_all(array, axis, join):
    gathered = jax.tree.map(
        lambda a, kind: lax.all_gather(a.astype(kind), axis),
        array,
        (jnp.bfloat16, jnp.bfloat16, jnp.bfloat16),
    )

    def take(source):
        return jax.tree.map(
            lambda a, own: lax.dynamic_index_in_dim(a, source, 0, False).astype(own.dtype),
            gathered,
            array,
        )

    return lax.fori_loop(
        1, lax.axis_size(axis), lambda source, state: join(state, take(source)), take(0)
    )


def padded_2(array, sides, width):
    for axis, dim in sides:
        count, length = (lax.axis_size(axis), array.shape[dim])
        up = [(i, (i + 1) % count) for i in range(count - 1)]
        down = [(j, i) for i, j in up]
        last = lax.slice_in_dim(array, length - width, length, axis=dim)
        initial = lax.slice_in_dim(array, 0, width, axis=dim)
        before = lax.ppermute(last, axis, up)
        after = lax.ppermute(initial, axis, down)
        array = jnp.concatenate([before, array, after], axis=dim)
    return array


def exact_einsum(pattern, operand_one, operand_two):
    return jnp.einsum(pattern, operand_one, operand_two, precision=PRECISE)


def dense_einsum(pattern, operand_one, operand_two):
    return jnp.einsum(pattern, operand_one, operand_two, preferred_element_type=jnp.float32)


def layer_norm(values, gain_vec, shift_vec):
    row_mean = jnp.mean(values, axis=-1, keepdims=True)
    centred = values - row_mean
    variance = jnp.mean(centred * centred, axis=-1, keepdims=True)
    return centred * lax.rsqrt(variance + 1e-05) * gain_vec + shift_vec


def pseudo_inverse(matrix):
    scale_sum = jnp.sum(matrix * matrix, axis=(-2, -1), keepdims=True)
    approx = jnp.swapaxes(matrix, -1, -2) / scale_sum
    identity = jnp.eye(matrix.shape[-1], dtype=jnp.float32)
    for sweep_index in range(NS_ITERS):
        product = exact_einsum("...ij,...jk->...ik", matrix, approx)
        nested = 7.0 * identity - product
        nested = 15.0 * identity - exact_einsum("...ij,...jk->...ik", product, nested)
        nested = 13.0 * identity - exact_einsum("...ij,...jk->...ik", product, nested)
        approx = 0.25 * exact_einsum("...ij,...jk->...ik", approx, nested)
    return approx


def unpack(params):
    blocks = [params[index * D : (index + 1) * D] for index in range(8)]
    bias_up = params[8 * D : 8 * D + FF]
    conv_taps = params[8 * D + FF :].reshape(HEADS, TAPS)
    return (blocks, bias_up, conv_taps)


def split_rows(weight_rows):
    model_width = weight_rows.shape[1]
    proj_weight = weight_rows[0 : 3 * model_width].reshape(3, model_width, model_width)
    out_weight = weight_rows[3 * model_width : 4 * model_width]
    up_weight = weight_rows[4 * model_width : 4 * model_width + FF]
    down_weight = weight_rows[4 * model_width + FF :]
    return (proj_weight, out_weight, up_weight, down_weight)


def landmark_kernel(query_marks, key_marks):
    seq_count, mark_count, model_width = query_marks.shape
    head_dim = model_width // HEADS
    mark_queries = query_marks.reshape(seq_count, mark_count, HEADS, head_dim)
    mark_keys = key_marks.reshape(seq_count, mark_count, HEADS, head_dim)
    scores = head_dim ** (-0.5) * exact_einsum("sjhe,smhe->shjm", mark_queries, mark_keys)
    return pseudo_inverse(jax.nn.softmax(scores, axis=-1))


def token_mixing(queries, key_marks, mixed_marks):
    seq_count, length, model_width = queries.shape
    head_dim = model_width // HEADS
    query_heads = queries.reshape(seq_count, length, HEADS, head_dim)
    mark_keys = key_marks.reshape(seq_count, key_marks.shape[1], HEADS, head_dim)
    token_weights = jax.nn.softmax(
        head_dim ** (-0.5) * exact_einsum("sthe,smhe->shtm", query_heads, mark_keys), axis=-1
    )
    return exact_einsum("shtm,shme->sthe", token_weights, mixed_marks).reshape(
        seq_count, length, model_width
    )


def key_partial(query_marks, keys_all, values, valid_mask):
    seq_count, length, model_width = keys_all.shape
    head_dim = model_width // HEADS
    mark_queries = query_marks.reshape(seq_count, query_marks.shape[1], HEADS, head_dim)
    key_heads = keys_all.reshape(seq_count, length, HEADS, head_dim)
    value_heads = values.reshape(seq_count, length, HEADS, head_dim)
    scores = head_dim ** (-0.5) * exact_einsum("sjhe,sthe->shjt", mark_queries, key_heads)
    scores = jnp.where(valid_mask[:, None, None, :] > 0, scores, -1e30)
    local_top = jnp.max(scores, axis=-1)
    expo = jnp.exp(scores - local_top[..., None]) * valid_mask[:, None, None, :]
    local_total = jnp.sum(expo, axis=-1)
    local_weighted = exact_einsum("shjt,sthe->shje", expo, value_heads)
    return (local_top, local_total, local_weighted)


def merge_keys(first_part, second_part):
    joint_top = jnp.maximum(first_part[0], second_part[0])
    scale_one = jnp.exp(first_part[0] - joint_top)
    scale_two = jnp.exp(second_part[0] - joint_top)
    joint_total = first_part[1] * scale_one + second_part[1] * scale_two
    joint_weighted = first_part[2] * scale_one[..., None] + second_part[2] * scale_two[..., None]
    return (joint_top, joint_total, joint_weighted)


def depth_conv(padded, conv_taps, length):
    result = conv_taps[:, 0][None, None, :, None] * padded[:, 0:length]
    for offset in range(1, conv_taps.shape[1]):
        result = (
            result + conv_taps[:, offset][None, None, :, None] * padded[:, offset : offset + length]
        )
    return result


def conv_back(grad_padded, conv_taps, length):
    twice_half = conv_taps.shape[1] - 1
    result = conv_taps[:, 0][None, None, :, None] * grad_padded[:, twice_half : twice_half + length]
    for offset in range(1, conv_taps.shape[1]):
        start_at = twice_half - offset
        result = (
            result
            + conv_taps[:, offset][None, None, :, None]
            * grad_padded[:, start_at : start_at + length]
        )
    return result


def forward_layer(inputs, weight_rows, params, member, counts, valid_mask):
    seq_count, length, model_width = inputs.shape
    head_dim = model_width // HEADS
    blocks, bias_up, conv_taps = unpack(params)
    proj_weight, out_weight, up_weight, down_weight = split_rows(weight_rows)
    low_in = inputs.astype(jnp.bfloat16)
    projected = dense_einsum("spd,kde->kspe", low_in, proj_weight)
    queries = projected[0] + blocks[0]
    keys_all = projected[1]
    values = projected[2] + blocks[1]
    query_sums, key_sums = lax.psum(
        (
            exact_einsum("spm,spe->sme", member, queries),
            exact_einsum("spm,spe->sme", member, keys_all),
        ),
        "dp",
    )
    query_marks = query_sums / counts[:, :, None]
    key_marks = key_sums / counts[:, :, None]
    inverse = landmark_kernel(query_marks, key_marks)
    local_top, local_total, local_weighted = key_partial(query_marks, keys_all, values, valid_mask)
    key_top, key_total, key_weighted = combined_all(
        (local_top, local_total, local_weighted), "dp", merge_keys
    )
    summary = key_weighted / key_total[..., None]
    mixed_marks = exact_einsum("shij,shje->shie", inverse, summary)
    attended = token_mixing(queries, key_marks, mixed_marks)
    half_width = TAPS // 2
    rimmed = padded_2(
        (values * valid_mask[:, :, None]).astype(jnp.bfloat16), (("dp", 1),), half_width
    ).astype(jnp.float32)
    rim_heads = rimmed.reshape(seq_count, length + 2 * half_width, HEADS, head_dim)
    conv_out = depth_conv(rim_heads, conv_taps, length).reshape(seq_count, length, model_width)
    low_comb = (attended + conv_out).astype(jnp.bfloat16)
    branch = dense_einsum("spd,de->spe", low_comb, out_weight) + blocks[2]
    resid_one = inputs + branch
    hidden_one = layer_norm(resid_one, blocks[4], blocks[5])
    low_hidden = hidden_one.astype(jnp.bfloat16)
    upward = dense_einsum("spd,fd->spf", low_hidden, up_weight) + bias_up
    low_act = jax.nn.gelu(upward).astype(jnp.bfloat16)
    down_out = dense_einsum("spf,fd->spd", low_act, down_weight) + blocks[3]
    resid_two = hidden_one + down_out
    output = layer_norm(resid_two, blocks[6], blocks[7])
    kept_state = (
        low_in,
        queries,
        keys_all,
        values,
        query_marks,
        key_marks,
        inverse,
        key_top,
        key_total,
        summary,
        mixed_marks,
        rimmed,
        low_comb,
        resid_one,
        low_hidden,
        upward,
        low_act,
        resid_two,
    )
    return (output, kept_state)


def backward_layer(grad_output, weight_rows, params, member, counts, valid_mask, kept_state):
    (
        low_in,
        queries,
        keys_all,
        values,
        query_marks,
        key_marks,
        inverse,
        key_top,
        key_total,
        summary,
        mixed_marks,
        rimmed,
        low_comb,
        resid_one,
        low_hidden,
        upward,
        low_act,
        resid_two,
    ) = kept_state
    seq_count, length, model_width = queries.shape
    head_dim = model_width // HEADS
    scale = head_dim ** (-0.5)
    blocks, bias_up, conv_taps = unpack(params)
    proj_weight, out_weight, up_weight, down_weight = split_rows(weight_rows)
    unused_two, pull_two = jax.vjp(layer_norm, resid_two, blocks[6], blocks[7])
    grad_resid_two, grad_gain_two, grad_shift_two = pull_two(grad_output)
    low_grad_down = grad_resid_two.astype(jnp.bfloat16)
    grad_bias_down = jnp.sum(low_grad_down.astype(jnp.float32), axis=(0, 1))
    grad_down = dense_einsum("spf,spd->fd", low_act, low_grad_down)
    grad_act = dense_einsum("spd,fd->spf", low_grad_down, down_weight)
    unused_gelu, pull_gelu = jax.vjp(jax.nn.gelu, upward)
    low_grad_up = pull_gelu(grad_act)[0].astype(jnp.bfloat16)
    grad_bias_up = jnp.sum(low_grad_up.astype(jnp.float32), axis=(0, 1))
    grad_up = dense_einsum("spf,spd->fd", low_grad_up, low_hidden)
    grad_hidden = grad_resid_two + dense_einsum("spf,fd->spd", low_grad_up, up_weight)
    unused_one, pull_one = jax.vjp(layer_norm, resid_one, blocks[4], blocks[5])
    grad_resid_one, grad_gain_one, grad_shift_one = pull_one(grad_hidden)
    low_grad_branch = grad_resid_one.astype(jnp.bfloat16)
    grad_bias_out = jnp.sum(low_grad_branch.astype(jnp.float32), axis=(0, 1))
    grad_out_weight = dense_einsum("spd,spe->de", low_comb, low_grad_branch)
    grad_comb = dense_einsum("spe,de->spd", low_grad_branch, out_weight)
    half_width = TAPS // 2
    grad_rim = padded_2(grad_comb.astype(jnp.bfloat16), (("dp", 1),), half_width).astype(
        grad_comb.dtype
    )
    grad_heads = grad_comb.reshape(seq_count, length, HEADS, head_dim)
    rim_heads = rimmed.reshape(seq_count, length + 2 * half_width, HEADS, head_dim)
    grad_masked = conv_back(
        grad_rim.reshape(seq_count, length + 2 * half_width, HEADS, head_dim), conv_taps, length
    )
    grad_taps = jnp.stack(
        [
            jnp.sum(grad_heads * rim_heads[:, offset : offset + length], axis=(0, 1, 3))
            for offset in range(TAPS)
        ],
        axis=1,
    )
    grad_values = grad_masked.reshape(seq_count, length, model_width) * valid_mask[:, :, None]
    unused_mix, pull_mix = jax.vjp(token_mixing, queries, key_marks, mixed_marks)
    grad_queries, grad_keymark_part, grad_mixed_part = pull_mix(grad_comb)
    grad_mixed, grad_keymark_tok = lax.psum((grad_mixed_part, grad_keymark_part), "dp")
    grad_inverse = exact_einsum("shie,shje->shij", grad_mixed, summary)
    grad_summary = exact_einsum("shij,shie->shje", inverse, grad_mixed)
    unused_kernel, pull_kernel = jax.vjp(landmark_kernel, query_marks, key_marks)
    grad_qmark_kernel, grad_kmark_kernel = pull_kernel(grad_inverse)
    mark_queries = query_marks.reshape(seq_count, query_marks.shape[1], HEADS, head_dim)
    key_heads = keys_all.reshape(seq_count, length, HEADS, head_dim)
    value_heads = values.reshape(seq_count, length, HEADS, head_dim)
    key_scores = scale * exact_einsum("sjhe,sthe->shjt", mark_queries, key_heads)
    key_scores = jnp.where(valid_mask[:, None, None, :] > 0, key_scores, -1e30)
    key_probs = jnp.exp(key_scores - key_top[..., None]) / key_total[..., None]
    grad_values = grad_values + exact_einsum("shjt,shje->sthe", key_probs, grad_summary).reshape(
        seq_count, length, model_width
    )
    grad_probs = exact_einsum("shje,sthe->shjt", grad_summary, value_heads)
    grad_scores = key_probs * (grad_probs - jnp.sum(grad_summary * summary, axis=-1)[..., None])
    grad_keys = scale * exact_einsum("shjt,sjhe->sthe", grad_scores, mark_queries).reshape(
        seq_count, length, model_width
    )
    grad_qmark_part = scale * exact_einsum("shjt,sthe->sjhe", grad_scores, key_heads).reshape(
        seq_count, query_marks.shape[1], model_width
    )
    grad_qmark_keys = lax.psum(grad_qmark_part, "dp")
    grad_qmark = grad_qmark_kernel + grad_qmark_keys
    grad_kmark = grad_kmark_kernel + grad_keymark_tok
    grad_queries = grad_queries + exact_einsum(
        "spm,sme->spe", member, grad_qmark / counts[:, :, None]
    )
    grad_keys = grad_keys + exact_einsum("spm,sme->spe", member, grad_kmark / counts[:, :, None])
    low_grads = jnp.stack([grad_queries, grad_keys, grad_values]).astype(jnp.bfloat16)
    grad_bias_q = jnp.sum(low_grads[0].astype(jnp.float32), axis=(0, 1))
    grad_bias_v = jnp.sum(low_grads[2].astype(jnp.float32), axis=(0, 1))
    grad_project = dense_einsum("spd,kspe->kde", low_in, low_grads)
    grad_in = grad_resid_one + dense_einsum("kspe,kde->spd", low_grads, proj_weight)
    grad_rows = jnp.concatenate(
        [grad_project.reshape(3 * model_width, model_width), grad_out_weight, grad_up, grad_down],
        axis=0,
    )
    grad_small = jnp.concatenate(
        [
            grad_bias_q,
            grad_bias_v,
            grad_bias_out,
            grad_bias_down,
            grad_gain_one,
            grad_shift_one,
            grad_gain_two,
            grad_shift_two,
            grad_bias_up,
            grad_taps.reshape(-1),
        ]
    )
    return (grad_in, grad_rows, grad_small)


def shards(
    hidden,
    bounds,
    cotangent,
    weights,
    small_params,
    first_big,
    second_big,
    first_small,
    second_small,
    outer_big,
    outer_small,
):
    piece_len = hidden.shape[3]
    positions = lax.axis_index("dp") * piece_len + jnp.arange(piece_len, dtype=jnp.int32)
    held_rows = []
    for level_index in range(LAYERS):
        held_rows.append(
            lax.all_gather(weights[level_index].astype(jnp.bfloat16), "dp", axis=0, tiled=True)
        )
    grad_parts = [jnp.zeros(weights.shape[1:], jnp.float32) for level_index in range(LAYERS)]
    grad_whole = [None for level_index in range(LAYERS)]
    small_parts = [jnp.zeros(small_params.shape[1:], jnp.float32) for level_index in range(LAYERS)]
    batch_outputs, batch_grads = ([], [])
    for micro_index in range(MICRO):
        bounds_row = bounds[0, micro_index]
        member = (
            (bounds_row[:, None, :-1] <= positions[None, :, None])
            & (positions[None, :, None] < bounds_row[:, None, 1:])
        ).astype(jnp.float32)
        counts = (bounds_row[:, 1:] - bounds_row[:, :-1]).astype(jnp.float32)
        valid_mask = (positions[None, :] < bounds_row[:, -1:]).astype(jnp.float32)
        activation = hidden[0, micro_index].astype(jnp.float32)
        kept_levels = []
        for level_index in range(LAYERS):
            weight_rows = held_rows[level_index]
            activation, kept_state = forward_layer(
                activation, weight_rows, small_params[level_index], member, counts, valid_mask
            )
            kept_levels.append(kept_state)
        batch_outputs.append(activation)
        gradient = cotangent[0, micro_index].astype(jnp.float32) * valid_mask[:, :, None]
        for level_index in reversed(range(LAYERS)):
            weight_rows = held_rows[level_index]
            gradient, grad_rows, grad_small = backward_layer(
                gradient,
                weight_rows,
                small_params[level_index],
                member,
                counts,
                valid_mask,
                kept_levels[level_index],
            )
            small_parts[level_index] = small_parts[level_index] + grad_small
            grad_whole[level_index] = (
                grad_rows if micro_index == 0 else grad_whole[level_index] + grad_rows
            )
        batch_grads.append(gradient)
    for level_index in range(LAYERS):
        grad_parts[level_index] = lax.psum_scatter(
            grad_whole[level_index], "dp", scatter_dimension=0, tiled=True
        )
    grad_big = jnp.stack(grad_parts)
    grad_small_all = lax.psum(jnp.stack(small_parts), "dp")
    correct_one = 1.0 - ADAM_ONE**STEP_COUNT
    correct_two = 1.0 - ADAM_TWO**STEP_COUNT
    new_first = ADAM_ONE * first_big[0] + (1.0 - ADAM_ONE) * grad_big
    new_second = ADAM_TWO * second_big[0] + (1.0 - ADAM_TWO) * grad_big * grad_big
    inner_big = weights - LR_INNER * (
        new_first / correct_one / (jnp.sqrt(new_second / correct_two) + ADAM_EPSILON)
        + WEIGHT_DECAY * weights
    )
    delta_big = weights - inner_big
    new_first_small = ADAM_ONE * first_small[0] + (1.0 - ADAM_ONE) * grad_small_all
    new_second_small = (
        ADAM_TWO * second_small[0] + (1.0 - ADAM_TWO) * grad_small_all * grad_small_all
    )
    inner_small = small_params - LR_SMALL * (
        new_first_small / correct_one / (jnp.sqrt(new_second_small / correct_two) + ADAM_EPSILON)
    )
    delta_small = small_params - inner_small
    total_big, total_small = (
        lax.psum(delta_big.astype(jnp.bfloat16), "rep").astype(jnp.float32),
        lax.psum(delta_small.astype(jnp.bfloat16), "rep").astype(jnp.float32),
    )
    mean_big = total_big / lax.axis_size("rep")
    mean_small = total_small / lax.axis_size("rep")
    outer_big_new = MOMENTUM * outer_big + mean_big
    outer_small_new = MOMENTUM * outer_small + mean_small
    weights_new = weights - LR_OUTER * (mean_big + MOMENTUM * outer_big_new)
    small_new = small_params - LR_OUTER * (mean_small + MOMENTUM * outer_small_new)
    return (
        jnp.stack(batch_outputs)[None],
        jnp.stack(batch_grads)[None],
        new_first[None],
        new_second[None],
        new_first_small[None],
        new_second_small[None],
        outer_big_new,
        outer_small_new,
        weights_new,
        small_new,
        weights_new.astype(jnp.bfloat16),
    )


def solution(mesh):
    placed = (
        P("rep", None, None, "dp", None),
        P("rep", None, None, None),
        P("rep", None, None, "dp", None),
        P(None, "dp", None),
        P(),
        P("rep", None, "dp", None),
        P("rep", None, "dp", None),
        P("rep", None, None),
        P("rep", None, None),
        P(None, "dp", None),
        P(),
    )
    return jax.shard_map(
        shards,
        mesh=mesh,
        in_specs=placed,
        out_specs=(
            P("rep", None, None, "dp", None),
            P("rep", None, None, "dp", None),
            P("rep", None, "dp", None),
            P("rep", None, "dp", None),
            P("rep", None, None),
            P("rep", None, None),
            P(None, "dp", None),
            P(),
            P(None, "dp", None),
            P(),
            P(None, "dp", None),
        ),
        check_vma=False,
    )
```

profile of v0, /device:TPU:0, one launch (start us, length us, event | category | flops | bytes accessed | tf_op | source)
XLA Modules:
  0.0 2555.5 jit_solution(3441105038666183661)
XLA Ops:
  63.0 60.9 %all-gather.29.cloned.1.call-done = bf16[1,9216,768]{2,1,0:T(8,128)(2,1)} async-done(((bf16[1,576,768]{2,1,0:T(8,128)(2,1)}), bf16[1,9216,768]{2,1,0:T(8,128)(2,1)}) %all-gather.29.cloned.1.call-update) | async-done | bytes 14155792 | tf_op jit(solution)/shard_map/all_gather | solution.py:372
  157.5 78.0 %all-gather.33.cloned.1.call-done = bf16[1,9216,768]{2,1,0:T(8,128)(2,1)} async-done(((bf16[1,576,768]{2,1,0:T(8,128)(2,1)}), bf16[1,9216,768]{2,1,0:T(8,128)(2,1)}) %all-gather.33.cloned.1.call-update) | async-done | bytes 14155792 | tf_op jit(solution)/shard_map/all_gather | solution.py:372
  240.6 91.2 %all-reduce.30.cloned.1.call-done = (f32[1,64,768]{2,1,0:T(8,128)}, f32[1,64,768]{2,1,0:T(8,128)}, f32[1,64,768]{2,1,0:T(8,128)}, f32[1,64,768]{2,1,0:T(8,128)}) async-done(((f32[1,64,768]{2,1,0:T(8,128)}, f32[1,64,768]{2,1,0:T(8,128)}, f32[1,64,768]{2,1,0:T(8,128)}, f32[1,64,768]{2,1,0:T(8,128)}), (f32[1,64,768]{2,1,0:T(8,128)}, f32[1,64,768]{2,1,0:T(8,128)}, f32[1,64,768]{2,1,0:T(8,128)}, ...) | async-done | bytes 786448 | tf_op jit(solution)/shard_map/psum | solution.py:181
  371.3 19.5 all-gather.18
  390.8 17.6 all-gather.19
  423.6 19.4 all-gather.14
  443.0 17.9 all-gather.15
  476.8 41.7 %while.78 = (s32[]{:T(128)}, f32[1,12,64]{2,1,0:T(8,128)S(1)}, f32[1,12,64]{2,1,0:T(8,128)S(1)}, f32[1,12,64,64]{3,2,1,0:T(8,128)S(1)}, bf16[16,1,12,64]{3,2,1,0...) while((s32[]{:T(128)}, f32[1,12,64]{2,1,0:T(8,128)S(1)}, ...), condition=%wide.region_38.39_spmd, body=%wide.region_37.38_spmd.sunk | while | flops 204293 | bytes 533147 | solution.py:41
  519.7 5.7 fusion.287
  539.8 21.0 while.76
  562.7 4.7 fusion.289
  595.3 92.4 %all-reduce.28.cloned.1.call-done = (f32[1,64,768]{2,1,0:T(8,128)}, f32[1,64,768]{2,1,0:T(8,128)}, f32[1,64,768]{2,1,0:T(8,128)}, f32[1,64,768]{2,1,0:T(8,128)}) async-done(((f32[1,64,768]{2,1,0:T(8,128)}, f32[1,64,768]{2,1,0:T(8,128)}, f32[1,64,768]{2,1,0:T(8,128)}, f32[1,64,768]{2,1,0:T(8,128)}), (f32[1,64,768]{2,1,0:T(8,128)}, f32[1,64,768]{2,1,0:T(8,128)}, f32[1,64,768]{2,1,0:T(8,128)}, ...) | async-done | bytes 786448 | tf_op jit(solution)/shard_map/psum | solution.py:181
  730.2 19.9 all-gather.16
  750.1 17.6 all-gather.17
  784.7 19.5 all-gather.20
  804.1 18.1 all-gather.21
  837.2 41.7 %while.77 = (s32[]{:T(128)}, f32[1,12,64]{2,1,0:T(8,128)S(1)}, f32[1,12,64]{2,1,0:T(8,128)S(1)}, f32[1,12,64,64]{3,2,1,0:T(8,128)S(1)}, bf16[16,1,12,64]{3,2,1,0...) while((s32[]{:T(128)}, f32[1,12,64]{2,1,0:T(8,128)S(1)}, ...), condition=%wide.region_23.24_spmd, body=%wide.region_22.23_spmd.sunk | while | flops 204293 | bytes 533147 | solution.py:41
  881.8 5.7 fusion.288
  899.0 31.7 %while.79 = (s32[]{:T(128)}, f32[1,12,64]{2,1,0:T(8,128)S(1)}, f32[1,12,64]{2,1,0:T(8,128)S(1)}, f32[1,12,64,64]{3,2,1,0:T(8,128)S(1)}, bf16[16,1,12,64]{3,2,1,0...) while((s32[]{:T(128)}, f32[1,12,64]{2,1,0:T(8,128)S(1)}, ...), condition=%wide.region_53.54_spmd, body=%wide.region_52.53_spmd.sunk | while | flops 204293 | bytes 533147 | solution.py:41
  933.5 5.7 fusion.286
  990.8 5.0 fusion.895
  995.9 5.1 fusion.860
  1002.9 5.0 fusion.897
  1007.9 5.0 fusion.854
  1085.3 4.8 fusion.436
  1091.9 4.9 fusion.500
  1097.6 79.6 %all-reduce.26.cloned.1.call-done = (f32[12,64,64]{1,2,0:T(8,128)}, f32[12,64,64]{1,2,0:T(8,128)}) async-done(((f32[12,64,64]{1,2,0:T(8,128)}, f32[12,64,64]{1,2,0:T(8,128)}), (f32[12,64,64]{1,2,0:T(8,128)}, f32[12,64,64]{1,2,0:T(8,128)})) %all-reduce.26.cloned.1.call-update) | async-done | bytes 393232 | tf_op jit(solution)/shard_map/psum | solution.py:299
  1310.6 87.5 %all-reduce.24.cloned.1.call-done = (f32[1,64,768]{2,1,0:T(8,128)}, f32[1,64,768]{2,1,0:T(8,128)}, f32[1,64,768]{2,1,0:T(8,128)}, f32[1,64,768]{2,1,0:T(8,128)}) async-done(((f32[1,64,768]{2,1,0:T(8,128)}, f32[1,64,768]{2,1,0:T(8,128)}, f32[1,64,768]{2,1,0:T(8,128)}, f32[1,64,768]{2,1,0:T(8,128)}), (f32[1,64,768]{2,1,0:T(8,128)}, f32[1,64,768]{2,1,0:T(8,128)}, f32[1,64,768]{2,1,0:T(8,128)}, ...) | async-done | bytes 786448 | tf_op jit(solution)/shard_map/psum | solution.py:299
  1419.4 4.7 convert_reduce_fusion.3
  1511.0 5.0 fusion.404
  1517.5 4.9 fusion.468
  1523.3 77.2 %all-reduce.22.cloned.1.call-done = (f32[12,64,64]{1,2,0:T(8,128)}, f32[12,64,64]{1,2,0:T(8,128)}) async-done(((f32[12,64,64]{1,2,0:T(8,128)}, f32[12,64,64]{1,2,0:T(8,128)}), (f32[12,64,64]{1,2,0:T(8,128)}, f32[12,64,64]{1,2,0:T(8,128)})) %all-reduce.22.cloned.1.call-update) | async-done | bytes 393232 | tf_op jit(solution)/shard_map/psum | solution.py:299
  1731.3 89.0 %all-reduce.20.cloned.1.call-done = (f32[1,64,768]{2,1,0:T(8,128)}, f32[1,64,768]{2,1,0:T(8,128)}) async-done(((f32[1,64,768]{2,1,0:T(8,128)}, f32[1,64,768]{2,1,0:T(8,128)}), (f32[1,64,768]{2,1,0:T(8,128)}, f32[1,64,768]{2,1,0:T(8,128)})) %all-reduce.20.cloned.1.call-update) | async-done | bytes 393232 | tf_op jit(solution)/shard_map/psum | solution.py:321
  1837.9 34.8 %maximum_add_fusion.1 = f32[9216,768]{1,0:T(8,128)} fusion(f32[3072,768]{1,0:T(8,128)} %fusion.895, f32[3072,768]{1,0:T(8,128)} %fusion.860, f32[768,768]{1,0:T(8,128)S(1)} %copy-done.51, f32[2304,768]{1,0:T(8,128)} %bitcast.2742, f32[3072,768]{1,0:T(8,128)} %fusion.897, f32[3072,768]{1,0:T(8,128)} %fusion.854, f32[768,768]{1,0:T(8,128)} %fusion.1062, ...), kind=kLoop, calls=%fused_computation.41 | loop fusion | flops 49545216 | bytes 84934656 | tf_op jit(solution)/shard_map/add | solution.py:409
  1877.9 5.0 fusion.863
  1882.9 5.1 fusion.857
  1888.1 5.1 fusion.894
  1893.2 5.0 fusion.896
  1910.5 17.9 all-reduce.18.cloned.1.call-done
  1935.6 4.6 fusion.780
  1940.3 40.2 %maximum_add_fusion = f32[9216,768]{1,0:T(8,128)} fusion(f32[3072,768]{1,0:T(8,128)} %fusion.894, f32[3072,768]{1,0:T(8,128)} %fusion.863, f32[768,768]{1,0:T(8,128)S(1)} %fusion.1059, f32[2304,768]{1,0:T(8,128)} %bitcast.2744, f32[3072,768]{1,0:T(8,128)} %fusion.896, f32[3072,768]{1,0:T(8,128)} %fusion.857, f32[768,768]{1,0:T(8,128)} %fusion.1060, ...), kind=kLoop, calls=%fused_computation.40 | loop fusion | flops 49545216 | bytes 84934656 | tf_op jit(solution)/shard_map/add | solution.py:409
  1984.9 9.0 psum.183
  1999.3 204.8 %reduce-scatter.5.cloned.1.call-done = f32[576,768]{1,0:T(8,128)} async-done(((f32[9216,768]{1,0:T(8,128)}), f32[576,768]{1,0:T(8,128)}) %reduce-scatter.5.cloned.1.call-update) | async-done | bytes 1769488 | tf_op jit(solution)/shard_map/reduce_scatter | solution.py:413
  2204.1 274.9 %reduce-scatter.3.cloned.1.call-done = f32[576,768]{1,0:T(8,128)} async-done(((f32[9216,768]{1,0:T(8,128)}), f32[576,768]{1,0:T(8,128)}) %reduce-scatter.3.cloned.1.call-update) | async-done | bytes 1769488 | tf_op jit(solution)/shard_map/reduce_scatter | solution.py:413
  2479.1 7.6 fusion.27
  2487.5 8.6 fusion.20
  2496.1 45.6 %all-reduce.16.cloned.1.call-done = bf16[2,576,768]{2,1,0:T(8,128)(2,1)} async-done(((bf16[2,576,768]{2,1,0:T(8,128)(2,1)}), bf16[2,576,768]{2,1,0:T(8,128)(2,1)}) %all-reduce.16.cloned.1.call-update) | async-done | bytes 1769488 | tf_op jit(solution)/shard_map/psum | solution.py:436
  2541.7 7.1 fusion.978
  (2732 shorter events, 978.5 us)
Async XLA Ops:
  7.2 116.6 %all-gather.29.cloned.1.call-start = ((), (), s32[]{:S(2)}) async-start(), calls=%async_computation.5 | async-start | bytes 15040512 | tf_op jit(solution)/shard_map/all_gather | solution.py:372
  10.8 224.7 %all-gather.33.cloned.1.call-start = ((), (), s32[]{:S(2)}) async-start(), calls=%async_computation.7 | async-start | bytes 15040512 | tf_op jit(solution)/shard_map/all_gather | solution.py:372
  11.5 320.3 %all-reduce.30.cloned.1.call-start = ((), (), s32[]{:S(2)}) async-start(), calls=%async_computation.17 | async-start | bytes 1572864 | tf_op jit(solution)/shard_map/psum | solution.py:181
  13.5 326.4 %copy-start.415 = (f32[12,64]{1,0:T(8,128)}, f32[12,64]{1,0:T(8,128)S(1)}, u32[]{:S(2)}) copy-start(f32[12,64]{1,0:T(8,128)S(1)} %add.1917) | copy-start | bytes 9220
  135.1 104.4 %collective-permute-start.5 = (bf16[1,16,768]{2,1,0:T(8,128)(2,1)S(1)}, bf16[1,16,768]{2,1,0:T(8,128)(2,1)S(1)}, u32[]{:S(2)}, u32[]{:S(2)}) collective-permute-start(bf16[1,16,768]{2,1,0:T(8,128)(2,1)S(1)} %get-tuple-element.1209), channel_id=1, source_target_pairs={{1,0},{2,1},{3,2},{4,3},{5,4},{6,5},{7,6},{8,7},{9,8},{10,9},{11,1... | collective-permute-start | bytes 73736 | tf_op jit(solution)/shard_map/ppermute | solution.py:54
  136.8 203.1 %copy-start.114 = (f32[1,1,64,768]{2,3,1,0:T(8,128)}, f32[1,1,64,768]{2,3,1,0:T(8,128)S(1)}, u32[]{:S(2)}) copy-start(f32[1,1,64,768]{2,3,1,0:T(8,128)S(1)} %copy.1720) | copy-start | bytes 589828
  136.8 102.9 %collective-permute-start.4 = (bf16[1,16,768]{2,1,0:T(8,128)(2,1)S(1)}, bf16[1,16,768]{2,1,0:T(8,128)(2,1)S(1)}, u32[]{:S(2)}, u32[]{:S(2)}) collective-permute-start(bf16[1,16,768]{2,1,0:T(8,128)(2,1)S(1)} %get-tuple-element.1208), channel_id=1, source_target_pairs={{0,1},{1,2},{2,3},{3,4},{4,5},{5,6},{6,7},{7,8},{8,9},{9,10},{10,1... | collective-permute-start | bytes 73736 | tf_op jit(solution)/shard_map/ppermute | solution.py:53
  141.6 98.3 %collective-permute-start.1 = (bf16[1,16,768]{2,1,0:T(8,128)(2,1)}, bf16[1,16,768]{2,1,0:T(8,128)(2,1)S(1)}, u32[]{:S(2)}, u32[]{:S(2)}) collective-permute-start(bf16[1,16,768]{2,1,0:T(8,128)(2,1)} %get-tuple-element.1207), channel_id=1, source_target_pairs={{1,0},{2,1},{3,2},{4,3},{5,4},{6,5},{7,6},{8,7},{9,8},{10,9},{11,1... | collective-permute-start | bytes 73736 | tf_op jit(solution)/shard_map/ppermute | solution.py:54
  142.9 97.2 %collective-permute-start = (bf16[1,16,768]{2,1,0:T(8,128)(2,1)}, bf16[1,16,768]{2,1,0:T(8,128)(2,1)S(1)}, u32[]{:S(2)}, u32[]{:S(2)}) collective-permute-start(bf16[1,16,768]{2,1,0:T(8,128)(2,1)} %get-tuple-element.1206), channel_id=1, source_target_pairs={{0,1},{1,2},{2,3},{3,4},{4,5},{5,6},{6,7},{7,8},{8,9},{9,10},{10,1... | collective-permute-start | bytes 73736 | tf_op jit(solution)/shard_map/ppermute | solution.py:53
  156.0 319.9 %all-gather.37.cloned.1.call-start = ((), (), s32[]{:S(2)}) async-start(), calls=%async_computation.9 | async-start | bytes 3342336 | tf_op jit(solution)/shard_map/all_gather | solution.py:29
  157.3 175.8 %copy-start.178 = (f32[1,1,64,768]{2,3,1,0:T(8,128)}, f32[1,1,64,768]{2,3,1,0:T(8,128)S(1)}, u32[]{:S(2)}) copy-start(f32[1,1,64,768]{2,3,1,0:T(8,128)S(1)} %copy.1808) | copy-start | bytes 589828
  157.5 180.2 %copy-start.176 = (f32[1,1,64,768]{2,3,1,0:T(8,128)}, f32[1,1,64,768]{2,3,1,0:T(8,128)S(1)}, u32[]{:S(2)}) copy-start(f32[1,1,64,768]{2,3,1,0:T(8,128)S(1)} %copy.1806) | copy-start | bytes 589828
  157.5 174.4 %copy-start.559 = (f32[64]{0:T(128)S(1)}, f32[64]{0:T(128)}, u32[]{:S(2)}) copy-start(f32[64]{0:T(128)} %get-tuple-element.1320) | copy-start | bytes 772
  157.5 175.6 %copy-start.552 = (pred[64]{0:T(512)(128)(4,1)S(1)}, pred[64]{0:T(512)(128)(4,1)}, u32[]{:S(2)}) copy-start(pred[64]{0:T(512)(128)(4,1)} %get-tuple-element.1160) | copy-start | bytes 196
  240.4 279.1 %copy-start = (f32[1,96,12,64]{1,3,2,0:T(8,128)}, f32[1,96,12,64]{1,3,2,0:T(8,128)S(1)}, u32[]{:S(2)}) copy-start(f32[1,96,12,64]{1,3,2,0:T(8,128)S(1)} %maximum_convert_fusion.2) | copy-start | bytes 884740
  240.6 321.7 %copy-start.2 = (f32[1,96,12,64]{1,3,2,0:T(8,128)}, f32[1,96,12,64]{1,3,2,0:T(8,128)S(1)}, u32[]{:S(2)}) copy-start(f32[1,96,12,64]{1,3,2,0:T(8,128)S(1)} %maximum_convert_fusion) | copy-start | bytes 884740
  348.7 122.2 %copy-start.61 = (f32[12,64,64]{1,2,0:T(8,128)}, f32[12,64,64]{1,2,0:T(8,128)S(1)}, u32[]{:S(2)}) copy-start(f32[12,64,64]{1,2,0:T(8,128)S(1)} %get-tuple-element.1334) | copy-start | bytes 589828
  371.3 147.4 %copy-start.310 = (f32[12,64,64]{2,1,0:T(8,128)}, f32[12,64,64]{2,1,0:T(8,128)S(1)}, u32[]{:S(2)}) copy-start(f32[12,64,64]{2,1,0:T(8,128)S(1)} %convolution_multiply_fusion.23) | copy-start | bytes 589828
  408.5 130.3 %all-gather.31.cloned.1.call-start = ((), (), s32[]{:S(2)}) async-start(), calls=%async_computation.6 | async-start | bytes 3342336 | tf_op jit(solution)/shard_map/all_gather | solution.py:29
  475.4 212.3 %all-reduce.28.cloned.1.call-start = ((), (), s32[]{:S(2)}) async-start(), calls=%async_computation.16 | async-start | bytes 1572864 | tf_op jit(solution)/shard_map/psum | solution.py:181
  535.3 404.0 %copy-start.52 = (f32[64,768]{1,0:T(8,128)}, f32[64,768]{1,0:T(8,128)S(1)}, u32[]{:S(2)}) copy-start(f32[64,768]{1,0:T(8,128)S(1)} %get-tuple-element.1332) | copy-start | bytes 589828
  581.3 12.9 collective-permute-start.3
  582.8 113.7 %copy-start.149 = (f32[1,1,64,768]{2,3,1,0:T(8,128)}, f32[1,1,64,768]{2,3,1,0:T(8,128)S(1)}, u32[]{:S(2)}) copy-start(f32[1,1,64,768]{2,3,1,0:T(8,128)S(1)} %copy.1729) | copy-start | bytes 589828
  582.8 11.6 collective-permute-start.2
  586.1 8.4 collective-permute-start.7
  587.4 7.3 collective-permute-start.6
  592.6 243.6 %all-gather.35.cloned.1.call-start = ((), (), s32[]{:S(2)}) async-start(), calls=%async_computation.8 | async-start | bytes 3342336 | tf_op jit(solution)/shard_map/all_gather | solution.py:29
  767.8 130.2 %all-gather.39.cloned.1.call-start = ((), (), s32[]{:S(2)}) async-start(), calls=%async_computation.10 | async-start | bytes 3342336 | tf_op jit(solution)/shard_map/all_gather | solution.py:29
  770.0 111.7 %copy-start.441 = (f32[12,64]{1,0:T(8,128)}, f32[12,64]{1,0:T(8,128)S(1)}, u32[]{:S(2)}) copy-start(f32[12,64]{1,0:T(8,128)S(1)} %get-tuple-element.1347) | copy-start | bytes 9220
  823.2 110.2 %copy-start.443 = (f32[12,64]{1,0:T(8,128)}, f32[12,64]{1,0:T(8,128)S(1)}, u32[]{:S(2)}) copy-start(f32[12,64]{1,0:T(8,128)S(1)} %get-tuple-element.1357) | copy-start | bytes 9220
  836.0 341.2 %all-reduce.26.cloned.1.call-start = ((), (), s32[]{:S(2)}) async-start(), calls=%async_computation.15 | async-start | bytes 1572864 | tf_op jit(solution)/shard_map/psum | solution.py:299
  1017.0 66.0 %collective-permute-start.13 = (bf16[1,16,768]{2,1,0:T(8,128)(2,1)}, bf16[1,16,768]{2,1,0:T(8,128)(2,1)}, u32[]{:S(2)}, u32[]{:S(2)}) collective-permute-start(bf16[1,16,768]{2,1,0:T(8,128)(2,1)} %get-tuple-element.1201), channel_id=1, source_target_pairs={{1,0},{2,1},{3,2},{4,3},{5,4},{6,5},{7,6},{8,7},{9,8},{10,9},{11,1... | collective-permute-start | bytes 73736 | tf_op jit(solution)/shard_map/ppermute | solution.py:54
  1018.3 65.6 %collective-permute-start.12 = (bf16[1,16,768]{2,1,0:T(8,128)(2,1)}, bf16[1,16,768]{2,1,0:T(8,128)(2,1)}, u32[]{:S(2)}, u32[]{:S(2)}) collective-permute-start(bf16[1,16,768]{2,1,0:T(8,128)(2,1)} %get-tuple-element.1200), channel_id=1, source_target_pairs={{0,1},{1,2},{2,3},{3,4},{4,5},{5,6},{6,7},{7,8},{8,9},{9,10},{10,1... | collective-permute-start | bytes 73736 | tf_op jit(solution)/shard_map/ppermute | solution.py:53
  1035.5 55.5 %collective-permute-start.9 = (bf16[1,16,768]{2,1,0:T(8,128)(2,1)}, bf16[1,16,768]{2,1,0:T(8,128)(2,1)S(1)}, u32[]{:S(2)}, u32[]{:S(2)}) collective-permute-start(bf16[1,16,768]{2,1,0:T(8,128)(2,1)} %get-tuple-element.1199), channel_id=1, source_target_pairs={{1,0},{2,1},{3,2},{4,3},{5,4},{6,5},{7,6},{8,7},{9,8},{10,9},{11,1... | collective-permute-start | bytes 73736 | tf_op jit(solution)/shard_map/ppermute | solution.py:54
  1036.8 54.4 %collective-permute-start.8 = (bf16[1,16,768]{2,1,0:T(8,128)(2,1)}, bf16[1,16,768]{2,1,0:T(8,128)(2,1)S(1)}, u32[]{:S(2)}, u32[]{:S(2)}) collective-permute-start(bf16[1,16,768]{2,1,0:T(8,128)(2,1)} %get-tuple-element.1198), channel_id=1, source_target_pairs={{0,1},{1,2},{2,3},{3,4},{4,5},{5,6},{6,7},{7,8},{8,9},{9,10},{10,1... | collective-permute-start | bytes 73736 | tf_op jit(solution)/shard_map/ppermute | solution.py:53
  1082.9 315.2 %all-reduce.24.cloned.1.call-start = ((), (), s32[]{:S(2)}) async-start(), calls=%async_computation.14 | async-start | bytes 1572864 | tf_op jit(solution)/shard_map/psum | solution.py:299
  1290.1 111.8 %copy-start.6 = (bf16[1,2304,768]{2,1,0:T(8,128)(2,1)S(1)}, bf16[1,2304,768]{2,1,0:T(8,128)(2,1)}, u32[]{:S(2)}) copy-start(bf16[1,2304,768]{2,1,0:T(8,128)(2,1)} %slice.2174) | copy-start | bytes 10616836
  1305.6 294.8 %all-reduce.22.cloned.1.call-start = ((), (), s32[]{:S(2)}) async-start(), calls=%async_computation.13 | async-start | bytes 1572864 | tf_op jit(solution)/shard_map/psum | solution.py:299
  1464.1 46.1 %collective-permute-start.15 = (bf16[1,16,768]{2,1,0:T(8,128)(2,1)S(1)}, bf16[1,16,768]{2,1,0:T(8,128)(2,1)S(1)}, u32[]{:S(2)}, u32[]{:S(2)}) collective-permute-start(bf16[1,16,768]{2,1,0:T(8,128)(2,1)S(1)} %get-tuple-element.1197), channel_id=1, source_target_pairs={{1,0},{2,1},{3,2},{4,3},{5,4},{6,5},{7,6},{8,7},{9,8},{10,9},{11,1... | collective-permute-start | bytes 73736 | tf_op jit(solution)/shard_map/ppermute | solution.py:54
  1465.4 44.9 %collective-permute-start.14 = (bf16[1,16,768]{2,1,0:T(8,128)(2,1)S(1)}, bf16[1,16,768]{2,1,0:T(8,128)(2,1)S(1)}, u32[]{:S(2)}, u32[]{:S(2)}) collective-permute-start(bf16[1,16,768]{2,1,0:T(8,128)(2,1)S(1)} %get-tuple-element.1196), channel_id=1, source_target_pairs={{0,1},{1,2},{2,3},{3,4},{4,5},{5,6},{6,7},{7,8},{8,9},{9,10},{10,1... | collective-permute-start | bytes 73736 | tf_op jit(solution)/shard_map/ppermute | solution.py:53
  1473.4 43.5 %collective-permute-start.11 = (bf16[1,16,768]{2,1,0:T(8,128)(2,1)S(1)}, bf16[1,16,768]{2,1,0:T(8,128)(2,1)S(1)}, u32[]{:S(2)}, u32[]{:S(2)}) collective-permute-start(bf16[1,16,768]{2,1,0:T(8,128)(2,1)S(1)} %get-tuple-element.1195), channel_id=1, source_target_pairs={{1,0},{2,1},{3,2},{4,3},{5,4},{6,5},{7,6},{8,7},{9,8},{10,9},{11,1... | collective-permute-start | bytes 73736 | tf_op jit(solution)/shard_map/ppermute | solution.py:54
  1474.7 42.4 %collective-permute-start.10 = (bf16[1,16,768]{2,1,0:T(8,128)(2,1)S(1)}, bf16[1,16,768]{2,1,0:T(8,128)(2,1)S(1)}, u32[]{:S(2)}, u32[]{:S(2)}) collective-permute-start(bf16[1,16,768]{2,1,0:T(8,128)(2,1)S(1)} %get-tuple-element.1194), channel_id=1, source_target_pairs={{0,1},{1,2},{2,3},{3,4},{4,5},{5,6},{6,7},{7,8},{8,9},{9,10},{10,1... | collective-permute-start | bytes 73736 | tf_op jit(solution)/shard_map/ppermute | solution.py:53
  1506.4 314.0 %all-reduce.20.cloned.1.call-start = ((), (), s32[]{:S(2)}) async-start(), calls=%async_computation.12 | async-start | bytes 786432 | tf_op jit(solution)/shard_map/psum | solution.py:321
  1718.5 119.4 %copy-start.51 = (f32[768,768]{1,0:T(8,128)S(1)}, f32[768,768]{1,0:T(8,128)}, u32[]{:S(2)}) copy-start(f32[768,768]{1,0:T(8,128)} %fusion.1061) | copy-start | bytes 7077892
  1729.6 198.8 %all-reduce.18.cloned.1.call-start = ((), (), s32[]{:S(2)}) async-start(), calls=%async_computation.11 | async-start | bytes 942080 | tf_op jit(solution)/shard_map/psum | solution.py:299
  1837.9 366.3 %reduce-scatter.5.cloned.1.call-start = ((), (), s32[]{:S(2)}) async-start(), calls=%async_computation.3 | async-start | bytes 30081024 | tf_op jit(solution)/shard_map/reduce_scatter | solution.py:413
  1872.8 606.3 %reduce-scatter.3.cloned.1.call-start = ((), (), s32[]{:S(2)}) async-start(), calls=%async_computation.2 | async-start | bytes 30081024 | tf_op jit(solution)/shard_map/reduce_scatter | solution.py:413
  1980.5 561.2 %all-reduce.16.cloned.1.call-start = ((), (), s32[]{:S(2)}) async-start(), calls=%async_computation.4 | async-start | bytes 3538944 | tf_op jit(solution)/shard_map/psum | solution.py:436
  (724 other events, 11211.9 us)
Sparse Core Ops, SparseCore 0:
  10.9 112.8 all-gather.28
  126.7 108.7 all-gather.32
  240.4 91.3 all-reduce.29
  408.6 43.9 all-gather.36
  475.5 43.8 all-gather.30
  592.8 94.8 all-reduce.27
  767.9 44.0 all-gather.34
  836.1 43.5 all-gather.38
  1083.0 94.1 all-reduce.25
  1305.8 92.2 all-reduce.23
  1506.5 93.9 all-reduce.21
  1729.7 90.5 all-reduce.19
  1838.0 90.4 all-reduce.17
  1932.5 271.6 reduce-scatter.4
  2208.2 270.8 reduce-scatter.2
  2486.8 54.9 all-reduce.15
where the time goes:
time: 2570 us; the launch traced here: 2560 us
  waiting for transfers between devices  1200 us (47%)
  matrix products  545 us (21%)
  other arithmetic  344 us (13%)
  local copies, waits for them, and re-layouts  237 us (9%)
  blocking collectives  159 us (6%)
  starting transfers between devices  41.3 us (2%)
  between operations  27 us (1%)
    reduce_scatter x2, waiting for transfers between devices, shards(): lax.psum_scatter(grad_whole[level_index], 'dp', scatter_dimension=0, tile...  480 us
    dot_general x376, matrix products, exact_einsum(): return jnp.einsum(pattern, operand_one, operand_two, precision=PRECISE)  396 us
    psum x4, waiting for transfers between devices, backward_layer(): lax.psum((grad_mixed_part, grad_keymark_part), 'dp')  262 us
    psum x2, waiting for transfers between devices, forward_layer(): lax.psum((exact_einsum('spm,spe->sme', member, queries), exact_einsum('sp...  184 us
    all_gather x8, blocking collectives, combined_all(): lax.all_gather(a.astype(kind), axis)  149 us
    dot_general x48, matrix products, dense_einsum(): jnp.einsum(pattern, operand_one, operand_two, preferred_element_type=jnp....  148 us
    all_gather x2, waiting for transfers between devices, shards(): lax.all_gather(weights[level_index].astype(jnp.bfloat16), 'dp', axis=0, t...  139 us
    psum x1, waiting for transfers between devices, backward_layer(): grad_qmark_keys = lax.psum(grad_qmark_part, 'dp')  89 us
  transfers between devices with their start and end apart: 32, of which 12 were waited for; matrix products, arithmetic and copies ran while one was open for 20% of the time, Pallas kernels for 0%

commit v1 on v0

v1 whole, which is shorter than its diff:
```python
import functools

import jax
import jax.numpy as jnp
from jax import lax
from jax.experimental import pallas as pl
from jax.experimental.pallas import tpu as pltpu
from jax.sharding import PartitionSpec as P

D = 768
HEADS = 12
FF = 3072
TAPS = 33
NS_ITERS = 6
LAYERS = 2
MICRO = 2
STEP_COUNT = 5


PRECISE = lax.Precision.HIGHEST
ADAM_ONE = 0.9
ADAM_TWO = 0.95
ADAM_EPSILON = 1e-08
WEIGHT_DECAY = 0.1
LR_INNER = 0.04
LR_SMALL = 0.2
LR_OUTER = 0.7
MOMENTUM = 0.9

HEAD_DIM = 64
MARKS = 64
HALF = TAPS // 2
PAIRS = HEADS // 2
LANES = 128
SCALE = HEAD_DIM**-0.5
NEG = -1e30
MESH = pl.DeviceIdType.MESH
F32 = jnp.float32
BF16 = jnp.bfloat16
NN = (((1,), (0,)), ((), ()))
NT = (((1,), (1,)), ((), ()))
TN = (((0,), (0,)), ((), ()))


def mm(a, b, dims=NN):
    return lax.dot_general(a, b, dims, preferred_element_type=F32)


def halves(a):
    high = a.astype(BF16)
    return high, (a - high.astype(F32)).astype(BF16)


def mm_left(a, b, dims=NN):
    high, rest = halves(a)
    return mm(high, b, dims) + mm(rest, b, dims)


def mm_both(a, b, dims=NN):
    ah, al = halves(a)
    bh, bl = halves(b)
    return mm(ah, bh, dims) + (mm(ah, bl, dims) + mm(al, bh, dims))


def exact(a, b, dims=NN):
    return lax.dot_general(a, b, dims, precision=PRECISE, preferred_element_type=F32)


def iota(shape, dim):
    return lax.broadcasted_iota(jnp.int32, shape, dim)


def diagonal_blocks():
    return (iota((LANES, LANES), 0) < MARKS) == (iota((LANES, LANES), 1) < HEAD_DIM)


def unit():
    return (iota((LANES, LANES), 0) == iota((LANES, LANES), 1)).astype(F32)


def per_head(marks):
    first = iota(marks.shape, 1) < HEAD_DIM
    return jnp.concatenate([jnp.where(first, marks, 0.0), jnp.where(first, 0.0, marks)], axis=0)


def head_sums(a):
    rows, cols = a.shape
    split = a.reshape(2, rows // 2, cols)
    return jnp.broadcast_to(jnp.sum(split, axis=1, keepdims=True), split.shape).reshape(rows, cols)


def head_tops(a):
    rows, cols = a.shape
    split = a.reshape(2, rows // 2, cols)
    return jnp.broadcast_to(jnp.max(split, axis=1, keepdims=True), split.shape).reshape(rows, cols)


def band(taps_row):
    wide = jnp.broadcast_to(taps_row, (LANES, 2 * LANES))
    return pltpu.roll(wide, 0, 1, stride=1, stride_axis=0)


def convolve(padded, bands, length, store):
    first = iota((LANES, LANES), 1) < HEAD_DIM
    pairs = [halves(one) for one in bands]

    def block(at, carry):
        start = pl.multiple_of(at * LANES, LANES)
        window = padded[pl.ds(start, 2 * LANES), :]
        out = [mm(high, window) + mm(rest, window) for high, rest in pairs]
        store(start, jnp.where(first, out[0], out[1]))
        return carry

    lax.fori_loop(0, length // LANES, block, 0)


def attend(queries, keys, values, low_marks, high_marks, taps, keep, padded, blended, result):
    length = queries.shape[0]
    at = iota((MARKS, length), 1)
    member = ((low_marks <= at) & (at < high_marks)).astype(F32).astype(BF16)
    counts = (high_marks - low_marks).astype(F32)
    blocks, eye = diagonal_blocks(), unit()
    q_marks = per_head(mm(member, queries) / counts)
    k_marks = per_head(mm(member, keys) / counts)
    scores = jnp.where(blocks, SCALE * exact(q_marks, k_marks, NT), NEG)
    weights = jnp.exp(scores - jnp.max(scores, axis=1, keepdims=True))
    kernel = weights / jnp.sum(weights, axis=1, keepdims=True)
    total = head_sums(jnp.broadcast_to(jnp.sum(kernel * kernel, axis=1, keepdims=True), kernel.shape))
    inverse = kernel.T / total
    keep["q_marks"][...] = q_marks
    keep["k_marks"][...] = k_marks
    keep["kernel"][...] = kernel
    keep["total"][...] = total
    for sweep in range(NS_ITERS):
        product = exact(kernel, inverse)
        one = 7.0 * eye - product
        two = 15.0 * eye - exact(product, one)
        three = 13.0 * eye - exact(product, two)
        keep["inverse"][sweep] = inverse
        keep["product"][sweep] = product
        keep["two"][sweep] = two
        keep["three"][sweep] = three
        inverse = 0.25 * exact(inverse, three)
    keep["inverse"][NS_ITERS] = inverse
    valid = at[:1] < high_marks[MARKS - 1 :]
    key_scores = jnp.where(valid, SCALE * mm_left(q_marks, keys, NT), NEG)
    key_exp = jnp.where(valid, jnp.exp(key_scores - jnp.max(key_scores, axis=1, keepdims=True)), 0.0)
    key_weights = key_exp / jnp.sum(key_exp, axis=1, keepdims=True)
    keep["key_weights"][...] = key_weights
    summary = jnp.where(blocks, mm_left(key_weights, values), 0.0)
    mixed = exact(inverse, summary)
    keep["summary"][...] = summary
    keep["mixed"][...] = mixed
    token_scores = SCALE * mm_left(k_marks, queries, NT)
    token_exp = jnp.exp(token_scores - head_tops(token_scores))
    token_weights = token_exp / head_sums(token_exp)
    keep["token_weights"][...] = token_weights
    blended[...] = mm_both(token_weights, mixed, TN)
    valid_column = iota((length, 1), 0) < high_marks[MARKS - 1 :]
    padded[0:HALF, :] = jnp.zeros((HALF, LANES), BF16)
    padded[HALF : HALF + length, :] = jnp.where(valid_column, values, jnp.zeros_like(values))
    padded[HALF + length :, :] = jnp.zeros((LANES - HALF, LANES), BF16)

    def store(start, block):
        result[pl.ds(start, LANES), :] = (blended[pl.ds(start, LANES), :] + block).astype(BF16)

    convolve(padded, [band(taps[0:1]), band(taps[1:2])], length, store)


def attend_back(grads, queries, keys, values, low_marks, high_marks, low_row, high_row, taps, keep, padded, padded_grads, blended, result, grad_taps):
    length = grads.shape[0]
    at = iota((length, MARKS), 0)
    member = ((low_row <= at) & (at < high_row)).astype(F32).astype(BF16)
    counts = (high_marks - low_marks).astype(F32)
    blocks, eye = diagonal_blocks(), unit()
    q_marks, k_marks = keep["q_marks"][...], keep["k_marks"][...]
    token_weights, key_weights = keep["token_weights"][...], keep["key_weights"][...]
    summary, mixed = keep["summary"][...], keep["mixed"][...]
    kernel = keep["kernel"][...]
    inverse = keep["inverse"][NS_ITERS]
    grad_mixed = jnp.where(blocks, mm_left(token_weights, grads), 0.0)
    grad_token = token_weights * mm_left(mixed, grads, NT)
    grad_token = SCALE * (grad_token - token_weights * head_sums(grad_token))
    grad_summary = exact(inverse, grad_mixed, TN)
    grad_inverse = exact(grad_mixed, summary, NT)
    grad_kernel = jnp.zeros_like(kernel)
    for sweep in reversed(range(NS_ITERS)):
        before, product = keep["inverse"][sweep], keep["product"][sweep]
        one = 7.0 * eye - product
        two, three = keep["two"][sweep], keep["three"][sweep]
        grad_three = 0.25 * exact(before, grad_inverse, TN)
        grad_two = -exact(product, grad_three, TN)
        grad_one = -exact(product, grad_two, TN)
        grad_product = -(exact(grad_three, two, NT) + exact(grad_two, one, NT) + grad_one)
        grad_kernel = grad_kernel + exact(grad_product, before, NT)
        grad_inverse = 0.25 * exact(grad_inverse, three, NT) + exact(kernel, grad_product, TN)
    total = keep["total"][...]
    turned = grad_inverse.T / total
    weighted = jnp.sum(jnp.where(blocks, turned * kernel, 0.0), axis=1, keepdims=True)
    weighted = head_sums(jnp.broadcast_to(weighted, kernel.shape))
    grad_kernel = grad_kernel + turned - 2.0 * kernel * weighted / total
    grad_scores = SCALE * kernel * (grad_kernel - jnp.sum(kernel * grad_kernel, axis=1, keepdims=True))
    grad_q_marks = exact(grad_scores, k_marks)
    grad_k_marks = exact(grad_scores, q_marks, TN)
    grad_k_marks = grad_k_marks + jnp.where(blocks, mm_left(grad_token, queries), 0.0)
    grad_key = mm_left(grad_summary, values, NT) - jnp.sum(grad_summary * summary, axis=1, keepdims=True)
    grad_key = SCALE * key_weights * grad_key
    grad_q_marks = grad_q_marks + jnp.where(blocks, mm_left(grad_key, keys), 0.0)
    grad_q_marks = (grad_q_marks[:MARKS] + grad_q_marks[MARKS:]) / counts
    grad_k_marks = (grad_k_marks[:MARKS] + grad_k_marks[MARKS:]) / counts
    high, rest = halves(grad_q_marks)
    result[0] = (mm_both(grad_token, k_marks, TN) + mm(member, high) + mm(member, rest)).astype(BF16)
    high, rest = halves(grad_k_marks)
    result[1] = (mm_both(grad_key, q_marks, TN) + mm(member, high) + mm(member, rest)).astype(BF16)
    blended[...] = mm_both(key_weights, grad_summary, TN)
    last = high_marks[MARKS - 1 :]
    valid_column = iota((length, 1), 0) < last
    padded[0:HALF, :] = jnp.zeros((HALF, LANES), BF16)
    padded[HALF : HALF + length, :] = jnp.where(valid_column, values, jnp.zeros_like(values))
    padded[HALF + length :, :] = jnp.zeros((LANES - HALF, LANES), BF16)
    padded_grads[0:HALF, :] = jnp.zeros((HALF, LANES), BF16)
    padded_grads[HALF : HALF + length, :] = grads
    padded_grads[HALF + length :, :] = jnp.zeros((LANES - HALF, LANES), BF16)

    def store(start, block):
        rows = start + iota((LANES, 1), 0)
        total_rows = blended[pl.ds(start, LANES), :] + jnp.where(rows < last, block, 0.0)
        result[2, pl.ds(start, LANES), :] = total_rows.astype(BF16)

    convolve(padded_grads, [band(taps[2:3]), band(taps[3:4])], length, store)
    first = iota((LANES, LANES), 1) < HEAD_DIM

    def block(step, carry):
        start = pl.multiple_of(step * LANES, LANES)
        own = padded_grads[pl.ds(start + HALF, LANES), :]
        window = padded[pl.ds(start, 2 * LANES), :]
        none = jnp.zeros_like(own)
        return (
            carry[0] + mm(jnp.where(first, own, none), window, NT),
            carry[1] + mm(jnp.where(first, none, own), window, NT),
        )

    start_sum = jnp.zeros((LANES, 2 * LANES), F32)
    sums = lax.fori_loop(0, length // LANES, block, (start_sum, start_sum))
    wide = 2 * LANES
    for head in range(2):
        folded = sums[head][0:8]
        for group in range(1, LANES // 8):
            rows = sums[head][8 * group : 8 * group + 8]
            folded = folded + pltpu.roll(rows, wide - 8 * group, 1)
        line = folded[0:1]
        for row in range(1, 8):
            line = line + pltpu.roll(folded[row : row + 1], wide - row, 1)
        grad_taps[head : head + 1, :] = line


TASKS = MICRO * PAIRS
KEPT = ("q_marks", "k_marks", "kernel", "total", "inverse", "product", "two", "three", "key_weights", "summary", "mixed", "token_weights")


def kept_shapes(length):
    square = (LANES, LANES)
    shapes = {name: square for name in KEPT}
    shapes["inverse"] = (NS_ITERS + 1,) + square
    for name in ("product", "two", "three"):
        shapes[name] = (NS_ITERS,) + square
    shapes["key_weights"] = shapes["token_weights"] = (LANES, length)
    return shapes


def owner_of(task, count):
    return task * count // TASKS


def task_of(me, count):
    task = (me * TASKS + count - 1) // count
    return task, owner_of(task, count) == me


def greet(count):
    me = lax.axis_index("dp")
    barrier = pltpu.get_barrier_semaphore()

    def signal(step, carry):
        pl.semaphore_signal(barrier, inc=1, device_id={"dp": lax.rem(me + step, count)}, device_id_type=MESH)
        return carry

    lax.fori_loop(1, count, signal, 0)
    pl.semaphore_wait(barrier, count - 1)


def scatter_tasks(count, piece, source, slab, send, receive):
    me = lax.axis_index("dp")

    def one(step, finish):
        task = lax.rem(task_of(me, count)[0] + step, TASKS)
        owner = owner_of(task, count)
        micro = task // PAIRS
        lanes = pl.ds(pl.multiple_of(lax.rem(task, PAIRS) * LANES, LANES), LANES)
        rows = pl.ds(pl.multiple_of(me * piece, piece), piece)
        outgoing = source.at[:, micro, :, lanes]
        landing = slab.at[:, rows, :]

        @pl.when(owner != me)
        def _():
            copy = pltpu.make_async_remote_copy(outgoing, landing, send.at[task], receive.at[me], device_id={"dp": owner}, device_id_type=MESH)
            if finish:
                copy.wait_send()
            else:
                copy.start()

        @pl.when((owner == me) & (not finish))
        def _():
            pltpu.make_async_copy(outgoing, landing, receive.at[me]).start()

    def run(finish):
        def body(step, carry):
            one(step, finish)
            return carry

        lax.fori_loop(0, TASKS, body, 0)

    return run


def await_slab(count, piece, slab, receive):
    def body(origin, carry):
        landing = slab.at[:, pl.ds(pl.multiple_of(origin * piece, piece), piece), :]
        pltpu.make_async_copy(landing, landing, receive.at[origin]).wait()
        return carry

    lax.fori_loop(0, count, body, 0)


def return_rows(count, piece, result, target, send, receive):
    me = lax.axis_index("dp")
    task = task_of(me, count)[0]
    micro = task // PAIRS
    lanes = pl.ds(pl.multiple_of(lax.rem(task, PAIRS) * LANES, LANES), LANES)

    def run(finish):
        def body(step, carry):
            peer = lax.rem(me + step, count)
            rows = pl.ds(pl.multiple_of(peer * piece, piece), piece)
            outgoing = result.at[:, rows, :]
            landing = target.at[:, micro, :, lanes]

            @pl.when(peer != me)
            def _():
                copy = pltpu.make_async_remote_copy(outgoing, landing, send.at[peer], receive.at[task], device_id={"dp": peer}, device_id_type=MESH)
                if finish:
                    copy.wait_send()
                else:
                    copy.start()

            @pl.when((peer == me) & (not finish))
            def _():
                pltpu.make_async_copy(outgoing, landing, receive.at[task]).start()

            return carry

        lax.fori_loop(0, count, body, 0)

    return run


def await_rows(target, receive):
    def body(task, carry):
        lanes = pl.ds(pl.multiple_of(lax.rem(task, PAIRS) * LANES, LANES), LANES)
        landing = target.at[:, task // PAIRS, :, lanes]
        pltpu.make_async_copy(landing, landing, receive.at[task]).wait()
        return carry

    lax.fori_loop(0, TASKS, body, 0)


def forward_kernel(count, piece, qkv, low_col, high_col, taps, mixed_rows, slab, *refs):
    keep = dict(zip(KEPT, refs))
    padded, blended, result, send_one, receive_one, send_two, receive_two = refs[len(KEPT) :]
    me = lax.axis_index("dp")
    task, owns = task_of(me, count)
    greet(count)
    out = scatter_tasks(count, piece, qkv, slab, send_one, receive_one)
    out(False)
    back = return_rows(count, piece, result, mixed_rows, send_two, receive_two)

    @pl.when(owns)
    def _():
        micro, pair = task // PAIRS, lax.rem(task, PAIRS)
        await_slab(count, piece, slab, receive_one)
        attend(slab[0], slab[1], slab[2], low_col[micro], high_col[micro], taps[pair], keep, padded, blended, result.at[0])
        back(False)

    out(True)
    await_rows(mixed_rows, receive_two)

    @pl.when(owns)
    def _():
        back(True)


def backward_kernel(count, piece, grads, low_col, high_col, low_row, high_row, taps, slab, *refs):
    keep = dict(zip(KEPT, refs))
    out_grads, grad_taps, grad_slab, padded, padded_grads, blended, result, send_one, receive_one, send_two, receive_two = refs[len(KEPT) :]
    me = lax.axis_index("dp")
    task, owns = task_of(me, count)
    greet(count)
    out = scatter_tasks(count, piece, grads, grad_slab, send_one, receive_one)
    out(False)
    back = return_rows(count, piece, result, out_grads, send_two, receive_two)
    grad_taps[...] = jnp.zeros(grad_taps.shape, F32)

    @pl.when(owns)
    def _():
        micro, pair = task // PAIRS, lax.rem(task, PAIRS)
        await_slab(count, piece, grad_slab, receive_one)
        attend_back(
            grad_slab[0], slab[0], slab[1], slab[2], low_col[micro], high_col[micro], low_row[micro], high_row[micro],
            taps[pair], keep, padded, padded_grads, blended, result, grad_taps.at[pair],
        )
        back(False)

    out(True)
    await_rows(out_grads, receive_two)

    @pl.when(owns)
    def _():
        back(True)


VMEM = pl.BlockSpec(memory_space=pltpu.VMEM)
DMA = pltpu.SemaphoreType.DMA


def attention_forward(count, qkv, marks, taps, ident):
    piece = qkv.shape[2]
    length = piece * count
    shapes = kept_shapes(length)
    results = pl.pallas_call(
        functools.partial(forward_kernel, count, piece),
        out_shape=[
            jax.ShapeDtypeStruct((1, MICRO, piece, D), BF16),
            jax.ShapeDtypeStruct((3, length, LANES), BF16),
        ]
        + [jax.ShapeDtypeStruct(shapes[name], F32) for name in KEPT],
        in_specs=[VMEM] * 4,
        out_specs=[VMEM] * (2 + len(KEPT)),
        scratch_shapes=[
            pltpu.VMEM((length + LANES, LANES), BF16),
            pltpu.VMEM((length, LANES), F32),
            pltpu.VMEM((1, length, LANES), BF16),
            DMA((TASKS,)),
            DMA((count,)),
            DMA((count,)),
            DMA((TASKS,)),
        ],
        compiler_params=pltpu.CompilerParams(collective_id=ident, has_side_effects=True, vmem_limit_bytes=60 << 20),
        name="attend_forward",
    )(qkv, marks[0], marks[1], taps)
    return results[0][0], results[1:]


def attention_backward(count, grads, marks, taps, kept, ident):
    piece = grads.shape[2]
    length = piece * count
    return pl.pallas_call(
        functools.partial(backward_kernel, count, piece),
        out_shape=[
            jax.ShapeDtypeStruct((3, MICRO, piece, D), BF16),
            jax.ShapeDtypeStruct((PAIRS, 2, 2 * LANES), F32),
        ],
        in_specs=[VMEM] * (7 + len(KEPT)),
        out_specs=[VMEM] * 2,
        scratch_shapes=[
            pltpu.VMEM((1, length, LANES), BF16),
            pltpu.VMEM((length + LANES, LANES), BF16),
            pltpu.VMEM((length + LANES, LANES), BF16),
            pltpu.VMEM((length, LANES), F32),
            pltpu.VMEM((3, length, LANES), BF16),
            DMA((TASKS,)),
            DMA((count,)),
            DMA((count,)),
            DMA((TASKS,)),
        ],
        compiler_params=pltpu.CompilerParams(collective_id=ident, has_side_effects=True, vmem_limit_bytes=60 << 20),
        name="attend_backward",
    )(grads, *marks, taps, *kept)


def dense(a, b, dims=NN):
    return mm(a, b, dims)


def layer_norm(values, gain_vec, shift_vec):
    row_mean = jnp.mean(values, axis=-1, keepdims=True)
    centred = values - row_mean
    variance = jnp.mean(centred * centred, axis=-1, keepdims=True)
    return centred * lax.rsqrt(variance + 1e-05) * gain_vec + shift_vec


def unpack(params):
    blocks = [params[index * D : (index + 1) * D] for index in range(8)]
    bias_up = params[8 * D : 8 * D + FF]
    conv_taps = params[8 * D + FF :].reshape(HEADS, TAPS)
    return (blocks, bias_up, conv_taps)


def pair_taps(conv_taps):
    both = jnp.stack([conv_taps.reshape(PAIRS, 2, TAPS), conv_taps[:, ::-1].reshape(PAIRS, 2, TAPS)], axis=1)
    both = both.reshape(PAIRS, 4, TAPS)
    return jnp.pad(both, ((0, 0), (0, 0), (0, 2 * LANES - TAPS)))


def split_rows(rows):
    return rows[: 3 * D].reshape(3, D, D), rows[3 * D : 4 * D], rows[4 * D : 4 * D + FF], rows[4 * D + FF :]


def forward_layer(count, inputs, rows, params, marks, ident):
    piece = inputs.shape[0] // MICRO
    blocks, bias_up, conv_taps = unpack(params)
    proj, out_weight, up_weight, down_weight = split_rows(rows)
    low_in = inputs.astype(BF16)
    bias = jnp.stack([blocks[0], jnp.zeros_like(blocks[0]), blocks[1]])
    qkv = jnp.stack([(dense(low_in, proj[part]) + bias[part]).astype(BF16) for part in range(3)])
    low_comb, kept = attention_forward(count, qkv.reshape(3, MICRO, piece, D), marks, pair_taps(conv_taps), ident)
    low_comb = low_comb.reshape(MICRO * piece, D)
    resid_one = inputs + (dense(low_comb, out_weight) + blocks[2])
    hidden_one = layer_norm(resid_one, blocks[4], blocks[5])
    low_hidden = hidden_one.astype(BF16)
    upward = dense(low_hidden, up_weight, NT) + bias_up
    low_act = jax.nn.gelu(upward).astype(BF16)
    resid_two = hidden_one + (dense(low_act, down_weight) + blocks[3])
    output = layer_norm(resid_two, blocks[6], blocks[7])
    return output, (low_in, kept, low_comb, resid_one, low_hidden, upward, low_act, resid_two)


def backward_layer(count, grad_output, rows, params, marks, state, ident):
    low_in, kept, low_comb, resid_one, low_hidden, upward, low_act, resid_two = state
    total = low_in.shape[0]
    piece = total // MICRO
    blocks, bias_up, conv_taps = unpack(params)
    proj, out_weight, up_weight, down_weight = split_rows(rows)
    _, pull_two = jax.vjp(layer_norm, resid_two, blocks[6], blocks[7])
    grad_two, grad_gain_two, grad_shift_two = pull_two(grad_output)
    low_down = grad_two.astype(BF16)
    grad_bias_down = jnp.sum(low_down.astype(F32), axis=0)
    grad_act = dense(low_down, down_weight, NT)
    _, pull_gelu = jax.vjp(jax.nn.gelu, upward)
    low_up = pull_gelu(grad_act)[0].astype(BF16)
    grad_bias_up = jnp.sum(low_up.astype(F32), axis=0)
    grad_hidden = grad_two + dense(low_up, up_weight)
    _, pull_one = jax.vjp(layer_norm, resid_one, blocks[4], blocks[5])
    grad_one, grad_gain_one, grad_shift_one = pull_one(grad_hidden)
    low_branch = grad_one.astype(BF16)
    grad_bias_out = jnp.sum(low_branch.astype(F32), axis=0)
    grad_comb = dense(low_branch, out_weight, NT).astype(BF16)
    low_grads, grad_taps = attention_backward(count, grad_comb.reshape(1, MICRO, piece, D), marks, pair_taps(conv_taps), kept, ident)
    low_grads = low_grads.reshape(3, total, D)
    grad_bias_q = jnp.sum(low_grads[0].astype(F32), axis=0)
    grad_bias_v = jnp.sum(low_grads[2].astype(F32), axis=0)
    grad_in = grad_one + sum(dense(low_grads[part], proj[part], NT) for part in range(3))
    parts = [dense(low_in, low_grads[part], TN).astype(BF16) for part in range(3)]
    parts = parts + [
        dense(low_comb, low_branch, TN).astype(BF16),
        dense(low_up, low_hidden, TN).astype(BF16),
        dense(low_act, low_down, TN).astype(BF16),
    ]
    grad_small = jnp.concatenate(
        [
            grad_bias_q,
            grad_bias_v,
            grad_bias_out,
            grad_bias_down,
            grad_gain_one,
            grad_shift_one,
            grad_gain_two,
            grad_shift_two,
            grad_bias_up,
            grad_taps[:, :, :TAPS].reshape(-1),
        ]
    )
    return grad_in, jnp.concatenate(parts, axis=0), grad_small


def adam(weights, first, second, grad, rate, decay):
    correct_one = 1.0 - ADAM_ONE**STEP_COUNT
    correct_two = 1.0 - ADAM_TWO**STEP_COUNT
    new_first = ADAM_ONE * first + (1.0 - ADAM_ONE) * grad
    new_second = ADAM_TWO * second + (1.0 - ADAM_TWO) * grad * grad
    step = new_first / correct_one / (jnp.sqrt(new_second / correct_two) + ADAM_EPSILON)
    return new_first, new_second, rate * (step + decay * weights)


def shards(
    hidden,
    bounds,
    cotangent,
    weights,
    small_params,
    first_big,
    second_big,
    first_small,
    second_small,
    outer_big,
    outer_small,
):
    count = lax.axis_size("dp")
    piece = hidden.shape[3]
    total = MICRO * piece
    held = [lax.all_gather(weights[level].astype(BF16), "dp", axis=0, tiled=True) for level in range(LAYERS)]
    edges = bounds[0, :, 0, :]
    low_edges, high_edges = edges[:, :-1], edges[:, 1:]
    marks = (low_edges[:, :, None], high_edges[:, :, None], low_edges[:, None, :], high_edges[:, None, :])
    positions = lax.axis_index("dp") * piece + jnp.arange(piece, dtype=jnp.int32)
    valid = (positions[None, :] < edges[:, -1:]).astype(F32).reshape(total, 1)
    activation = hidden[0, :, 0].reshape(total, D).astype(F32)
    states = []
    for level in range(LAYERS):
        activation, state = forward_layer(count, activation, held[level], small_params[level], marks, 1)
        states.append(state)
    gradient = cotangent[0, :, 0].reshape(total, D).astype(F32) * valid
    grad_parts, small_parts = [None] * LAYERS, [None] * LAYERS
    for level in reversed(range(LAYERS)):
        gradient, grad_rows, small_parts[level] = backward_layer(count, gradient, held[level], small_params[level], marks, states[level], 2)
        grad_parts[level] = lax.psum_scatter(grad_rows, "dp", scatter_dimension=0, tiled=True).astype(F32)
    grad_big = jnp.stack(grad_parts)
    grad_small = lax.psum(jnp.stack(small_parts), "dp")
    new_first, new_second, delta_big = adam(weights, first_big[0], second_big[0], grad_big, LR_INNER, WEIGHT_DECAY)
    new_first_small, new_second_small, delta_small = adam(small_params, first_small[0], second_small[0], grad_small, LR_SMALL, 0.0)
    reps = lax.axis_size("rep")
    mean_big = lax.psum(delta_big.astype(BF16), "rep").astype(F32) / reps
    mean_small = lax.psum(delta_small.astype(BF16), "rep").astype(F32) / reps
    outer_big_new = MOMENTUM * outer_big + mean_big
    outer_small_new = MOMENTUM * outer_small + mean_small
    weights_new = weights - LR_OUTER * (mean_big + MOMENTUM * outer_big_new)
    small_new = small_params - LR_OUTER * (mean_small + MOMENTUM * outer_small_new)
    shape = (1, MICRO, 1, piece, D)
    return (
        activation.reshape(shape),
        gradient.reshape(shape),
        new_first[None],
        new_second[None],
        new_first_small[None],
        new_second_small[None],
        outer_big_new,
        outer_small_new,
        weights_new,
        small_new,
        weights_new.astype(BF16),
    )


def solution(mesh):
    placed = (
        P("rep", None, None, "dp", None),
        P("rep", None, None, None),
        P("rep", None, None, "dp", None),
        P(None, "dp", None),
        P(),
        P("rep", None, "dp", None),
        P("rep", None, "dp", None),
        P("rep", None, None),
        P("rep", None, None),
        P(None, "dp", None),
        P(),
    )
    return jax.shard_map(
        shards,
        mesh=mesh,
        in_specs=placed,
        out_specs=(
            P("rep", None, None, "dp", None),
            P("rep", None, None, "dp", None),
            P("rep", None, "dp", None),
            P("rep", None, "dp", None),
            P("rep", None, None),
            P("rep", None, None),
            P(None, "dp", None),
            P(),
            P(None, "dp", None),
            P(),
            P(None, "dp", None),
        ),
        check_vma=False,
    )
```

time: 2570 us -> 913 us (0.36)
  waiting for transfers between devices: 1200 us -> 566 us
  matrix products: 545 us -> 93.5 us
  other arithmetic: 344 us -> 42.1 us
  local copies, waits for them, and re-layouts: 237 us -> 8.75 us
  Pallas kernels: 0 us -> 168 us
  blocking collectives: 159 us -> 9.07 us
  starting transfers between devices: 41.3 us -> 0.5 us
    psum x8 -> x2, waiting for transfers between devices: 580 us -> 111 us  [the longest x1 66.2 us: shards(): grad_small = lax.psum(jnp.stack(small_parts), 'dp')]
    dot_general x424 -> x36, matrix products: 545 us -> 93.5 us  [mm(): return lax.dot_general(a, b, dims, preferred_element_type=F32)]
    reduce_scatter x2, waiting for transfers between devices: 480 us -> 286 us  [shards(): lax.psum_scatter(grad_rows, 'dp', scatter_dimension=0, tiled=True)]
    add x72 -> x2, other arithmetic: 185 us -> 8.67 us  [the longest x1 8.67 us: adam(): new_second = ADAM_TWO * second + (1.0 - ADAM_TWO) * grad * grad]
    pallas_call x0 -> x4, Pallas kernels: none -> 168 us  [the longest x2 86.4 us: attention_backward(): pl.pallas_call(functools.partial(backward_kernel, count, piece), out_shap...]
    all_gather x8 -> x0, blocking collectives: 149 us -> none  [combined_all(): lax.all_gather(a.astype(kind), axis)]
    unnamed x1582 -> x96, local copies, waits for them, and re-layouts: 78.5 us -> 1.01 us
    another operation x208 -> x6, local copies, waits for them, and re-layouts: 71.7 us -> 0.27 us  [the longest x4 0.21 us: pair_taps(): jnp.stack([conv_taps.reshape(PAIRS, 2, TAPS), conv_taps[:, ::-1].reshape(...]
  transfers between devices with their start and end apart: 32 -> 6, of which waited for: 12 -> 6; matrix products, arithmetic and copies ran while one was open for 20% -> 7% of each run, Pallas kernels for 0% -> 5%
where the time goes in v1:
time: 913 us; the launch traced here: 904 us
  waiting for transfers between devices  566 us (62%)
  Pallas kernels  168 us (18%)
  matrix products  93.5 us (10%)
  other arithmetic  42.1 us (5%)
  between operations  15.4 us (2%)
    reduce_scatter x2, waiting for transfers between devices, shards(): lax.psum_scatter(grad_rows, 'dp', scatter_dimension=0, tiled=True)  286 us
    all_gather x2, waiting for transfers between devices, shards(): lax.all_gather(weights[level].astype(BF16), 'dp', axis=0, tiled=True)  169 us
    dot_general x36, matrix products, mm(): return lax.dot_general(a, b, dims, preferred_element_type=F32)  93.5 us
    pallas_call x2, Pallas kernels, attention_backward(): pl.pallas_call(functools.partial(backward_kernel, count, piece), out_shap...  86.4 us
    pallas_call x2, Pallas kernels, attention_forward(): pl.pallas_call(functools.partial(forward_kernel, count, piece), out_shape...  81.7 us
    psum x1, waiting for transfers between devices, shards(): grad_small = lax.psum(jnp.stack(small_parts), 'dp')  66.2 us
    psum x1, waiting for transfers between devices, shards(): mean_big = lax.psum(delta_big.astype(BF16), 'rep').astype(F32) / reps  44.7 us
  transfers between devices with their start and end apart: 6, of which 6 were waited for; matrix products, arithmetic and copies ran while one was open for 7% of the time, Pallas kernels for 5%

profile of v1, /device:TPU:0, one launch (start us, length us, event | category | flops | bytes accessed | tf_op | source)
XLA Modules:
  0.0 903.9 jit_solution(5660095719082328635)
XLA Ops:
  7.2 2.2 convert.6
  16.2 107.6 %all-gather.5.cloned.1.call-done = bf16[1,9216,768]{2,1,0:T(8,128)(2,1)} async-done(((bf16[1,576,768]{2,1,0:T(8,128)(2,1)}), bf16[1,9216,768]{2,1,0:T(8,128)(2,1)}) %all-gather.5.cloned.1.call-update) | async-done | bytes 14155792 | tf_op jit(solution)/shard_map/all_gather | solution.py:610
  123.8 1.6 convolution_convert_fusion.15
  125.4 1.6 fusion.59
  127.0 1.6 fusion.58
  129.5 47.8 %attend_forward.2 = (bf16[1,2,64,768]{3,2,1,0:T(8,128)(2,1)}, bf16[3,1024,128]{2,1,0:T(8,128)(2,1)}, f32[128,128]{1,0:T(8,128)}, f32[128,128]{1,0:T(8,128)}, f32...) custom-call(bf16[3,2,64,768]{3,2,1,0:T(8,128)(2,1)} %pad_maximum_fus, ...), custom_call_target="tpu_custom_call" | custom-call | tf_op jit(solution)/shard_map/attend_forward/pallas_call | solution.py:439
  177.3 1.8 fusion.93
  179.3 4.0 fusion.13
  183.4 5.0 fusion.94
  188.7 61.1 %all-gather.7.cloned.1.call-done = bf16[1,9216,768]{2,1,0:T(8,128)(2,1)} async-done(((bf16[1,576,768]{2,1,0:T(8,128)(2,1)}), bf16[1,9216,768]{2,1,0:T(8,128)(2,1)}) %all-gather.7.cloned.1.call-update) | async-done | bytes 14155792 | tf_op jit(solution)/shard_map/all_gather | solution.py:610
  249.8 1.6 convolution_convert_fusion.14
  251.4 1.6 fusion.61
  253.0 1.6 fusion.60
  255.5 33.9 %attend_forward.3 = (bf16[1,2,64,768]{3,2,1,0:T(8,128)(2,1)}, bf16[3,1024,128]{2,1,0:T(8,128)(2,1)}, f32[128,128]{1,0:T(8,128)}, f32[128,128]{1,0:T(8,128)}, f32...) custom-call(bf16[3,2,64,768]{3,2,1,0:T(8,128)(2,1)} %pad_maximum_fus, ...), custom_call_target="tpu_custom_call" | custom-call | tf_op jit(solution)/shard_map/attend_forward/pallas_call | solution.py:439
  289.4 1.8 fusion.95
  291.4 4.0 fusion.12
  295.5 4.0 fusion.96
  301.1 4.9 convert_reduce_fusion
  306.0 3.9 multiply_reduce_fusion.2
  310.3 2.5 convolution_convert_fusion.13
  312.8 41.2 %attend_backward.2 = (bf16[3,2,64,768]{3,2,1,0:T(8,128)(2,1)}, f32[6,2,256]{2,1,0:T(2,128)}) custom-call(bf16[1,2,64,768]{3,2,1,0:T(8,128)(2,1)} %bitcast.261, s32[2,64,1]{2,1,0:T(8,128)} %copy.39.low_col, s32[2,64,1]{2,1,0:T(8,128)} %copy.40.high_col, s32[2,1,64]{2,1,0:T(1,128)} %bitcast.270, s32[2,1,64]{2,1,0:T(1,128)} %bitcast.268, ...), custom_call_target="tpu_custom_call" | custom-call | tf_op jit(solution)/shard_map/attend_backward/pallas_call | solution.py:466
  357.8 1.8 fusion.63
  359.6 1.8 convolution_add_fusion.3
  361.5 2.1 multiply_reduce_fusion.3
  363.9 4.9 convert_reduce_fusion.1
  368.9 3.9 multiply_reduce_fusion.4
  373.6 1.6 fusion.39
  378.3 3.7 fusion.1
  382.4 2.5 convolution_convert_fusion.12
  384.9 45.2 %attend_backward.3 = (bf16[3,2,64,768]{3,2,1,0:T(8,128)(2,1)}, f32[6,2,256]{2,1,0:T(2,128)}) custom-call(bf16[1,2,64,768]{3,2,1,0:T(8,128)(2,1)} %bitcast.260, s32[2,64,1]{2,1,0:T(8,128)} %copy.39.low_col, s32[2,64,1]{2,1,0:T(8,128)} %copy.40.high_col, s32[2,1,64]{2,1,0:T(1,128)} %bitcast.271, s32[2,1,64]{2,1,0:T(1,128)} %bitcast.269, ...), custom_call_target="tpu_custom_call" | custom-call | tf_op jit(solution)/shard_map/attend_backward/pallas_call | solution.py:466
  433.0 5.2 fusion
  445.5 3.6 fusion.3
  449.2 3.9 fusion.2
  453.1 1.8 fusion.62
  455.0 1.9 convolution_add_fusion.1
  456.8 2.6 fusion.51
  459.4 66.2 %all-reduce.5.cloned.1.call-done = f32[2,9612]{1,0:T(2,128)} async-done(((f32[2,9612]{1,0:T(2,128)}), f32[2,9612]{1,0:T(2,128)}) %all-reduce.5.cloned.1.call-update) | async-done | bytes 76912 | tf_op jit(solution)/shard_map/psum | solution.py:627
  525.6 1.8 multiply_convert_fusion.3
  527.4 9.1 %psum.23 = bf16[2,9612]{1,0:T(2,128)(2,1)} all-reduce(bf16[2,9612]{1,0:T(2,128)(2,1)S(1)} %get-tuple-element.166), channel_id=1, replica_groups=mesh['rep'=2,'dp'=16] {'rep'}, use_global_device_ids=true, to_apply=%region_38.39 | all-reduce | flops 19224 | bytes 76896 | tf_op jit(solution)/shard_map/psum | solution.py:632
  536.5 140.1 %reduce-scatter.5.cloned.1.call-done = bf16[576,768]{1,0:T(8,128)(2,1)} async-done(((bf16[9216,768]{1,0:T(8,128)(2,1)}), bf16[576,768]{1,0:T(8,128)(2,1)}) %reduce-scatter.5.cloned.1.call-update) | async-done | bytes 884752 | tf_op jit(solution)/shard_map/reduce_scatter | solution.py:625
  676.6 3.2 convert_bitcast_fusion
  679.8 145.9 %reduce-scatter.3.cloned.1.call-done = bf16[576,768]{1,0:T(8,128)(2,1)} async-done(((bf16[9216,768]{1,0:T(8,128)(2,1)}), bf16[576,768]{1,0:T(8,128)(2,1)}) %reduce-scatter.3.cloned.1.call-update) | async-done | bytes 884752 | tf_op jit(solution)/shard_map/reduce_scatter | solution.py:625
  825.7 2.6 convert_bitcast_fusion.2
  828.3 6.0 multiply_convert_fusion
  834.4 1.7 multiply_subtract_fusion.1
  836.1 8.7 fusion.14
  844.8 44.7 %all-reduce.7.cloned.1.call-done = bf16[2,576,768]{2,1,0:T(8,128)(2,1)} async-done(((bf16[2,576,768]{2,1,0:T(8,128)(2,1)}), bf16[2,576,768]{2,1,0:T(8,128)(2,1)}) %all-reduce.7.cloned.1.call-update) | async-done | bytes 1769488 | tf_op jit(solution)/shard_map/psum | solution.py:631
  889.5 7.1 fusion.80
  (186 shorter events, 29.7 us)
Async XLA Ops:
  7.2 116.6 %all-gather.5.cloned.1.call-start = ((), (), s32[]{:S(2)}) async-start(), calls=%async_computation.6 | async-start | bytes 15040512 | tf_op jit(solution)/shard_map/all_gather | solution.py:610
  9.4 2.2 copy-start.20
  9.4 4.3 copy-start.4
  9.4 6.6 copy-start.1
  9.4 114.3 %copy-start.3 = (bf16[1,2,1,64,768]{4,3,2,1,0:T(8,128)(2,1)S(1)}, bf16[1,2,1,64,768]{4,3,2,1,0:T(8,128)(2,1)}, u32[]{:S(2)}) copy-start(bf16[1,2,1,64,768]{4,3,2,1,0:T(8,128)(2,1)} %param.11) | copy-start | bytes 589828
  10.8 239.0 %all-gather.7.cloned.1.call-start = ((), (), s32[]{:S(2)}) async-start(), calls=%async_computation.7 | async-start | bytes 15040512 | tf_op jit(solution)/shard_map/all_gather | solution.py:610
  11.5 514.1 %all-reduce.5.cloned.1.call-start = ((), (), s32[]{:S(2)}) async-start(), calls=%async_computation.4 | async-start | bytes 155648 | tf_op jit(solution)/shard_map/psum | solution.py:627
  179.1 4.3 copy-start.15
  179.3 4.0 copy-start.31
  179.3 4.0 copy-start.26
  183.3 5.0 copy-start.35
  188.3 101.0 %copy-start.13 = (f32[128]{0:T(128)}, f32[128]{0:T(128)S(1)}, u32[]{:S(2)}) copy-start(f32[128]{0:T(128)S(1)} %broadcast_multiply_fusion.2) | copy-start | bytes 1540
  188.5 66.1 %copy-start.33 = (f32[128]{0:T(128)}, f32[128]{0:T(128)S(1)}, u32[]{:S(2)}) copy-start(f32[128]{0:T(128)S(1)} %multiply_reduce_fusion.11) | copy-start | bytes 1540
  188.6 100.8 %copy-start.18 = (f32[128]{0:T(128)}, f32[128]{0:T(128)S(1)}, u32[]{:S(2)}) copy-start(f32[128]{0:T(128)S(1)} %fusion.71) | copy-start | bytes 1540
  295.5 5.7 copy-start.38
  357.8 3.6 copy-start.14
  357.8 3.7 copy-start.19
  359.6 3.9 copy-start.34
  361.4 2.5 copy-start.36
  363.9 5.0 copy-start.7
  363.9 5.0 copy-start.16
  363.9 5.0 copy-start.27
  368.9 3.9 copy-start.32
  372.8 4.0 copy-start.6
  378.3 3.7 copy-start.25
  378.3 3.9 copy-start.22
  378.3 3.9 copy-start.21
  378.3 3.9 copy-start.11
  378.3 4.0 copy-start.29
  384.9 47.1 %copy-start.24 = (f32[768]{0:T(1024)S(1)}, f32[768]{0:T(1024)}, u32[]{:S(2)}) copy-start(f32[768]{0:T(1024)} %get-tuple-element.99) | copy-start | bytes 9220
  384.9 47.2 %copy-start.23 = (f32[768]{0:T(1024)S(1)}, f32[768]{0:T(1024)}, u32[]{:S(2)}) copy-start(f32[768]{0:T(1024)} %get-tuple-element.110) | copy-start | bytes 9220
  384.9 47.2 %copy-start.12 = (f32[3072]{0:T(1024)S(1)}, f32[3072]{0:T(1024)}, u32[]{:S(2)}) copy-start(f32[3072]{0:T(1024)} %get-tuple-element.192) | copy-start | bytes 36868
  432.9 243.7 %reduce-scatter.5.cloned.1.call-start = ((), (), s32[]{:S(2)}) async-start(), calls=%async_computation.3 | async-start | bytes 15040512 | tf_op jit(solution)/shard_map/reduce_scatter | solution.py:625
  438.2 1.1 copy-start.2
  438.2 387.5 %reduce-scatter.3.cloned.1.call-start = ((), (), s32[]{:S(2)}) async-start(), calls=%async_computation.2 | async-start | bytes 15040512 | tf_op jit(solution)/shard_map/reduce_scatter | solution.py:625
  439.3 4.7 copy-start.5
  440.8 4.7 copy-start.17
  440.8 4.7 copy-start.28
  445.5 3.7 copy-start.8
  445.5 3.7 copy-start.37
  453.1 3.7 copy-start.30
  453.1 436.4 %all-reduce.7.cloned.1.call-start = ((), (), s32[]{:S(2)}) async-start(), calls=%async_computation.5 | async-start | bytes 3538944 | tf_op jit(solution)/shard_map/psum | solution.py:631
  454.9 70.7 %copy-start.9 = (f32[1,2,9612]{2,1,0:T(2,128)S(1)}, f32[1,2,9612]{2,1,0:T(2,128)}, u32[]{:S(2)}) copy-start(f32[1,2,9612]{2,1,0:T(2,128)} %param.18) | copy-start | bytes 230692
  455.0 70.7 %copy-start.10 = (f32[1,2,9612]{2,1,0:T(2,128)S(1)}, f32[1,2,9612]{2,1,0:T(2,128)}, u32[]{:S(2)}) copy-start(f32[1,2,9612]{2,1,0:T(2,128)} %param.19) | copy-start | bytes 230692
  679.8 148.5 %copy-start = (f32[2,576,768]{2,1,0:T(8,128)S(1)}, f32[2,576,768]{2,1,0:T(8,128)}, u32[]{:S(2)}) copy-start(f32[2,576,768]{2,1,0:T(8,128)} %param.14) | copy-start | bytes 10616836
Sparse Core Ops, SparseCore 0:
  10.9 112.8 all-gather.4
  126.6 123.1 all-gather.6
  433.0 92.5 all-reduce.4
  529.7 146.8 reduce-scatter.4
  680.6 145.0 reduce-scatter.2
  834.5 54.9 all-reduce.6

commit v2 on v1

--- a/solution.py
+++ b/solution.py
@@ -487,6 +487,253 @@
     )(grads, *marks, taps, *kept)
 
 
+CHUNK = 48
+SLICE = 16
+
+
+def settle_kernel(
+    block_rows, grads_last, grads_first, weights, first, second, small, small_first, small_second,
+    grad_out, mean_out, small_out,
+    own, got_core, got_y, got_z, inner, step_own, step_got, small_got, small_own, small_step, small_step_got,
+    own_sem, core_send, core_got, y_send, y_got, z_send, z_got, inner_sem, rep_send, rep_got, small_send, small_sem, back_send, back_sem, small_rep,
+):
+    me = lax.axis_index("dp")
+    other_rep = 1 - lax.axis_index("rep")
+    core, y, z = lax.rem(me, 2), lax.rem(me // 2, 2), me // 4
+    devices = 16
+    per_layer = block_rows // CHUNK
+    chunks = LAYERS * per_layer
+
+    barrier = pltpu.get_barrier_semaphore()
+
+    def signal(step, carry):
+        pl.semaphore_signal(barrier, inc=1, device_id={"dp": lax.rem(me + step, devices)}, device_id_type=MESH)
+        return carry
+
+    lax.fori_loop(1, devices, signal, 0)
+    pl.semaphore_signal(barrier, inc=1, device_id={"rep": other_rep}, device_id_type=MESH)
+    pl.semaphore_wait(barrier, devices)
+
+    def to_dp(source, target, send, receive, peer):
+        return pltpu.make_async_remote_copy(source, target, send, receive, device_id={"dp": peer}, device_id_type=MESH)
+
+    def to_rep(source, target, send, receive):
+        return pltpu.make_async_remote_copy(source, target, send, receive, device_id={"rep": other_rep}, device_id_type=MESH)
+
+    def rows_of(part):
+        return pl.ds(pl.multiple_of(part * CHUNK, CHUNK), CHUNK)
+
+    def core_copy(source, chunk, part):
+        return to_dp(source.at[:, :, 1 - core, rows_of(part), :], got_core.at[chunk], core_send.at[chunk], core_got.at[chunk], me + 1 - 2 * core)
+
+    def own_copy(source, chunk, part):
+        return pltpu.make_async_copy(source.at[:, :, core, rows_of(part), :], own.at[chunk], own_sem.at[chunk])
+
+    for order, source in enumerate((grads_last, grads_first)):
+
+        def begin(part, carry):
+            chunk = order * per_layer + part
+            core_copy(source, chunk, part).start()
+            own_copy(source, chunk, part).start()
+            return carry
+
+        lax.fori_loop(0, per_layer, begin, 0)
+
+    def small_copy(step):
+        peer = lax.rem(me + step, devices)
+        return to_dp(small.at[peer], small_got.at[me], small_send.at[peer], small_sem.at[me], peer)
+
+    def small_begin(step, carry):
+        small_copy(step).start()
+        return carry
+
+    lax.fori_loop(1, devices, small_begin, 0)
+
+    def y_copy(chunk):
+        return to_dp(own.at[chunk, :, 1 - y], got_y.at[chunk], y_send.at[chunk], y_got.at[chunk], me + 2 - 4 * y)
+
+    def z_copy(chunk, hop):
+        there = lax.rem(z + hop, 4)
+        return to_dp(own.at[chunk, there, y], got_z.at[chunk, hop - 1], z_send.at[chunk, hop - 1], z_got.at[chunk, hop - 1], there * 4 + lax.rem(me, 4))
+
+    def place(chunk):
+        return LAYERS - 1 - chunk // per_layer, rows_of(lax.rem(chunk, per_layer))
+
+    def inner_copies(chunk):
+        level, rows = place(chunk)
+        slot = lax.rem(chunk, 4)
+        return [
+            pltpu.make_async_copy(array.at[level, rows, :], inner.at[slot, index], inner_sem.at[slot, index])
+            for index, array in enumerate((weights, first, second))
+        ]
+
+    def rep_copy(chunk):
+        return to_rep(step_own.at[chunk], step_got.at[chunk], rep_send.at[chunk], rep_got.at[chunk])
+
+    def change(grad, first_old, second_old):
+        new_first = ADAM_ONE * first_old + (1.0 - ADAM_ONE) * grad
+        new_second = ADAM_TWO * second_old + (1.0 - ADAM_TWO) * grad * grad
+        return new_first * (1.0 / (1.0 - ADAM_ONE**STEP_COUNT)) / (jnp.sqrt(new_second * (1.0 / (1.0 - ADAM_TWO**STEP_COUNT))) + ADAM_EPSILON)
+
+    def stage_core(chunk):
+        own_copy(grads_last, chunk, 0).wait()
+        core_copy(grads_last, chunk, 0).wait_recv()
+        for there in range(4):
+            for side in range(2):
+                own[chunk, there, side] = own[chunk, there, side] + got_core[chunk, there, side]
+        y_copy(chunk).start()
+        for copy in inner_copies(chunk):
+            copy.start()
+
+    def stage_y(chunk):
+        y_copy(chunk).wait_recv()
+        for there in range(4):
+            own[chunk, there, y] = own[chunk, there, y] + got_y[chunk, there]
+        for hop in range(1, 4):
+            z_copy(chunk, hop).start()
+
+    def stage_z(chunk):
+        for hop in range(1, 4):
+            z_copy(chunk, hop).wait_recv()
+        for copy in inner_copies(chunk):
+            copy.wait()
+        total = own[chunk, z, y].astype(F32)
+        for hop in range(3):
+            total = total + got_z[chunk, hop].astype(F32)
+        level, rows = place(chunk)
+        grad_out[level, rows, :] = total
+        slot = lax.rem(chunk, 4)
+        step = change(total, inner[slot, 1], inner[slot, 2]) + WEIGHT_DECAY * inner[slot, 0]
+        step_own[chunk] = (LR_INNER * step).astype(BF16)
+        rep_copy(chunk).start()
+
+    def stage_rep(chunk):
+        rep_copy(chunk).wait_recv()
+        level, rows = place(chunk)
+        mean_out[level, rows, :] = 0.5 * (step_own[chunk].astype(F32) + step_got[chunk].astype(F32))
+
+    def small_rep_copy():
+        return to_rep(small_step, small_step_got, small_rep.at[0], small_rep.at[1])
+
+    def small_back(step):
+        peer = lax.rem(me + step, devices)
+        return to_dp(small_own, small_out.at[me], back_send.at[peer], back_sem.at[me], peer)
+
+    def small_sum():
+        total = small[me]
+
+        def add(step, total):
+            peer = lax.rem(me + step, devices)
+            pltpu.make_async_copy(small_got.at[peer], small_got.at[peer], small_sem.at[peer]).wait()
+            return total + small_got[peer]
+
+        total = lax.fori_loop(1, devices, add, total)
+        small_own[0] = total
+        small_step[...] = (LR_SMALL * change(total, small_first[me], small_second[me])).astype(BF16)
+        small_rep_copy().start()
+
+    def small_spread():
+        small_rep_copy().wait_recv()
+        small_own[1] = 0.5 * (small_step[...].astype(F32) + small_step_got[...].astype(F32))
+        small_out[me] = small_own[...]
+
+        def send(step, carry):
+            small_back(step).start()
+            return carry
+
+        lax.fori_loop(1, devices, send, 0)
+
+    def turn(now, carry):
+        for lag, stage in ((0, stage_core), (2, stage_y), (3, stage_z), (4, stage_rep)):
+
+            @pl.when((now >= lag) & (now < chunks + lag))
+            def _():
+                stage(now - lag)
+
+        pl.when(now == 2)(small_sum)
+        pl.when(now == 5)(small_spread)
+        return carry
+
+    lax.fori_loop(0, chunks + 4, turn, 0)
+
+    def drain(chunk, carry):
+        core_copy(grads_last, chunk, 0).wait_send()
+        y_copy(chunk).wait_send()
+        for hop in range(1, 4):
+            z_copy(chunk, hop).wait_send()
+        rep_copy(chunk).wait_send()
+        return carry
+
+    lax.fori_loop(0, chunks, drain, 0)
+
+    def small_drain(step, carry):
+        peer = lax.rem(me + step, devices)
+        small_copy(step).wait_send()
+        small_back(step).wait_send()
+        pltpu.make_async_copy(small_own, small_out.at[peer], back_sem.at[peer]).wait()
+        return carry
+
+    lax.fori_loop(1, devices, small_drain, 0)
+    small_rep_copy().wait_send()
+
+
+def settle(grads, weights, first, second, small, small_first, small_second):
+    block_rows = weights.shape[1]
+    chunks = LAYERS * block_rows // CHUNK
+    anywhere = pl.BlockSpec(memory_space=pl.ANY)
+    devices = 16
+    piece = (CHUNK, D)
+    return pl.pallas_call(
+        functools.partial(settle_kernel, block_rows),
+        out_shape=[
+            jax.ShapeDtypeStruct(weights.shape, F32),
+            jax.ShapeDtypeStruct(weights.shape, F32),
+            jax.ShapeDtypeStruct((devices, 2, SLICE, LANES), F32),
+        ],
+        in_specs=[anywhere] * 5 + [VMEM] * 3,
+        out_specs=[VMEM] * 3,
+        scratch_shapes=[
+            pltpu.VMEM((chunks, 4, 2) + piece, BF16),
+            pltpu.VMEM((chunks, 4, 2) + piece, BF16),
+            pltpu.VMEM((chunks, 4) + piece, BF16),
+            pltpu.VMEM((chunks, 3) + piece, BF16),
+            pltpu.VMEM((4, 3) + piece, F32),
+            pltpu.VMEM((chunks,) + piece, BF16),
+            pltpu.VMEM((chunks,) + piece, BF16),
+            pltpu.VMEM((devices, SLICE, LANES), F32),
+            pltpu.VMEM((2, SLICE, LANES), F32),
+            pltpu.VMEM((SLICE, LANES), BF16),
+            pltpu.VMEM((SLICE, LANES), BF16),
+            DMA((chunks,)),
+            DMA((chunks,)),
+            DMA((chunks,)),
+            DMA((chunks,)),
+            DMA((chunks,)),
+            DMA((chunks, 3)),
+            DMA((chunks, 3)),
+            DMA((4, 3)),
+            DMA((chunks,)),
+            DMA((chunks,)),
+            DMA((devices,)),
+            DMA((devices,)),
+            DMA((devices,)),
+            DMA((devices,)),
+            DMA((2,)),
+        ],
+        compiler_params=pltpu.CompilerParams(collective_id=3, has_side_effects=True, vmem_limit_bytes=63 << 20),
+        name="settle",
+    )(*[array.reshape(4, 2, 2, block_rows, D) for array in grads], weights, first, second, small, small_first, small_second)
+
+
+def sliced(array):
+    flat = array.reshape(-1)
+    return jnp.pad(flat, (0, 16 * SLICE * LANES - flat.shape[0])).reshape(16, SLICE, LANES)
+
+
+def unsliced(array, shape):
+    return array.reshape(-1)[: shape[0] * shape[1]].reshape(shape)
+
+
 def dense(a, b, dims=NN):
     return mm(a, b, dims)
 
@@ -582,11 +829,14 @@
     return grad_in, jnp.concatenate(parts, axis=0), grad_small
 
 
+def moments(first, second, grad):
+    return ADAM_ONE * first + (1.0 - ADAM_ONE) * grad, ADAM_TWO * second + (1.0 - ADAM_TWO) * grad * grad
+
+
 def adam(weights, first, second, grad, rate, decay):
     correct_one = 1.0 - ADAM_ONE**STEP_COUNT
     correct_two = 1.0 - ADAM_TWO**STEP_COUNT
-    new_first = ADAM_ONE * first + (1.0 - ADAM_ONE) * grad
-    new_second = ADAM_TWO * second + (1.0 - ADAM_TWO) * grad * grad
+    new_first, new_second = moments(first, second, grad)
     step = new_first / correct_one / (jnp.sqrt(new_second / correct_two) + ADAM_EPSILON)
     return new_first, new_second, rate * (step + decay * weights)
 
@@ -622,14 +872,23 @@
     grad_parts, small_parts = [None] * LAYERS, [None] * LAYERS
     for level in reversed(range(LAYERS)):
         gradient, grad_rows, small_parts[level] = backward_layer(count, gradient, held[level], small_params[level], marks, states[level], 2)
-        grad_parts[level] = lax.psum_scatter(grad_rows, "dp", scatter_dimension=0, tiled=True).astype(F32)
-    grad_big = jnp.stack(grad_parts)
-    grad_small = lax.psum(jnp.stack(small_parts), "dp")
-    new_first, new_second, delta_big = adam(weights, first_big[0], second_big[0], grad_big, LR_INNER, WEIGHT_DECAY)
-    new_first_small, new_second_small, delta_small = adam(small_params, first_small[0], second_small[0], grad_small, LR_SMALL, 0.0)
-    reps = lax.axis_size("rep")
-    mean_big = lax.psum(delta_big.astype(BF16), "rep").astype(F32) / reps
-    mean_small = lax.psum(delta_small.astype(BF16), "rep").astype(F32) / reps
+        grad_parts[level] = grad_rows
+    small_parts = jnp.stack(small_parts)
+    if count == 16:
+        grad_big, mean_big, small_both = settle(
+            grad_parts[::-1], weights, first_big[0], second_big[0], sliced(small_parts), sliced(first_small[0]), sliced(second_small[0])
+        )
+        grad_small, mean_small = [unsliced(small_both[:, which], small_parts.shape) for which in range(2)]
+    else:
+        grad_big = jnp.stack([lax.psum_scatter(rows, "dp", scatter_dimension=0, tiled=True).astype(F32) for rows in grad_parts])
+        grad_small = lax.psum(small_parts, "dp")
+        reps = lax.axis_size("rep")
+        delta_big = adam(weights, first_big[0], second_big[0], grad_big, LR_INNER, WEIGHT_DECAY)[2]
+        delta_small = adam(small_params, first_small[0], second_small[0], grad_small, LR_SMALL, 0.0)[2]
+        mean_big = lax.psum(delta_big.astype(BF16), "rep").astype(F32) / reps
+        mean_small = lax.psum(delta_small.astype(BF16), "rep").astype(F32) / reps
+    new_first, new_second = moments(first_big[0], second_big[0], grad_big)
+    new_first_small, new_second_small = moments(first_small[0], second_small[0], grad_small)
     outer_big_new = MOMENTUM * outer_big + mean_big
     outer_small_new = MOMENTUM * outer_small + mean_small
     weights_new = weights - LR_OUTER * (mean_big + MOMENTUM * outer_big_new)

time: 913 us -> 708 us (0.78)
  waiting for transfers between devices: 566 us -> 167 us
  Pallas kernels: 168 us -> 363 us
  local copies, waits for them, and re-layouts: 8.75 us -> 39.4 us
  other arithmetic: 42.1 us -> 28.7 us
    reduce_scatter x2 -> x0, waiting for transfers between devices: 286 us -> none  [shards(): lax.psum_scatter(grad_rows, 'dp', scatter_dimension=0, tiled=True)]
    pallas_call x0 -> x1, Pallas kernels: none -> 195 us  [settle(): pl.pallas_call(functools.partial(settle_kernel, block_rows), out_shape=[j...]
    psum x2 -> x0, waiting for transfers between devices: 111 us -> none  [the longest x1 66.2 us: shards(): grad_small = lax.psum(jnp.stack(small_parts), 'dp')]
    unnamed x96 -> x120, local copies, waits for them, and re-layouts: 1.01 us -> 24.3 us
  transfers between devices with their start and end apart: 6 -> 2, of which waited for: 6 -> 2; matrix products, arithmetic and copies ran while one was open for 7% -> 3% of each run, Pallas kernels for 5% -> 7%
where the time goes in v2:
time: 708 us; the launch traced here: 698 us
  Pallas kernels  363 us (51%)
  waiting for transfers between devices  167 us (24%)
  matrix products  84.4 us (12%)
  local copies, waits for them, and re-layouts  39.4 us (6%)
  other arithmetic  28.7 us (4%)
  between operations  15.1 us (2%)
    pallas_call x1, Pallas kernels, settle(): pl.pallas_call(functools.partial(settle_kernel, block_rows), out_shape=[j...  195 us
    all_gather x2, waiting for transfers between devices, shards(): lax.all_gather(weights[level].astype(BF16), 'dp', axis=0, tiled=True)  167 us
    pallas_call x2, Pallas kernels, attention_backward(): pl.pallas_call(functools.partial(backward_kernel, count, piece), out_shap...  86.4 us
    dot_general x36, matrix products, mm(): return lax.dot_general(a, b, dims, preferred_element_type=F32)  84.4 us
    pallas_call x2, Pallas kernels, attention_forward(): pl.pallas_call(functools.partial(forward_kernel, count, piece), out_shape...  81.6 us
    unnamed x120, local copies, waits for them, and re-layouts  24.3 us
  transfers between devices with their start and end apart: 2, of which 2 were waited for; matrix products, arithmetic and copies ran while one was open for 3% of the time, Pallas kernels for 7%

profile of v2, /device:TPU:0, one launch (start us, length us, event | category | flops | bytes accessed | tf_op | source)
XLA Modules:
  0.0 698.5 jit_solution(13878635540493840945)
XLA Ops:
  7.2 2.2 convert.6
  9.4 1.3 fusion.75
  18.3 105.4 %all-gather.5.cloned.1.call-done = bf16[1,9216,768]{2,1,0:T(8,128)(2,1)} async-done(((bf16[1,576,768]{2,1,0:T(8,128)(2,1)}), bf16[1,9216,768]{2,1,0:T(8,128)(2,1)}) %all-gather.5.cloned.1.call-update) | async-done | bytes 14155792 | tf_op jit(solution)/shard_map/all_gather | solution.py:860
  123.8 1.6 convolution_convert_fusion.15
  125.4 1.6 fusion.52
  127.0 1.6 fusion.51
  129.5 47.7 %attend_forward.2 = (bf16[1,2,64,768]{3,2,1,0:T(8,128)(2,1)}, bf16[3,1024,128]{2,1,0:T(8,128)(2,1)}, f32[128,128]{1,0:T(8,128)}, f32[128,128]{1,0:T(8,128)}, f32...) custom-call(bf16[3,2,64,768]{3,2,1,0:T(8,128)(2,1)} %pad_maximum_fus, ...), custom_call_target="tpu_custom_call" | custom-call | tf_op jit(solution)/shard_map/attend_forward/pallas_call | solution.py:439
  177.2 1.8 fusion.81
  179.2 4.0 fusion.13
  183.3 4.9 fusion.82
  188.5 61.3 %all-gather.7.cloned.1.call-done = bf16[1,9216,768]{2,1,0:T(8,128)(2,1)} async-done(((bf16[1,576,768]{2,1,0:T(8,128)(2,1)}), bf16[1,9216,768]{2,1,0:T(8,128)(2,1)}) %all-gather.7.cloned.1.call-update) | async-done | bytes 14155792 | tf_op jit(solution)/shard_map/all_gather | solution.py:860
  249.8 1.6 convolution_convert_fusion.14
  251.4 1.6 fusion.54
  253.0 1.6 fusion.53
  255.5 33.8 %attend_forward.3 = (bf16[1,2,64,768]{3,2,1,0:T(8,128)(2,1)}, bf16[3,1024,128]{2,1,0:T(8,128)(2,1)}, f32[128,128]{1,0:T(8,128)}, f32[128,128]{1,0:T(8,128)}, f32...) custom-call(bf16[3,2,64,768]{3,2,1,0:T(8,128)(2,1)} %pad_maximum_fus, ...), custom_call_target="tpu_custom_call" | custom-call | tf_op jit(solution)/shard_map/attend_forward/pallas_call | solution.py:439
  289.3 1.8 fusion.83
  291.4 4.0 fusion.12
  295.4 4.0 fusion.84
  301.6 5.0 convert_reduce_fusion
  306.6 3.9 multiply_reduce_fusion.2
  311.4 2.6 convolution_convert_fusion.13
  314.0 41.1 %attend_backward.2 = (bf16[3,2,64,768]{3,2,1,0:T(8,128)(2,1)}, f32[6,2,256]{2,1,0:T(2,128)}) custom-call(bf16[1,2,64,768]{3,2,1,0:T(8,128)(2,1)} %bitcast.248, s32[2,64,1]{2,1,0:T(8,128)} %copy.39.low_col, s32[2,64,1]{2,1,0:T(8,128)} %copy.40.high_col, s32[2,1,64]{2,1,0:T(1,128)} %bitcast.257, s32[2,1,64]{2,1,0:T(1,128)} %bitcast.255, ...), custom_call_target="tpu_custom_call" | custom-call | tf_op jit(solution)/shard_map/attend_backward/pallas_call | solution.py:466
  355.1 1.7 convert_reduce_fusion.4
  357.9 1.9 fusion.56
  359.8 1.8 convolution_add_fusion.3
  361.6 2.5 multiply_reduce_fusion.3
  365.6 4.9 convert_reduce_fusion.1
  370.5 4.2 multiply_reduce_fusion.4
  375.6 2.6 convolution_convert_fusion.12
  378.2 45.3 %attend_backward.3 = (bf16[3,2,64,768]{3,2,1,0:T(8,128)(2,1)}, f32[6,2,256]{2,1,0:T(2,128)}) custom-call(bf16[1,2,64,768]{3,2,1,0:T(8,128)(2,1)} %bitcast.247, s32[2,64,1]{2,1,0:T(8,128)} %copy.39.low_col, s32[2,64,1]{2,1,0:T(8,128)} %copy.40.high_col, s32[2,1,64]{2,1,0:T(1,128)} %bitcast.258, s32[2,1,64]{2,1,0:T(1,128)} %bitcast.256, ...), custom_call_target="tpu_custom_call" | custom-call | tf_op jit(solution)/shard_map/attend_backward/pallas_call | solution.py:466
  423.5 1.7 convert_reduce_fusion.8
  426.4 1.5 fusion.34
  438.5 1.3 constant_dynamic-update-slice_fusion.3
  442.0 1.3 constant_dynamic-update-slice_fusion
  452.4 1.3 constant_dynamic-update-slice_fusion.2
  458.3 1.5 fusion.1
  459.8 1.6 fusion
  461.4 1.5 fusion.33
  463.0 1.5 fusion.32
  464.5 1.6 fusion.31
  466.1 3.7 fusion.3
  469.8 3.9 fusion.2
  473.7 195.5 %settle.1 = (f32[2,576,768]{2,1,0:T(8,128)}, f32[2,576,768]{2,1,0:T(8,128)}, f32[16,2,16,128]{3,2,1,0:T(8,128)}) custom-call(bf16[4,2,2,576,768]{4,3,2,1,0:T(8,128)(2,1)} %bitcast.50.grads_last, bf16[4,2,2,576,768]{4,3,2,1,0:T(8,128)(2,1)} %bitcast.208, f32[2,576,768]{2,1,0:T(8,128)} %weights.1, f32[2,576,768]{2,1,0:T(8,128)} %bitcast.209, ...), custom_call_target="tpu_custom_call" | custom-call | tf_op jit(solution)/shard_map/settle/pallas_call | solution.py:686
  671.2 8.7 %fusion.15 = (f32[1,2,576,768]{3,2,1,0:T(8,128)}, f32[1,2,576,768]{3,2,1,0:T(8,128)}) fusion(f32[2,576,768]{2,1,0:T(8,128)} %get-tuple-element.78, f32[1,2,576,768]{3,2,1,0:T(8,128)} %param.17, f32[1,2,576,768]{3,2,1,0:T(8,128)} %param.16), kind=kLoop, calls=%fused_computation.24 | loop fusion | flops 6193152 | bytes 17694720 | tf_op jit(solution)/shard_map/broadcast_in_dim | solution.py:901
  680.8 4.4 fusion.70
  685.2 1.8 fusion.55
  687.0 1.8 convolution_add_fusion.1
  688.9 2.6 fusion.44
  (206 shorter events, 46.9 us)
Async XLA Ops:
  7.2 116.6 %all-gather.5.cloned.1.call-start = ((), (), s32[]{:S(2)}) async-start(), calls=%async_computation | async-start | bytes 15040512 | tf_op jit(solution)/shard_map/all_gather | solution.py:860
  10.7 1.2 copy-start.16
  10.7 5.2 copy-start.18
  10.7 5.9 copy-start.20
  10.7 6.9 copy-start.6
  10.7 113.0 %copy-start.7 = (bf16[1,2,1,64,768]{4,3,2,1,0:T(8,128)(2,1)S(1)}, bf16[1,2,1,64,768]{4,3,2,1,0:T(8,128)(2,1)}, u32[]{:S(2)}) copy-start(bf16[1,2,1,64,768]{4,3,2,1,0:T(8,128)(2,1)} %param.11) | copy-start | bytes 589828
  10.8 239.0 %all-gather.7.cloned.1.call-start = ((), (), s32[]{:S(2)}) async-start(), calls=%async_computation.1 | async-start | bytes 15040512 | tf_op jit(solution)/shard_map/all_gather | solution.py:860
  17.6 165.7 %copy-start.31 = (f32[768]{0:T(1024)}, f32[768]{0:T(1024)S(1)}, u32[]{:S(2)}) copy-start(f32[768]{0:T(1024)S(1)} %get-tuple-element.128) | copy-start | bytes 9220
  17.6 277.8 %copy-start.29 = (f32[768]{0:T(1024)}, f32[768]{0:T(1024)S(1)}, u32[]{:S(2)}) copy-start(f32[768]{0:T(1024)S(1)} %get-tuple-element.120) | copy-start | bytes 9220
  179.0 195.6 %copy-start.34 = (f32[128]{0:T(128)}, f32[128]{0:T(128)S(1)}, u32[]{:S(2)}) copy-start(f32[128]{0:T(128)S(1)} %broadcast_multiply_fusion.3) | copy-start | bytes 1540
  179.2 195.4 %copy-start.40 = (f32[128]{0:T(128)}, f32[128]{0:T(128)S(1)}, u32[]{:S(2)}) copy-start(f32[128]{0:T(128)S(1)} %fusion.62) | copy-start | bytes 1540
  183.3 4.9 copy-start.46
  291.2 19.3 %copy-start.36 = (f32[128]{0:T(128)}, f32[128]{0:T(128)S(1)}, u32[]{:S(2)}) copy-start(f32[128]{0:T(128)S(1)} %broadcast_multiply_fusion.1) | copy-start | bytes 1540
  291.4 19.1 %copy-start.42 = (f32[128]{0:T(128)}, f32[128]{0:T(128)S(1)}, u32[]{:S(2)}) copy-start(f32[128]{0:T(128)S(1)} %fusion.64) | copy-start | bytes 1540
  295.4 6.2 copy-start.49
  301.6 5.0 copy-start.24
  311.4 43.7 %copy-start.12 = (bf16[128,768]{1,0:T(8,128)(2,1)}, bf16[128,768]{1,0:T(8,128)(2,1)S(1)}, u32[]{:S(2)}) copy-start(bf16[128,768]{1,0:T(8,128)(2,1)S(1)} %get-tuple-element.148) | copy-start | bytes 589828
  357.9 3.7 copy-start.10
  364.2 1.4 copy-start.47
  365.1 5.3 copy-start.26
  370.5 4.2 copy-start.4
  374.9 48.6 %copy-start.44 = (f32[128]{0:T(128)}, f32[128]{0:T(128)S(1)}, u32[]{:S(2)}) copy-start(f32[128]{0:T(128)S(1)} %negate_multiply_fusion) | copy-start | bytes 1540
  375.6 47.9 %copy-start.14 = (bf16[128,768]{1,0:T(8,128)(2,1)}, bf16[128,768]{1,0:T(8,128)(2,1)S(1)}, u32[]{:S(2)}) copy-start(bf16[128,768]{1,0:T(8,128)(2,1)S(1)} %get-tuple-element.144) | copy-start | bytes 589828
  423.5 2.9 copy-start.11
  423.5 4.4 copy-start.39
  425.3 10.6 %copy-start.33 = (f32[768]{0:T(1024)S(1)}, f32[768]{0:T(1024)}, u32[]{:S(2)}) copy-start(f32[768]{0:T(1024)} %get-tuple-element.109) | copy-start | bytes 9220
  426.4 30.1 %copy-start.8 = (bf16[1,2,64,768]{3,2,1,0:T(8,128)(2,1)}, bf16[1,2,64,768]{3,2,1,0:T(8,128)(2,1)S(1)}, u32[]{:S(2)}) copy-start(bf16[1,2,64,768]{3,2,1,0:T(8,128)(2,1)S(1)} %get-tuple-element.163) | copy-start | bytes 589828
  457.0 1.2 copy-start.5
  457.1 1.2 copy-start.32
  458.2 1.5 copy-start.27
  458.2 1.5 copy-start.48
  461.4 8.4 %copy-start.1 = (bf16[9216,768]{1,0:T(8,128)(2,1)}, bf16[9216,768]{1,0:T(8,128)(2,1)S(1)}, u32[]{:S(2)}) copy-start(bf16[9216,768]{1,0:T(8,128)(2,1)S(1)} %fusion) | copy-start | bytes 42467332
  461.4 3.1 copy-start.13
  461.4 3.1 copy-start.23
  463.0 3.1 copy-start.30
  463.0 3.1 copy-start.37
  463.0 3.1 copy-start.43
  466.1 3.7 copy-start.25
  466.1 3.7 copy-start.50
  473.7 196.7 %copy-start.19 = (f32[1,2,9612]{2,1,0:T(2,128)S(1)}, f32[1,2,9612]{2,1,0:T(2,128)}, u32[]{:S(2)}) copy-start(f32[1,2,9612]{2,1,0:T(2,128)} %param.18) | copy-start | bytes 230692
  473.7 196.7 %copy-start.21 = (f32[1,2,9612]{2,1,0:T(2,128)S(1)}, f32[1,2,9612]{2,1,0:T(2,128)}, u32[]{:S(2)}) copy-start(f32[1,2,9612]{2,1,0:T(2,128)} %param.19) | copy-start | bytes 230692
  671.2 8.8 %copy-start.17 = (f32[2,9612]{1,0:T(2,128)S(1)}, f32[2,9612]{1,0:T(2,128)}, u32[]{:S(2)}) copy-start(f32[2,9612]{1,0:T(2,128)} %param.15) | copy-start | bytes 230692
  671.2 8.8 %copy-start.28 = (f32[2,9612]{1,0:T(2,128)S(1)}, f32[2,9612]{1,0:T(2,128)}, u32[]{:S(2)}) copy-start(f32[2,9612]{1,0:T(2,128)} %param.21) | copy-start | bytes 230692
  671.2 9.5 %copy-start = (f32[2,576,768]{2,1,0:T(8,128)S(1)}, f32[2,576,768]{2,1,0:T(8,128)}, u32[]{:S(2)}) copy-start(f32[2,576,768]{2,1,0:T(8,128)} %weights.1) | copy-start | bytes 10616836
  671.2 9.5 %copy-start.2 = (f32[2,576,768]{2,1,0:T(8,128)S(1)}, f32[2,576,768]{2,1,0:T(8,128)}, u32[]{:S(2)}) copy-start(f32[2,576,768]{2,1,0:T(8,128)} %param.20) | copy-start | bytes 10616836
  671.2 9.6 %copy-start.3 = (f32[2,576,768]{2,1,0:T(8,128)S(1)}, f32[2,576,768]{2,1,0:T(8,128)}, u32[]{:S(2)}) copy-start(f32[2,576,768]{2,1,0:T(8,128)} %get-tuple-element.80) | copy-start | bytes 10616836
  680.8 4.4 copy-start.9
  685.2 3.6 copy-start.45
  (5 other events, 5.4 us)
Sparse Core Ops, SparseCore 0:
  10.9 112.8 all-gather.4
  126.6 123.1 all-gather.6

commit v3 on v2

--- a/solution.py
+++ b/solution.py
@@ -487,6 +487,180 @@
     )(grads, *marks, taps, *kept)
 
 
+def gather_kernel(shard, out, local_sem, z_send, z_got, x_send, x_got, y_send, y_got, core_send, core_got):
+    me = lax.axis_index("dp")
+    x = lax.axis_index("rep")
+    core, y, z = lax.rem(me, 2), lax.rem(me // 2, 2), me // 4
+    half = shard.shape[0] // 2
+    part = half // 2
+
+    barrier = pltpu.get_barrier_semaphore()
+
+    def peer(axis, sign=1):
+        if axis == "x":
+            return {"rep": 1 - x}
+        if axis == "y":
+            return {"dp": me + 2 - 4 * y}
+        if axis == "core":
+            return {"dp": me + 1 - 2 * core}
+        return {"dp": me + 4 * sign}
+
+    for axis in ("x", "y", "core"):
+        pl.semaphore_signal(barrier, inc=1, device_id=peer(axis), device_id_type=MESH)
+    for sign in (1, -1):
+
+        @pl.when((z + sign >= 0) & (z + sign < 4))
+        def _():
+            pl.semaphore_signal(barrier, inc=1, device_id=peer("z", sign), device_id_type=MESH)
+
+    pl.semaphore_wait(barrier, 4 + jnp.where((z > 0) & (z < 3), 1, 0))
+
+    def rows(side, sub):
+        return pl.ds(pl.multiple_of(side * half + sub * part, part), part)
+
+    def side_rows(side):
+        return pl.ds(pl.multiple_of(side * half, half), half)
+
+    def remote(source, target, send, receive, where):
+        return pltpu.make_async_remote_copy(source, target, send, receive, device_id=where, device_id_type=MESH)
+
+    def spot(plane, row, side, sub):
+        return out.at[plane, row, core, rows(side, sub), :]
+
+    def move(axis, plane, row, side, sub, source=None):
+        target = spot(plane, row, side, sub)
+        source = target if source is None else source
+        if axis == "core":
+            return remote(source, target, core_send.at[plane, row, side, sub], core_got, peer("core"))
+        send, receive = (x_send, x_got) if axis == "x" else (y_send, y_got)
+        return remote(source, target, send.at[plane, row, side, sub], receive.at[plane, row, side, sub], peer(axis))
+
+    def climb(plane, sub, sign, source=None):
+        target = spot(plane, y, x, sub)
+        way = 0 if sign > 0 else 1
+        return remote(target if source is None else source, target, z_send.at[plane, sub, way], z_got.at[plane, sub], peer("z", sign))
+
+    own = pltpu.make_async_copy(shard, out.at[z, y, core], local_sem)
+    own.start()
+    for sub in range(2):
+        for sign in (1, -1):
+
+            @pl.when((z + sign >= 0) & (z + sign < 4))
+            def _():
+                climb(z, sub, sign, shard.at[rows(x, sub), :]).start()
+
+        move("y", z, y, x, sub, shard.at[rows(x, sub), :]).start()
+    for side in range(2):
+        for sub in range(2):
+            move("core", z, y, side, sub, shard.at[rows(side, sub), :]).start()
+
+    def at_distance(distance, act):
+        for sign in (1, -1):
+            plane = z - sign * distance
+
+            @pl.when((plane >= 0) & (plane < 4))
+            def _():
+                act(plane, sign)
+
+    def from_z(plane, sign):
+        for sub in range(2):
+            climb(plane, sub, sign).wait_recv()
+
+            @pl.when((z + sign >= 0) & (z + sign < 4))
+            def _():
+                climb(plane, sub, sign).start()
+
+            for axis in ("x", "y", "core"):
+                move(axis, plane, y, x, sub).start()
+
+    def take(axis, plane, row, side, sub, onward=None):
+        move(axis, plane, row, side, sub).wait_recv()
+        if onward is not None:
+            move(onward, plane, row, side, sub).start()
+        move("core", plane, row, side, sub).start()
+
+    def first_square(plane, sign):
+        take("x", plane, y, 1 - x, 0, "y")
+        take("y", plane, 1 - y, x, 1, "x")
+        take("y", plane, 1 - y, x, 0)
+        take("x", plane, y, 1 - x, 1)
+
+    def second_square(plane, sign):
+        take("y", plane, 1 - y, 1 - x, 0)
+        take("x", plane, 1 - y, 1 - x, 1)
+
+    at_distance(1, from_z)
+    for sub in range(2):
+        take("y", z, 1 - y, x, sub, "x")
+    at_distance(2, from_z)
+    at_distance(1, first_square)
+    at_distance(3, from_z)
+    at_distance(2, first_square)
+    for sub in range(2):
+        take("x", z, 1 - y, 1 - x, sub)
+    at_distance(1, second_square)
+    at_distance(3, first_square)
+    at_distance(2, second_square)
+    at_distance(3, second_square)
+    own.wait()
+
+    def finish(plane, sign):
+        for sub in range(2):
+
+            @pl.when((z + sign >= 0) & (z + sign < 4))
+            def _():
+                climb(plane, sub, sign).wait_send()
+
+            move("x", plane, y, x, sub).wait_send()
+            move("y", plane, y, x, sub).wait_send()
+        move("y", plane, y, 1 - x, 0).wait_send()
+        move("x", plane, 1 - y, x, 1).wait_send()
+
+    for distance in (1, 2, 3):
+        at_distance(distance, finish)
+    for sub in range(2):
+        for sign in (1, -1):
+
+            @pl.when((z + sign >= 0) & (z + sign < 4))
+            def _():
+                climb(z, sub, sign).wait_send()
+
+        move("y", z, y, x, sub).wait_send()
+        move("x", z, 1 - y, x, sub).wait_send()
+
+    def core_sent(index, carry):
+        plane, row, side, sub = index // 8, lax.rem(index // 4, 2), lax.rem(index // 2, 2), lax.rem(index, 2)
+        move("core", plane, row, side, sub).wait_send()
+        return carry
+
+    lax.fori_loop(0, 32, core_sent, 0)
+    column = out.at[:, :, 1 - core]
+    pltpu.make_async_copy(column, column, core_got).wait()
+
+
+def gather(shard):
+    block_rows = shard.shape[0]
+    return pl.pallas_call(
+        gather_kernel,
+        out_shape=jax.ShapeDtypeStruct((4, 2, 2, block_rows, D), BF16),
+        in_specs=[VMEM],
+        out_specs=pl.BlockSpec(memory_space=pl.ANY),
+        scratch_shapes=[
+            DMA,
+            DMA((4, 2, 2)),
+            DMA((4, 2)),
+            DMA((4, 2, 2, 2)),
+            DMA((4, 2, 2, 2)),
+            DMA((4, 2, 2, 2)),
+            DMA((4, 2, 2, 2)),
+            DMA((4, 2, 2, 2)),
+            DMA,
+        ],
+        compiler_params=pltpu.CompilerParams(collective_id=4, has_side_effects=True),
+        name="gather",
+    )(shard).reshape(16 * block_rows, D)
+
+
 CHUNK = 48
 SLICE = 16
 
@@ -857,7 +1031,10 @@
     count = lax.axis_size("dp")
     piece = hidden.shape[3]
     total = MICRO * piece
-    held = [lax.all_gather(weights[level].astype(BF16), "dp", axis=0, tiled=True) for level in range(LAYERS)]
+    low_weights = weights.astype(BF16)
+    held = [lax.all_gather(low_weights[level], "dp", axis=0, tiled=True) for level in range(LAYERS)]
+    if count == 16:
+        held[0] = gather(low_weights[0])
     edges = bounds[0, :, 0, :]
     low_edges, high_edges = edges[:, :-1], edges[:, 1:]
     marks = (low_edges[:, :, None], high_edges[:, :, None], low_edges[:, None, :], high_edges[:, None, :])

time: 708 us -> 674 us (0.952)
  waiting for transfers between devices: 167 us -> 0.02 us
  Pallas kernels: 363 us -> 476 us
  local copies, waits for them, and re-layouts: 39.4 us -> 56.9 us
    all_gather x2 -> x1, waiting for transfers between devices: 167 us -> 0.01 us  [shards(): lax.all_gather(low_weights[level], 'dp', axis=0, tiled=True)]
    pallas_call x0 -> x1, Pallas kernels: none -> 117 us  [gather(): pl.pallas_call(gather_kernel, out_shape=jax.ShapeDtypeStruct((4, 2, 2, bl...]
    unnamed x120 -> x206, local copies, waits for them, and re-layouts: 24.3 us -> 29.2 us
  transfers between devices with their start and end apart: 2 -> 1, of which waited for: 2 -> 0; matrix products, arithmetic and copies ran while one was open for 3% -> 4% of each run, Pallas kernels for 7% -> 24%
where the time goes in v3:
time: 674 us; the launch traced here: 666 us
  Pallas kernels  476 us (71%)
  matrix products  86.8 us (13%)
  local copies, waits for them, and re-layouts  56.9 us (8%)
  other arithmetic  30.7 us (5%)
  between operations  15.4 us (2%)
    pallas_call x1, Pallas kernels, settle(): pl.pallas_call(functools.partial(settle_kernel, block_rows), out_shape=[j...  196 us
    pallas_call x1, Pallas kernels, gather(): pl.pallas_call(gather_kernel, out_shape=jax.ShapeDtypeStruct((4, 2, 2, bl...  117 us
    dot_general x36, matrix products, mm(): return lax.dot_general(a, b, dims, preferred_element_type=F32)  86.8 us
    pallas_call x2, Pallas kernels, attention_backward(): pl.pallas_call(functools.partial(backward_kernel, count, piece), out_shap...  86 us
    pallas_call x2, Pallas kernels, attention_forward(): pl.pallas_call(functools.partial(forward_kernel, count, piece), out_shape...  77.4 us
    unnamed x206, local copies, waits for them, and re-layouts  29.2 us
  transfers between devices with their start and end apart: 1, of which 0 were waited for; matrix products, arithmetic and copies ran while one was open for 4% of the time, Pallas kernels for 24%

profile of v3, /device:TPU:0, one launch (start us, length us, event | category | flops | bytes accessed | tf_op | source)
XLA Modules:
  0.0 665.7 jit_solution(12365920616021823222)
XLA Ops:
  7.2 2.2 convert_element_type.178
  18.5 116.8 %gather.1 = bf16[4,2,2,576,768]{4,3,2,1,0:T(8,128)(2,1)} custom-call(bf16[576,768]{1,0:T(8,128)(2,1)} %get-tuple-element.159.shard), custom_call_target="tpu_custom_call" | custom-call | tf_op jit(solution)/shard_map/gather/pallas_call | solution.py:643
  135.4 2.3 slice.239
  140.3 42.7 %attend_forward.2 = (bf16[1,2,64,768]{3,2,1,0:T(8,128)(2,1)}, bf16[3,1024,128]{2,1,0:T(8,128)(2,1)}, f32[128,128]{1,0:T(8,128)}, f32[128,128]{1,0:T(8,128)}, f32...) custom-call(bf16[3,2,64,768]{3,2,1,0:T(8,128)(2,1)} %pad_maximum_fus, ...), custom_call_target="tpu_custom_call" | custom-call | tf_op jit(solution)/shard_map/attend_forward/pallas_call | solution.py:439
  183.7 1.8 fusion.96
  186.9 4.0 fusion.16
  191.0 4.0 fusion.97
  197.1 1.7 convolution_convert_fusion.14
  198.9 1.6 fusion.68
  200.5 1.6 fusion.67
  203.1 34.7 %attend_forward.3 = (bf16[1,2,64,768]{3,2,1,0:T(8,128)(2,1)}, bf16[3,1024,128]{2,1,0:T(8,128)(2,1)}, f32[128,128]{1,0:T(8,128)}, f32[128,128]{1,0:T(8,128)}, f32...) custom-call(bf16[3,2,64,768]{3,2,1,0:T(8,128)(2,1)} %pad_maximum_fus, ...), custom_call_target="tpu_custom_call" | custom-call | tf_op jit(solution)/shard_map/attend_forward/pallas_call | solution.py:439
  237.9 1.8 fusion.98
  240.0 4.0 fusion.19
  244.0 4.1 fusion.99
  250.3 4.9 convert_reduce_fusion
  255.3 4.2 multiply_reduce_fusion.2
  261.8 2.5 convolution_convert_fusion.13
  264.3 40.6 %attend_backward.2 = (bf16[3,2,64,768]{3,2,1,0:T(8,128)(2,1)}, f32[6,2,256]{2,1,0:T(2,128)}) custom-call(bf16[1,2,64,768]{3,2,1,0:T(8,128)(2,1)} %bitcast.234, s32[2,64,1]{2,1,0:T(8,128)} %copy.39.low_col, s32[2,64,1]{2,1,0:T(8,128)} %copy.40.high_col, s32[2,1,64]{2,1,0:T(1,128)} %bitcast.243, s32[2,1,64]{2,1,0:T(1,128)} %bitcast.241, ...), custom_call_target="tpu_custom_call" | custom-call | tf_op jit(solution)/shard_map/attend_backward/pallas_call | solution.py:466
  304.9 1.7 convert_reduce_fusion.4
  307.8 2.0 fusion.70
  309.8 1.8 convolution_add_fusion.3
  311.7 2.5 multiply_reduce_fusion.3
  315.6 5.0 convert_reduce_fusion.1
  320.6 4.1 multiply_reduce_fusion.4
  327.2 2.5 convolution_convert_fusion.12
  329.6 45.3 %attend_backward.3 = (bf16[3,2,64,768]{3,2,1,0:T(8,128)(2,1)}, f32[6,2,256]{2,1,0:T(2,128)}) custom-call(bf16[1,2,64,768]{3,2,1,0:T(8,128)(2,1)} %bitcast.233, s32[2,64,1]{2,1,0:T(8,128)} %copy.39.low_col, s32[2,64,1]{2,1,0:T(8,128)} %copy.40.high_col, s32[2,1,64]{2,1,0:T(1,128)} %bitcast.244, s32[2,1,64]{2,1,0:T(1,128)} %bitcast.242, ...), custom_call_target="tpu_custom_call" | custom-call | tf_op jit(solution)/shard_map/attend_backward/pallas_call | solution.py:466
  375.0 1.7 convert_reduce_fusion.8
  376.7 2.0 fusion.91
  379.9 1.5 fusion.44
  381.5 1.5 fusion.42
  398.0 1.4 stack.56
  414.6 1.5 pad_maximum_fusion.2
  416.1 1.6 reshape.361
  417.7 1.6 pad.21
  419.3 1.7 convolution_add_fusion.1
  421.0 1.6 fusion.46
  423.9 1.6 fusion.48
  425.5 1.6 fusion.38
  427.1 3.7 fusion.1
  430.7 3.9 fusion
  434.6 1.5 fusion.41
  436.2 1.5 fusion.40
  437.7 1.5 fusion.39
  439.3 3.7 fusion.3
  442.9 3.9 fusion.2
  446.8 195.7 %settle.1 = (f32[2,576,768]{2,1,0:T(8,128)}, f32[2,576,768]{2,1,0:T(8,128)}, f32[16,2,16,128]{3,2,1,0:T(8,128)}) custom-call(bf16[4,2,2,576,768]{4,3,2,1,0:T(8,128)(2,1)} %bitcast.50.grads_last, bf16[4,2,2,576,768]{4,3,2,1,0:T(8,128)(2,1)} %bitcast.188, f32[2,576,768]{2,1,0:T(8,128)} %weights.1, f32[2,576,768]{2,1,0:T(8,128)} %bitcast.189, ...), custom_call_target="tpu_custom_call" | custom-call | tf_op jit(solution)/shard_map/settle/pallas_call | solution.py:860
  644.6 8.7 %fusion.21 = (f32[1,2,576,768]{3,2,1,0:T(8,128)}, f32[1,2,576,768]{3,2,1,0:T(8,128)}) fusion(f32[2,576,768]{2,1,0:T(8,128)} %get-tuple-element.78, f32[1,2,576,768]{3,2,1,0:T(8,128)} %param.17, f32[1,2,576,768]{3,2,1,0:T(8,128)} %param.16), kind=kLoop, calls=%fused_computation.26 | loop fusion | flops 6193152 | bytes 17694720 | tf_op jit(solution)/shard_map/broadcast_in_dim | solution.py:1078
  654.2 4.4 fusion.86
  (291 shorter events, 62.1 us)
Async XLA Ops:
  7.2 189.9 %all-gather.3.cloned.1.call-start = ((), (), s32[]{:S(2)}) async-start(), calls=%async_computation | async-start | bytes 15040512 | tf_op jit(solution)/shard_map/all_gather | solution.py:1035
  9.4 7.6 %copy-start.40 = (f32[1,2,9612]{2,1,0:T(2,128)S(1)}, f32[1,2,9612]{2,1,0:T(2,128)}, u32[]{:S(2)}) copy-start(f32[1,2,9612]{2,1,0:T(2,128)} %param.18) | copy-start | bytes 230692
  10.7 7.0 %copy-start.42 = (f32[1,2,9612]{2,1,0:T(2,128)S(1)}, f32[1,2,9612]{2,1,0:T(2,128)}, u32[]{:S(2)}) copy-start(f32[1,2,9612]{2,1,0:T(2,128)} %param.19) | copy-start | bytes 230692
  138.4 52.5 %copy-start.53 = (f32[768]{0:T(1024)}, f32[768]{0:T(1024)S(1)}, u32[]{:S(2)}) copy-start(f32[768]{0:T(1024)S(1)} %get-tuple-element.128) | copy-start | bytes 9220
  138.4 57.3 %copy-start.56 = (f32[768]{0:T(1024)}, f32[768]{0:T(1024)S(1)}, u32[]{:S(2)}) copy-start(f32[768]{0:T(1024)S(1)} %get-tuple-element.125) | copy-start | bytes 9220
  139.1 43.9 %copy-start.23 = (bf16[1,2,1,64,768]{4,3,2,1,0:T(8,128)(2,1)S(1)}, bf16[1,2,1,64,768]{4,3,2,1,0:T(8,128)(2,1)}, u32[]{:S(2)}) copy-start(bf16[1,2,1,64,768]{4,3,2,1,0:T(8,128)(2,1)} %param.13) | copy-start | bytes 589828
  139.1 43.9 %copy-start.70 = (f32[2,64]{1,0:T(2,128)S(1)}, f32[2,64]{1,0:T(2,128)}, u32[]{:S(2)}) copy-start(f32[2,64]{1,0:T(2,128)} %copy-done.69) | copy-start | bytes 1540
  185.5 5.4 copy-start.3
  185.6 5.4 copy-start.62
  186.3 4.7 copy-start.78
  190.9 4.1 copy-start.89
  200.5 37.4 %copy-start.2 = (f32[128,768]{1,0:T(8,128)S(1)}, f32[128,768]{1,0:T(8,128)}, u32[]{:S(2)}) copy-start(f32[128,768]{1,0:T(8,128)} %copy-done.1) | copy-start | bytes 1179652
  200.5 37.4 %copy-start.57 = (f32[768]{0:T(1024)S(1)}, f32[768]{0:T(1024)}, u32[]{:S(2)}) copy-start(f32[768]{0:T(1024)} %copy-done.56) | copy-start | bytes 9220
  200.5 37.4 %copy-start.61 = (f32[128]{0:T(128)S(1)}, f32[128]{0:T(128)}, u32[]{:S(2)}) copy-start(f32[128]{0:T(128)} %copy-done.60) | copy-start | bytes 1540
  200.5 37.4 %copy-start.68 = (f32[128]{0:T(128)S(1)}, f32[128]{0:T(128)}, u32[]{:S(2)}) copy-start(f32[128]{0:T(128)} %copy-done.67) | copy-start | bytes 1540
  200.5 37.4 %copy-start.72 = (f32[768]{0:T(1024)S(1)}, f32[768]{0:T(1024)}, u32[]{:S(2)}) copy-start(f32[768]{0:T(1024)} %get-tuple-element.122) | copy-start | bytes 9220
  239.7 19.7 %copy-start.6 = (f32[128,768]{1,0:T(8,128)}, f32[128,768]{1,0:T(8,128)S(1)}, u32[]{:S(2)}) copy-start(f32[128,768]{1,0:T(8,128)S(1)} %get-tuple-element.185) | copy-start | bytes 1179652
  239.7 19.7 %copy-start.65 = (f32[128]{0:T(128)}, f32[128]{0:T(128)S(1)}, u32[]{:S(2)}) copy-start(f32[128]{0:T(128)S(1)} %broadcast_multiply_fusion.1) | copy-start | bytes 1540
  239.9 19.5 %copy-start.81 = (f32[128]{0:T(128)}, f32[128]{0:T(128)S(1)}, u32[]{:S(2)}) copy-start(f32[128]{0:T(128)S(1)} %fusion.80) | copy-start | bytes 1540
  240.0 4.0 copy-start.71
  244.0 6.3 copy-start.92
  244.0 4.3 copy-start.24
  244.0 4.3 copy-start.77
  244.0 5.1 copy-start.55
  250.3 5.0 copy-start.46
  255.2 4.2 copy-start.14
  307.8 3.9 copy-start.20
  307.8 3.9 copy-start.32
  307.8 3.9 copy-start.18
  307.8 3.9 copy-start.11
  315.2 5.4 copy-start.48
  315.6 5.0 copy-start.4
  315.6 5.0 copy-start.63
  315.6 5.0 copy-start.79
  320.6 4.2 copy-start.16
  320.6 4.2 copy-start.86
  325.1 49.9 %copy-start.83 = (f32[128]{0:T(128)}, f32[128]{0:T(128)S(1)}, u32[]{:S(2)}) copy-start(f32[128]{0:T(128)S(1)} %negate_multiply_fusion) | copy-start | bytes 1540
  379.9 12.9 %copy-start.58 = (f32[768]{0:T(1024)S(1)}, f32[768]{0:T(1024)}, u32[]{:S(2)}) copy-start(f32[768]{0:T(1024)} %get-tuple-element.109) | copy-start | bytes 9220
  430.7 3.9 copy-start.21
  430.7 3.9 copy-start.27
  439.3 3.7 copy-start.47
  446.8 197.0 %copy-start.41 = (f32[1,2,9612]{2,1,0:T(2,128)S(1)}, f32[1,2,9612]{2,1,0:T(2,128)}, u32[]{:S(2)}) copy-start(f32[1,2,9612]{2,1,0:T(2,128)} %param.18) | copy-start | bytes 230692
  446.8 197.0 %copy-start.43 = (f32[1,2,9612]{2,1,0:T(2,128)S(1)}, f32[1,2,9612]{2,1,0:T(2,128)}, u32[]{:S(2)}) copy-start(f32[1,2,9612]{2,1,0:T(2,128)} %param.19) | copy-start | bytes 230692
  644.6 8.8 %copy-start.39 = (f32[2,9612]{1,0:T(2,128)S(1)}, f32[2,9612]{1,0:T(2,128)}, u32[]{:S(2)}) copy-start(f32[2,9612]{1,0:T(2,128)} %param.15) | copy-start | bytes 230692
  644.6 8.8 %copy-start.50 = (f32[2,9612]{1,0:T(2,128)S(1)}, f32[2,9612]{1,0:T(2,128)}, u32[]{:S(2)}) copy-start(f32[2,9612]{1,0:T(2,128)} %param.21) | copy-start | bytes 230692
  644.6 9.5 %copy-start = (f32[2,576,768]{2,1,0:T(8,128)S(1)}, f32[2,576,768]{2,1,0:T(8,128)}, u32[]{:S(2)}) copy-start(f32[2,576,768]{2,1,0:T(8,128)} %weights.1) | copy-start | bytes 10616836
  644.6 9.5 %copy-start.8 = (f32[2,576,768]{2,1,0:T(8,128)S(1)}, f32[2,576,768]{2,1,0:T(8,128)}, u32[]{:S(2)}) copy-start(f32[2,576,768]{2,1,0:T(8,128)} %param.20) | copy-start | bytes 10616836
  644.6 9.6 %copy-start.9 = (f32[2,576,768]{2,1,0:T(8,128)S(1)}, f32[2,576,768]{2,1,0:T(8,128)}, u32[]{:S(2)}) copy-start(f32[2,576,768]{2,1,0:T(8,128)} %get-tuple-element.80) | copy-start | bytes 10616836
  (47 other events, 112.3 us)
Sparse Core Ops, SparseCore 0:
  10.9 162.9 all-gather.2

commit v4 on v3

--- a/solution.py
+++ b/solution.py
@@ -662,15 +662,25 @@
 
 
 CHUNK = 48
-SLICE = 16
-
-
-def settle_kernel(
-    block_rows, grads_last, grads_first, weights, first, second, small, small_first, small_second,
-    grad_out, mean_out, small_out,
-    own, got_core, got_y, got_z, inner, step_own, step_got, small_got, small_own, small_step, small_step_got,
-    own_sem, core_send, core_got, y_send, y_got, z_send, z_got, inner_sem, rep_send, rep_got, small_send, small_sem, back_send, back_sem, small_rep,
-):
+RING = 8
+LINES = 13
+MATES = ("low_in", "low_comb", "low_up", "low_act", "low_grads", "low_branch", "low_hidden", "low_down", "gain_one", "shift_one", "gain_two", "shift_two", "taps")
+
+
+def change(grad, first_old, second_old):
+    new_first = ADAM_ONE * first_old + (1.0 - ADAM_ONE) * grad
+    new_second = ADAM_TWO * second_old + (1.0 - ADAM_TWO) * grad * grad
+    return new_first * (1.0 / (1.0 - ADAM_ONE**STEP_COUNT)) / (jnp.sqrt(new_second * (1.0 / (1.0 - ADAM_TWO**STEP_COUNT))) + ADAM_EPSILON)
+
+
+def settle_kernel(block_rows, *refs):
+    count = len(MATES)
+    mates = [dict(zip(MATES, refs[level * count : (level + 1) * count])) for level in range(LAYERS)]
+    (
+        weights, first, second, small_first, small_second, grad_out, mean_out, small_out,
+        turned, right, staged, own, got_core, got_y, got_z, inner, step_own, step_got, small, small_got, small_own, small_step, small_step_got,
+        core_send, core_got, y_send, y_got, z_send, z_got, inner_sem, rep_send, rep_got, small_send, small_sem, back_send, back_sem, small_rep,
+    ) = refs[LAYERS * count :]
     me = lax.axis_index("dp")
     other_rep = 1 - lax.axis_index("rep")
     core, y, z = lax.rem(me, 2), lax.rem(me // 2, 2), me // 4
@@ -686,7 +696,6 @@
 
     lax.fori_loop(1, devices, signal, 0)
     pl.semaphore_signal(barrier, inc=1, device_id={"rep": other_rep}, device_id_type=MESH)
-    pl.semaphore_wait(barrier, devices)
 
     def to_dp(source, target, send, receive, peer):
         return pltpu.make_async_remote_copy(source, target, send, receive, device_id={"dp": peer}, device_id_type=MESH)
@@ -694,24 +703,49 @@
     def to_rep(source, target, send, receive):
         return pltpu.make_async_remote_copy(source, target, send, receive, device_id={"rep": other_rep}, device_id_type=MESH)
 
-    def rows_of(part):
-        return pl.ds(pl.multiple_of(part * CHUNK, CHUNK), CHUNK)
-
-    def core_copy(source, chunk, part):
-        return to_dp(source.at[:, :, 1 - core, rows_of(part), :], got_core.at[chunk], core_send.at[chunk], core_got.at[chunk], me + 1 - 2 * core)
-
-    def own_copy(source, chunk, part):
-        return pltpu.make_async_copy(source.at[:, :, core, rows_of(part), :], own.at[chunk], own_sem.at[chunk])
-
-    for order, source in enumerate((grads_last, grads_first)):
-
-        def begin(part, carry):
-            chunk = order * per_layer + part
-            core_copy(source, chunk, part).start()
-            own_copy(source, chunk, part).start()
-            return carry
-
-        lax.fori_loop(0, per_layer, begin, 0)
+    def spot(slot):
+        return lax.rem(slot, RING)
+
+    features = D * 2 + FF * 2
+    for order, level in enumerate(reversed(range(LAYERS))):
+        mate = mates[level]
+        at = order * features
+        for name in MATES[:4]:
+            for part in range(mate[name].shape[1] // LANES):
+                turned[at : at + LANES, :] = mate[name][:, part * LANES : (part + 1) * LANES].T
+                at += LANES
+        for part in range(3):
+            right[order * 6 + part] = mate["low_grads"][part]
+        for part, name in enumerate(MATES[5:8]):
+            right[order * 6 + 3 + part] = mate[name][...]
+
+    def put(level, line, row):
+        index = level * LINES + line
+        small[index // 2, index % 2 : index % 2 + 1, :] = row
+
+    def column_sum(array):
+        return jnp.sum(array.astype(F32), axis=0, keepdims=True)
+
+    for level in range(LAYERS):
+        mate = mates[level]
+        put(level, 0, column_sum(mate["low_grads"][0]))
+        put(level, 1, column_sum(mate["low_grads"][2]))
+        put(level, 2, column_sum(mate["low_branch"][...]))
+        put(level, 3, column_sum(mate["low_down"][...]))
+        for line, name in enumerate(MATES[8:12]):
+            put(level, 4 + line, mate[name][...])
+        for part in range(FF // D):
+            put(level, 8 + part, column_sum(mate["low_up"][:, part * D : (part + 1) * D]))
+        line = jnp.zeros((1, D), F32)
+        for head in range(HEADS):
+            taps = jnp.concatenate([mate["taps"][head // 2][head % 2 : head % 2 + 1], jnp.zeros((1, D - 2 * LANES), F32)], axis=1)
+            taps = jnp.where(iota((1, D), 1) < TAPS, taps, 0.0)
+            line = line + (pltpu.roll(taps, TAPS * head, 1) if head else taps)
+        put(level, 12, line)
+    for index in range(LAYERS * LINES, 2 * devices):
+        small[index // 2, index % 2 : index % 2 + 1, :] = jnp.zeros((1, D), F32)
+
+    pl.semaphore_wait(barrier, devices)
 
     def small_copy(step):
         peer = lax.rem(me + step, devices)
@@ -723,15 +757,19 @@
 
     lax.fori_loop(1, devices, small_begin, 0)
 
+    def core_copy(chunk):
+        return to_dp(staged.at[lax.rem(chunk, 2)], got_core.at[spot(chunk)], core_send.at[lax.rem(chunk, 2)], core_got.at[spot(chunk)], me + 1 - 2 * core)
+
     def y_copy(chunk):
-        return to_dp(own.at[chunk, :, 1 - y], got_y.at[chunk], y_send.at[chunk], y_got.at[chunk], me + 2 - 4 * y)
+        return to_dp(own.at[spot(chunk), :, 1 - y], got_y.at[spot(chunk)], y_send.at[spot(chunk)], y_got.at[spot(chunk)], me + 2 - 4 * y)
 
     def z_copy(chunk, hop):
         there = lax.rem(z + hop, 4)
-        return to_dp(own.at[chunk, there, y], got_z.at[chunk, hop - 1], z_send.at[chunk, hop - 1], z_got.at[chunk, hop - 1], there * 4 + lax.rem(me, 4))
+        slot = spot(chunk)
+        return to_dp(own.at[slot, there, y], got_z.at[slot, hop - 1], z_send.at[slot, hop - 1], z_got.at[slot, hop - 1], there * 4 + lax.rem(me, 4))
 
     def place(chunk):
-        return LAYERS - 1 - chunk // per_layer, rows_of(lax.rem(chunk, per_layer))
+        return LAYERS - 1 - chunk // per_layer, pl.ds(pl.multiple_of(lax.rem(chunk, per_layer) * CHUNK, CHUNK), CHUNK)
 
     def inner_copies(chunk):
         level, rows = place(chunk)
@@ -742,49 +780,67 @@
         ]
 
     def rep_copy(chunk):
-        return to_rep(step_own.at[chunk], step_got.at[chunk], rep_send.at[chunk], rep_got.at[chunk])
-
-    def change(grad, first_old, second_old):
-        new_first = ADAM_ONE * first_old + (1.0 - ADAM_ONE) * grad
-        new_second = ADAM_TWO * second_old + (1.0 - ADAM_TWO) * grad * grad
-        return new_first * (1.0 / (1.0 - ADAM_ONE**STEP_COUNT)) / (jnp.sqrt(new_second * (1.0 / (1.0 - ADAM_TWO**STEP_COUNT))) + ADAM_EPSILON)
+        return to_rep(step_own.at[spot(chunk)], step_got.at[spot(chunk)], rep_send.at[spot(chunk)], rep_got.at[spot(chunk)])
+
+    def product(chunk, there, row, side):
+        order = chunk // per_layer
+        block = (there * 2 + row) * 2 + side
+        piece = block * per_layer + lax.rem(chunk, per_layer)
+        narrow = D // CHUNK
+        line = jnp.where(piece < 3 * narrow, lax.rem(piece, narrow), piece - 2 * narrow)
+        group = jnp.where(piece < 4 * narrow, piece // narrow, jnp.where(piece < 4 * narrow + FF // CHUNK, 4, 5))
+        rows = pl.ds(pl.multiple_of(order * features + line * CHUNK, 16), CHUNK)
+        return mm(turned[rows, :], right[order * 6 + group]).astype(BF16)
+
+    def stage_product(chunk):
+        for there in range(4):
+            for row in range(2):
+                staged[lax.rem(chunk, 2), there, row] = product(chunk, there, row, 1 - core)
+        core_copy(chunk).start()
+        for there in range(4):
+            for row in range(2):
+                own[spot(chunk), there, row] = product(chunk, there, row, core)
 
     def stage_core(chunk):
-        own_copy(grads_last, chunk, 0).wait()
-        core_copy(grads_last, chunk, 0).wait_recv()
+        core_copy(chunk).wait()
+        slot = spot(chunk)
         for there in range(4):
             for side in range(2):
-                own[chunk, there, side] = own[chunk, there, side] + got_core[chunk, there, side]
+                own[slot, there, side] = own[slot, there, side] + got_core[slot, there, side]
         y_copy(chunk).start()
+
+    def stage_y(chunk):
+        y_copy(chunk).wait_recv()
+        slot = spot(chunk)
+        for there in range(4):
+            own[slot, there, y] = own[slot, there, y] + got_y[slot, there]
+        for hop in range(1, 4):
+            z_copy(chunk, hop).start()
         for copy in inner_copies(chunk):
             copy.start()
 
-    def stage_y(chunk):
-        y_copy(chunk).wait_recv()
-        for there in range(4):
-            own[chunk, there, y] = own[chunk, there, y] + got_y[chunk, there]
-        for hop in range(1, 4):
-            z_copy(chunk, hop).start()
-
     def stage_z(chunk):
+        y_copy(chunk).wait_send()
         for hop in range(1, 4):
             z_copy(chunk, hop).wait_recv()
         for copy in inner_copies(chunk):
             copy.wait()
-        total = own[chunk, z, y].astype(F32)
+        total = own[spot(chunk), z, y].astype(F32)
         for hop in range(3):
-            total = total + got_z[chunk, hop].astype(F32)
+            total = total + got_z[spot(chunk), hop].astype(F32)
         level, rows = place(chunk)
         grad_out[level, rows, :] = total
         slot = lax.rem(chunk, 4)
         step = change(total, inner[slot, 1], inner[slot, 2]) + WEIGHT_DECAY * inner[slot, 0]
-        step_own[chunk] = (LR_INNER * step).astype(BF16)
+        step_own[spot(chunk)] = (LR_INNER * step).astype(BF16)
         rep_copy(chunk).start()
 
     def stage_rep(chunk):
-        rep_copy(chunk).wait_recv()
+        for hop in range(1, 4):
+            z_copy(chunk, hop).wait_send()
+        rep_copy(chunk).wait()
         level, rows = place(chunk)
-        mean_out[level, rows, :] = 0.5 * (step_own[chunk].astype(F32) + step_got[chunk].astype(F32))
+        mean_out[level, rows, :] = 0.5 * (step_own[spot(chunk)].astype(F32) + step_got[spot(chunk)].astype(F32))
 
     def small_rep_copy():
         return to_rep(small_step, small_step_got, small_rep.at[0], small_rep.at[1])
@@ -794,14 +850,12 @@
         return to_dp(small_own, small_out.at[me], back_send.at[peer], back_sem.at[me], peer)
 
     def small_sum():
-        total = small[me]
-
         def add(step, total):
             peer = lax.rem(me + step, devices)
             pltpu.make_async_copy(small_got.at[peer], small_got.at[peer], small_sem.at[peer]).wait()
             return total + small_got[peer]
 
-        total = lax.fori_loop(1, devices, add, total)
+        total = lax.fori_loop(1, devices, add, small[me])
         small_own[0] = total
         small_step[...] = (LR_SMALL * change(total, small_first[me], small_second[me])).astype(BF16)
         small_rep_copy().start()
@@ -818,27 +872,17 @@
         lax.fori_loop(1, devices, send, 0)
 
     def turn(now, carry):
-        for lag, stage in ((0, stage_core), (2, stage_y), (3, stage_z), (4, stage_rep)):
+        for lag, stage in ((0, stage_product), (1, stage_core), (3, stage_y), (5, stage_z), (7, stage_rep)):
 
             @pl.when((now >= lag) & (now < chunks + lag))
             def _():
                 stage(now - lag)
 
-        pl.when(now == 2)(small_sum)
-        pl.when(now == 5)(small_spread)
+        pl.when(now == 4)(small_sum)
+        pl.when(now == 7)(small_spread)
         return carry
 
-    lax.fori_loop(0, chunks + 4, turn, 0)
-
-    def drain(chunk, carry):
-        core_copy(grads_last, chunk, 0).wait_send()
-        y_copy(chunk).wait_send()
-        for hop in range(1, 4):
-            z_copy(chunk, hop).wait_send()
-        rep_copy(chunk).wait_send()
-        return carry
-
-    lax.fori_loop(0, chunks, drain, 0)
+    lax.fori_loop(0, chunks + 7, turn, 0)
 
     def small_drain(step, carry):
         peer = lax.rem(me + step, devices)
@@ -851,43 +895,46 @@
     small_rep_copy().wait_send()
 
 
-def settle(grads, weights, first, second, small, small_first, small_second):
+def settle(mates, weights, first, second, small_first, small_second):
     block_rows = weights.shape[1]
-    chunks = LAYERS * block_rows // CHUNK
     anywhere = pl.BlockSpec(memory_space=pl.ANY)
     devices = 16
     piece = (CHUNK, D)
+    tokens = mates[0]["low_in"].shape[0]
     return pl.pallas_call(
         functools.partial(settle_kernel, block_rows),
         out_shape=[
             jax.ShapeDtypeStruct(weights.shape, F32),
             jax.ShapeDtypeStruct(weights.shape, F32),
-            jax.ShapeDtypeStruct((devices, 2, SLICE, LANES), F32),
+            jax.ShapeDtypeStruct((devices, 2, 2, D), F32),
         ],
-        in_specs=[anywhere] * 5 + [VMEM] * 3,
+        in_specs=[VMEM] * (LAYERS * len(MATES)) + [anywhere] * 3 + [VMEM] * 2,
         out_specs=[VMEM] * 3,
         scratch_shapes=[
-            pltpu.VMEM((chunks, 4, 2) + piece, BF16),
-            pltpu.VMEM((chunks, 4, 2) + piece, BF16),
-            pltpu.VMEM((chunks, 4) + piece, BF16),
-            pltpu.VMEM((chunks, 3) + piece, BF16),
+            pltpu.VMEM((LAYERS * 2 * (D + FF), tokens), BF16),
+            pltpu.VMEM((LAYERS * 6, tokens, D), BF16),
+            pltpu.VMEM((2, 4, 2) + piece, BF16),
+            pltpu.VMEM((RING, 4, 2) + piece, BF16),
+            pltpu.VMEM((RING, 4, 2) + piece, BF16),
+            pltpu.VMEM((RING, 4) + piece, BF16),
+            pltpu.VMEM((RING, 3) + piece, BF16),
             pltpu.VMEM((4, 3) + piece, F32),
-            pltpu.VMEM((chunks,) + piece, BF16),
-            pltpu.VMEM((chunks,) + piece, BF16),
-            pltpu.VMEM((devices, SLICE, LANES), F32),
-            pltpu.VMEM((2, SLICE, LANES), F32),
-            pltpu.VMEM((SLICE, LANES), BF16),
-            pltpu.VMEM((SLICE, LANES), BF16),
-            DMA((chunks,)),
-            DMA((chunks,)),
-            DMA((chunks,)),
-            DMA((chunks,)),
-            DMA((chunks,)),
-            DMA((chunks, 3)),
-            DMA((chunks, 3)),
+            pltpu.VMEM((RING,) + piece, BF16),
+            pltpu.VMEM((RING,) + piece, BF16),
+            pltpu.VMEM((devices, 2, D), F32),
+            pltpu.VMEM((devices, 2, D), F32),
+            pltpu.VMEM((2, 2, D), F32),
+            pltpu.VMEM((2, D), BF16),
+            pltpu.VMEM((2, D), BF16),
+            DMA((2,)),
+            DMA((RING,)),
+            DMA((RING,)),
+            DMA((RING,)),
+            DMA((RING, 3)),
+            DMA((RING, 3)),
             DMA((4, 3)),
-            DMA((chunks,)),
-            DMA((chunks,)),
+            DMA((RING,)),
+            DMA((RING,)),
             DMA((devices,)),
             DMA((devices,)),
             DMA((devices,)),
@@ -896,16 +943,16 @@
         ],
         compiler_params=pltpu.CompilerParams(collective_id=3, has_side_effects=True, vmem_limit_bytes=63 << 20),
         name="settle",
-    )(*[array.reshape(4, 2, 2, block_rows, D) for array in grads], weights, first, second, small, small_first, small_second)
+    )(*[mate[name] for mate in mates for name in MATES], weights, first, second, small_first, small_second)
 
 
 def sliced(array):
-    flat = array.reshape(-1)
-    return jnp.pad(flat, (0, 16 * SLICE * LANES - flat.shape[0])).reshape(16, SLICE, LANES)
+    wide = jnp.pad(array, ((0, 0), (0, LINES * D - array.shape[1]))).reshape(LAYERS * LINES, D)
+    return jnp.pad(wide, ((0, 32 - LAYERS * LINES), (0, 0))).reshape(16, 2, D)
 
 
 def unsliced(array, shape):
-    return array.reshape(-1)[: shape[0] * shape[1]].reshape(shape)
+    return array.reshape(32, D)[: LAYERS * LINES].reshape(LAYERS, LINES * D)[:, : shape[1]]
 
 
 def dense(a, b, dims=NN):
@@ -964,43 +1011,30 @@
     _, pull_two = jax.vjp(layer_norm, resid_two, blocks[6], blocks[7])
     grad_two, grad_gain_two, grad_shift_two = pull_two(grad_output)
     low_down = grad_two.astype(BF16)
-    grad_bias_down = jnp.sum(low_down.astype(F32), axis=0)
     grad_act = dense(low_down, down_weight, NT)
     _, pull_gelu = jax.vjp(jax.nn.gelu, upward)
     low_up = pull_gelu(grad_act)[0].astype(BF16)
-    grad_bias_up = jnp.sum(low_up.astype(F32), axis=0)
     grad_hidden = grad_two + dense(low_up, up_weight)
     _, pull_one = jax.vjp(layer_norm, resid_one, blocks[4], blocks[5])
     grad_one, grad_gain_one, grad_shift_one = pull_one(grad_hidden)
     low_branch = grad_one.astype(BF16)
-    grad_bias_out = jnp.sum(low_branch.astype(F32), axis=0)
     grad_comb = dense(low_branch, out_weight, NT).astype(BF16)
     low_grads, grad_taps = attention_backward(count, grad_comb.reshape(1, MICRO, piece, D), marks, pair_taps(conv_taps), kept, ident)
     low_grads = low_grads.reshape(3, total, D)
-    grad_bias_q = jnp.sum(low_grads[0].astype(F32), axis=0)
-    grad_bias_v = jnp.sum(low_grads[2].astype(F32), axis=0)
     grad_in = grad_one + sum(dense(low_grads[part], proj[part], NT) for part in range(3))
-    parts = [dense(low_in, low_grads[part], TN).astype(BF16) for part in range(3)]
-    parts = parts + [
-        dense(low_comb, low_branch, TN).astype(BF16),
-        dense(low_up, low_hidden, TN).astype(BF16),
-        dense(low_act, low_down, TN).astype(BF16),
-    ]
-    grad_small = jnp.concatenate(
-        [
-            grad_bias_q,
-            grad_bias_v,
-            grad_bias_out,
-            grad_bias_down,
-            grad_gain_one,
-            grad_shift_one,
-            grad_gain_two,
-            grad_shift_two,
-            grad_bias_up,
-            grad_taps[:, :, :TAPS].reshape(-1),
-        ]
-    )
-    return grad_in, jnp.concatenate(parts, axis=0), grad_small
+    vectors = [vector.reshape(1, D) for vector in (grad_gain_one, grad_shift_one, grad_gain_two, grad_shift_two)]
+    values = (low_in, low_comb, low_up, low_act, low_grads, low_branch, low_hidden, low_down, *vectors, grad_taps)
+    return grad_in, dict(zip(MATES, values))
+
+
+def plain_grads(mate):
+    parts = [dense(mate["low_in"], mate["low_grads"][part], TN) for part in range(3)]
+    parts = parts + [dense(mate[left], mate[right], TN) for left, right in (("low_comb", "low_branch"), ("low_up", "low_hidden"), ("low_act", "low_down"))]
+    sums = [mate["low_grads"][0], mate["low_grads"][2], mate["low_branch"], mate["low_down"]]
+    sums = [jnp.sum(one.astype(F32), axis=0) for one in sums]
+    sums = sums + [mate[name].reshape(-1) for name in MATES[8:12]]
+    sums = sums + [jnp.sum(mate["low_up"].astype(F32), axis=0), mate["taps"][:, :, :TAPS].reshape(-1)]
+    return jnp.concatenate(parts, axis=0).astype(BF16), jnp.concatenate(sums)
 
 
 def moments(first, second, grad):
@@ -1046,19 +1080,16 @@
         activation, state = forward_layer(count, activation, held[level], small_params[level], marks, 1)
         states.append(state)
     gradient = cotangent[0, :, 0].reshape(total, D).astype(F32) * valid
-    grad_parts, small_parts = [None] * LAYERS, [None] * LAYERS
+    mates = [None] * LAYERS
     for level in reversed(range(LAYERS)):
-        gradient, grad_rows, small_parts[level] = backward_layer(count, gradient, held[level], small_params[level], marks, states[level], 2)
-        grad_parts[level] = grad_rows
-    small_parts = jnp.stack(small_parts)
+        gradient, mates[level] = backward_layer(count, gradient, held[level], small_params[level], marks, states[level], 2)
     if count == 16:
-        grad_big, mean_big, small_both = settle(
-            grad_parts[::-1], weights, first_big[0], second_big[0], sliced(small_parts), sliced(first_small[0]), sliced(second_small[0])
-        )
-        grad_small, mean_small = [unsliced(small_both[:, which], small_parts.shape) for which in range(2)]
+        grad_big, mean_big, small_both = settle(mates, weights, first_big[0], second_big[0], sliced(first_small[0]), sliced(second_small[0]))
+        grad_small, mean_small = [unsliced(small_both[:, which], small_params.shape) for which in range(2)]
     else:
-        grad_big = jnp.stack([lax.psum_scatter(rows, "dp", scatter_dimension=0, tiled=True).astype(F32) for rows in grad_parts])
-        grad_small = lax.psum(small_parts, "dp")
+        rows, sums = zip(*[plain_grads(mate) for mate in mates])
+        grad_big = jnp.stack([lax.psum_scatter(one, "dp", scatter_dimension=0, tiled=True).astype(F32) for one in rows])
+        grad_small = lax.psum(jnp.stack(sums), "dp")
         reps = lax.axis_size("rep")
         delta_big = adam(weights, first_big[0], second_big[0], grad_big, LR_INNER, WEIGHT_DECAY)[2]
         delta_small = adam(small_params, first_small[0], second_small[0], grad_small, LR_SMALL, 0.0)[2]

time: 674 us -> 599 us (0.89)
  Pallas kernels: 476 us -> 442 us
  matrix products: 86.8 us -> 57.5 us
  local copies, waits for them, and re-layouts: 56.9 us -> 47.7 us
    dot_general x36 -> x24, matrix products: 86.8 us -> 57.5 us  [mm(): return lax.dot_general(a, b, dims, preferred_element_type=F32)]
    unnamed x206 -> x106, local copies, waits for them, and re-layouts: 29.2 us -> 5.83 us
    pallas_call x1, Pallas kernels: 117 us -> 98 us  [gather(): pl.pallas_call(gather_kernel, out_shape=jax.ShapeDtypeStruct((4, 2, 2, bl...]
    reshape x5 -> x14, local copies, waits for them, and re-layouts: 4 us -> 14.3 us  [the longest x8 4.69 us: layer_norm(): return centred * lax.rsqrt(variance + 1e-05) * gain_vec + shift_vec]
    pallas_call x1, Pallas kernels: 196 us -> 188 us  [settle(): pl.pallas_call(functools.partial(settle_kernel, block_rows), out_shape=[j...]
  transfers between devices with their start and end apart: 1 -> 1, of which waited for: 0 -> 0; matrix products, arithmetic and copies ran while one was open for 4% -> 8% of each run, Pallas kernels for 24% -> 23%
where the time goes in v4:
time: 599 us; the launch traced here: 591 us
  Pallas kernels  442 us (74%)
  matrix products  57.5 us (10%)
  local copies, waits for them, and re-layouts  47.7 us (8%)
  other arithmetic  28.3 us (5%)
  between operations  15.2 us (3%)
    pallas_call x1, Pallas kernels, settle(): pl.pallas_call(functools.partial(settle_kernel, block_rows), out_shape=[j...  188 us
    pallas_call x1, Pallas kernels, gather(): pl.pallas_call(gather_kernel, out_shape=jax.ShapeDtypeStruct((4, 2, 2, bl...  98 us
    pallas_call x2, Pallas kernels, attention_backward(): pl.pallas_call(functools.partial(backward_kernel, count, piece), out_shap...  85.5 us
    pallas_call x2, Pallas kernels, attention_forward(): pl.pallas_call(functools.partial(forward_kernel, count, piece), out_shape...  70.9 us
    dot_general x24, matrix products, mm(): return lax.dot_general(a, b, dims, preferred_element_type=F32)  57.5 us
  transfers between devices with their start and end apart: 1, of which 0 were waited for; matrix products, arithmetic and copies ran while one was open for 8% of the time, Pallas kernels for 23%

profile of v4, /device:TPU:0, one launch (start us, length us, event | category | flops | bytes accessed | tf_op | source)
XLA Modules:
  0.0 590.8 jit_solution(14855041057310943057)
XLA Ops:
  7.2 2.2 convert_element_type.101
  9.4 1.3 fusion.73
  10.7 98.0 %gather.1 = bf16[4,2,2,576,768]{4,3,2,1,0:T(8,128)(2,1)} custom-call(bf16[576,768]{1,0:T(8,128)(2,1)} %get-tuple-element.148.shard), custom_call_target="tpu_custom_call" | custom-call | tf_op jit(solution)/shard_map/gather/pallas_call | solution.py:643
  108.8 2.3 slice.229
  113.7 1.9 slice_reduce_fusion.17
  116.4 1.4 stack_reshape_reshape.8
  124.6 1.5 pad.25
  126.1 1.6 reshape.358
  127.7 1.5 pad.26
  129.3 1.6 reshape.359.refs_29_
  130.9 1.5 pad.27
  132.5 1.6 reshape.360
  134.0 1.5 pad.28
  135.6 1.6 reshape.361.refs_30_
  137.2 1.6 slice_reduce_fusion.1
  141.6 35.8 %attend_forward.2 = (bf16[1,2,64,768]{3,2,1,0:T(8,128)(2,1)}, bf16[3,1024,128]{2,1,0:T(8,128)(2,1)}, f32[128,128]{1,0:T(8,128)}, f32[128,128]{1,0:T(8,128)}, f32...) custom-call(bf16[3,2,64,768]{3,2,1,0:T(8,128)(2,1)} %pad_maximum_fus, ...), custom_call_target="tpu_custom_call" | custom-call | tf_op jit(solution)/shard_map/attend_forward/pallas_call | solution.py:439
  177.4 1.8 fusion.79
  180.2 1.4 fusion.77
  181.6 5.2 multiply_convert_fusion.1
  186.9 3.5 fusion.80
  192.6 1.7 convolution_convert_fusion.2
  194.4 1.6 fusion.53
  196.0 1.6 fusion.52
  198.6 35.1 %attend_forward.3 = (bf16[1,2,64,768]{3,2,1,0:T(8,128)(2,1)}, bf16[3,1024,128]{2,1,0:T(8,128)(2,1)}, f32[128,128]{1,0:T(8,128)}, f32[128,128]{1,0:T(8,128)}, f32...) custom-call(bf16[3,2,64,768]{3,2,1,0:T(8,128)(2,1)} %pad_maximum_fus, ...), custom_call_target="tpu_custom_call" | custom-call | tf_op jit(solution)/shard_map/attend_forward/pallas_call | solution.py:439
  233.7 1.8 fusion.81
  235.9 4.1 multiply_convert_fusion
  240.1 3.5 fusion.82
  245.3 4.3 fusion.31.refs_15_
  249.6 3.6 multiply_reduce_fusion.2
  254.9 2.5 convolution_convert_fusion.1
  257.4 40.1 %attend_backward.2 = (bf16[3,2,64,768]{3,2,1,0:T(8,128)(2,1)}, f32[6,2,256]{2,1,0:T(2,128)}) custom-call(bf16[1,2,64,768]{3,2,1,0:T(8,128)(2,1)} %bitcast.199, s32[2,64,1]{2,1,0:T(8,128)} %copy.39.low_col, s32[2,64,1]{2,1,0:T(8,128)} %copy.40.high_col, s32[2,1,64]{2,1,0:T(1,128)} %bitcast.208, s32[2,1,64]{2,1,0:T(1,128)} %bitcast.206, ...), custom_call_target="tpu_custom_call" | custom-call | tf_op jit(solution)/shard_map/attend_backward/pallas_call | solution.py:466
  298.7 1.9 fusion.55
  300.6 1.8 convolution_add_fusion.3
  302.4 1.9 multiply_reduce_fusion.3
  305.9 4.2 fusion.24.refs_2_
  310.2 3.6 multiply_reduce_fusion.4
  315.5 2.5 convolution_convert_fusion
  318.0 45.3 %attend_backward.3 = (bf16[3,2,64,768]{3,2,1,0:T(8,128)(2,1)}, f32[6,2,256]{2,1,0:T(2,128)}) custom-call(bf16[1,2,64,768]{3,2,1,0:T(8,128)(2,1)} %bitcast.198, s32[2,64,1]{2,1,0:T(8,128)} %copy.39.low_col, s32[2,64,1]{2,1,0:T(8,128)} %copy.40.high_col, s32[2,1,64]{2,1,0:T(1,128)} %bitcast.209, s32[2,1,64]{2,1,0:T(1,128)} %bitcast.207, ...), custom_call_target="tpu_custom_call" | custom-call | tf_op jit(solution)/shard_map/attend_backward/pallas_call | solution.py:466
  363.4 1.9 fusion.74
  365.3 1.3 fusion.54
  370.7 187.7 %settle.1 = (f32[2,576,768]{2,1,0:T(8,128)}, f32[2,576,768]{2,1,0:T(8,128)}, f32[16,2,2,768]{3,2,1,0:T(2,128)}) custom-call(bf16[128,768]{1,0:T(8,128)(2,1)} %bitcast.184, bf16[128,768]{1,0:T(8,128)(2,1)} %bitcast.189, bf16[128,3072]{1,0:T(8,128)(2,1)} %copy-done.22, bf16[128,3072]{1,0:T(8,128)(2,1)} %copy-done.19, bf16[3,128,768]{2,1,0:T(8,128)(2,1)} %bitcast.172, ...), custom_call_target="tpu_custom_call" | custom-call | tf_op jit(solution)/shard_map/settle/pallas_call | solution.py:904
  558.4 8.2 %fusion.17 = (f32[1,2,576,768]{3,2,1,0:T(8,128)}, f32[1,2,576,768]{3,2,1,0:T(8,128)}) fusion(f32[2,576,768]{2,1,0:T(8,128)} %get-tuple-element.78, f32[1,2,576,768]{3,2,1,0:T(8,128)} %param.17, f32[1,2,576,768]{3,2,1,0:T(8,128)} %param.16), kind=kLoop, calls=%fused_computation.18 | loop fusion | flops 6193152 | bytes 17694720 | tf_op jit(solution)/shard_map/broadcast_in_dim | solution.py:1109
  567.3 1.6 reshape.362
  568.9 1.7 fusion.63
  570.7 1.6 reshape.363
  572.3 1.8 convolution_add_fusion.1
  574.1 1.3 fusion.37
  575.4 7.6 %fusion.68 = (bf16[2,576,768]{2,1,0:T(8,128)(2,1)}, f32[2,576,768]{2,1,0:T(8,128)}, f32[2,576,768]{2,1,0:T(8,128)}) fusion(f32[2,576,768]{2,1,0:T(8,128)S(1)} %copy-done, f32[2,576,768]{2,1,0:T(8,128)} %get-tuple-element.80, f32[2,576,768]{2,1,0:T(8,128)} %param.20), kind=kLoop, calls=%fused_computation.165 | loop fusion | flops 6193152 | bytes 19464192 | tf_op jit(solution)/shard_map/convert_element_type | solution.py:1116
  (176 shorter events, 30.6 us)
Async XLA Ops:
  7.2 185.4 %all-gather.3.cloned.1.call-start = ((), (), s32[]{:S(2)}) async-start(), calls=%async_computation | async-start | bytes 15040512 | tf_op jit(solution)/shard_map/all_gather | solution.py:1069
  108.8 2.4 copy-start.44
  111.2 254.1 %copy-start.1 = (bf16[1,2,2,576,768]{4,3,2,1,0:T(8,128)(2,1)}, bf16[1,2,2,576,768]{4,3,2,1,0:T(8,128)(2,1)S(1)}, u32[]{:S(2)}) copy-start(bf16[1,2,2,576,768]{4,3,2,1,0:T(8,128)(2,1)S(1)} %slice.229) | copy-start | bytes 10616836
  137.2 2.9 copy-start.26
  138.8 52.4 %copy-start.31 = (f32[768]{0:T(1024)}, f32[768]{0:T(1024)S(1)}, u32[]{:S(2)}) copy-start(f32[768]{0:T(1024)S(1)} %get-tuple-element.121) | copy-start | bytes 9220
  179.2 7.6 %copy-start.5 = (f32[128,768]{1,0:T(8,128)}, f32[128,768]{1,0:T(8,128)S(1)}, u32[]{:S(2)}) copy-start(f32[128,768]{1,0:T(8,128)S(1)} %get-tuple-element.169) | copy-start | bytes 1179652
  179.3 7.6 %copy-start.36 = (f32[128]{0:T(128)}, f32[128]{0:T(128)S(1)}, u32[]{:S(2)}) copy-start(f32[128]{0:T(128)S(1)} %broadcast_multiply_fusion.3) | copy-start | bytes 1540
  179.5 7.4 %copy-start.46 = (f32[128]{0:T(128)}, f32[128]{0:T(128)S(1)}, u32[]{:S(2)}) copy-start(f32[128]{0:T(128)S(1)} %fusion.64) | copy-start | bytes 1540
  180.2 6.7 %copy-start.12 = (bf16[128,768]{1,0:T(8,128)(2,1)}, bf16[128,768]{1,0:T(8,128)(2,1)S(1)}, u32[]{:S(2)}) copy-start(bf16[128,768]{1,0:T(8,128)(2,1)S(1)} %fusion.59.refs_6_) | copy-start | bytes 589828
  186.9 3.5 copy-start.19
  190.4 0.8 copy-start.3
  190.4 0.8 copy-start.34
  192.6 1.8 copy-start.13
  192.6 1.8 copy-start.43
  192.6 3.4 copy-start.42
  196.0 37.7 %copy-start.4 = (f32[128,768]{1,0:T(8,128)S(1)}, f32[128,768]{1,0:T(8,128)}, u32[]{:S(2)}) copy-start(f32[128,768]{1,0:T(8,128)} %copy-done.3) | copy-start | bytes 1179652
  196.0 37.7 %copy-start.32 = (f32[768]{0:T(1024)S(1)}, f32[768]{0:T(1024)}, u32[]{:S(2)}) copy-start(f32[768]{0:T(1024)} %copy-done.31) | copy-start | bytes 9220
  196.0 37.7 %copy-start.35 = (f32[128]{0:T(128)S(1)}, f32[128]{0:T(128)}, u32[]{:S(2)}) copy-start(f32[128]{0:T(128)} %copy-done.34) | copy-start | bytes 1540
  196.0 37.7 %copy-start.39 = (f32[128]{0:T(128)S(1)}, f32[128]{0:T(128)}, u32[]{:S(2)}) copy-start(f32[128]{0:T(128)} %copy-done.38) | copy-start | bytes 1540
  196.0 37.7 %copy-start.41 = (f32[768]{0:T(1024)S(1)}, f32[768]{0:T(1024)}, u32[]{:S(2)}) copy-start(f32[768]{0:T(1024)} %get-tuple-element.118) | copy-start | bytes 9220
  233.6 2.1 copy-start.30
  233.7 2.2 copy-start.33
  235.9 4.2 copy-start.14
  235.9 4.2 copy-start.40
  240.1 3.6 copy-start.20
  240.1 3.8 copy-start.11
  240.1 3.8 copy-start.45
  240.1 4.1 copy-start.29
  245.3 4.3 copy-start.15
  249.6 3.6 copy-start.21
  253.4 0.8 copy-start.7
  298.7 3.7 copy-start.8
  302.4 2.0 copy-start.51
  304.4 1.5 copy-start.52
  304.7 5.4 copy-start.17
  305.9 4.3 copy-start.6
  305.9 4.3 copy-start.37
  305.9 4.3 copy-start.47
  310.2 3.6 copy-start.22
  310.2 3.6 copy-start.49
  558.4 8.2 %copy-start.27 = (f32[16,2,2,768]{3,2,1,0:T(2,128)S(1)}, f32[16,2,2,768]{3,2,1,0:T(2,128)}, u32[]{:S(2)}) copy-start(f32[16,2,2,768]{3,2,1,0:T(2,128)} %get-tuple-element.79) | copy-start | bytes 589828
  558.4 13.8 %copy-start.2 = (bf16[1,2,2,576,768]{4,3,2,1,0:T(8,128)(2,1)S(1)}, bf16[1,2,2,576,768]{4,3,2,1,0:T(8,128)(2,1)}, u32[]{:S(2)}) copy-start(bf16[1,2,2,576,768]{4,3,2,1,0:T(8,128)(2,1)} %copy-done.1) | copy-start | bytes 10616836
  572.2 1.8 copy-start.10
  572.2 1.8 copy-start.23
  572.3 3.1 copy-start
  575.4 7.6 %copy-start.24 = (f32[2,9984]{1,0:T(2,128)S(1)}, f32[2,9984]{1,0:T(2,128)}, u32[]{:S(2)}) copy-start(f32[2,9984]{1,0:T(2,128)} %reshape.363) | copy-start | bytes 239620
  575.4 7.6 %copy-start.25 = (f32[2,9612]{1,0:T(2,128)S(1)}, f32[2,9612]{1,0:T(2,128)}, u32[]{:S(2)}) copy-start(f32[2,9612]{1,0:T(2,128)} %param.15) | copy-start | bytes 230692
  575.4 7.6 %copy-start.28 = (f32[2,9612]{1,0:T(2,128)S(1)}, f32[2,9612]{1,0:T(2,128)}, u32[]{:S(2)}) copy-start(f32[2,9612]{1,0:T(2,128)} %param.21) | copy-start | bytes 230692
  (6 other events, 3.9 us)
Sparse Core Ops, SparseCore 0:
  10.9 139.4 all-gather.2

commit v5 on v4

--- a/solution.py
+++ b/solution.py
@@ -17,7 +17,6 @@
 STEP_COUNT = 5
 
 
-PRECISE = lax.Precision.HIGHEST
 ADAM_ONE = 0.9
 ADAM_TWO = 0.95
 ADAM_EPSILON = 1e-08
@@ -31,6 +30,9 @@
 MARKS = 64
 HALF = TAPS // 2
 PAIRS = HEADS // 2
+LINES = 13
+TAP_LINE = 12
+SMALL = 8 * D + FF + HEADS * TAPS
 LANES = 128
 SCALE = HEAD_DIM**-0.5
 NEG = -1e30
@@ -63,7 +65,7 @@
 
 
 def exact(a, b, dims=NN):
-    return lax.dot_general(a, b, dims, precision=PRECISE, preferred_element_type=F32)
+    return mm_both(a, b, dims)
 
 
 def iota(shape, dim):
@@ -95,9 +97,34 @@
     return jnp.broadcast_to(jnp.max(split, axis=1, keepdims=True), split.shape).reshape(rows, cols)
 
 
+def head_taps(lines, pair):
+    row = jnp.broadcast_to(lines[TAP_LINE : TAP_LINE + 1, :], (8, D))
+    rows = []
+    for side in range(2):
+        turned = pltpu.roll(row, lax.rem(D - TAPS * (2 * pair + side), D), 1)[0:1, : 2 * LANES]
+        rows.append(jnp.where(iota((1, 2 * LANES), 1) < TAPS, turned, 0.0))
+    return rows
+
+
 def band(taps_row):
     wide = jnp.broadcast_to(taps_row, (LANES, 2 * LANES))
     return pltpu.roll(wide, 0, 1, stride=1, stride_axis=0)
+
+
+def band_back(taps_row):
+    wide = jnp.broadcast_to(taps_row, (2 * LANES, 2 * LANES))
+    return pltpu.roll(wide, 2 * LANES - 2 * HALF, 1, stride=1, stride_axis=0)[:, :LANES].T
+
+
+def mark_columns(edges):
+    low = jnp.broadcast_to(edges, (LANES, LANES)).T[:MARKS, :1]
+    high = jnp.broadcast_to(pltpu.roll(edges, LANES - 1, 1), (LANES, LANES)).T[:MARKS, :1]
+    return low.astype(jnp.int32), high.astype(jnp.int32)
+
+
+def mark_rows(edges):
+    low, high = edges[:, :MARKS], pltpu.roll(edges, LANES - 1, 1)[:, :MARKS]
+    return low.astype(jnp.int32), high.astype(jnp.int32)
 
 
 def convolve(padded, bands, length, store):
@@ -114,8 +141,9 @@
     lax.fori_loop(0, length // LANES, block, 0)
 
 
-def attend(queries, keys, values, low_marks, high_marks, taps, keep, padded, blended, result):
+def attend(queries, keys, values, edges, taps, keep, padded, blended, result):
     length = queries.shape[0]
+    low_marks, high_marks = mark_columns(edges)
     at = iota((MARKS, length), 1)
     member = ((low_marks <= at) & (at < high_marks)).astype(F32).astype(BF16)
     counts = (high_marks - low_marks).astype(F32)
@@ -164,11 +192,13 @@
     def store(start, block):
         result[pl.ds(start, LANES), :] = (blended[pl.ds(start, LANES), :] + block).astype(BF16)
 
-    convolve(padded, [band(taps[0:1]), band(taps[1:2])], length, store)
-
-
-def attend_back(grads, queries, keys, values, low_marks, high_marks, low_row, high_row, taps, keep, padded, padded_grads, blended, result, grad_taps):
+    convolve(padded, [band(one) for one in taps], length, store)
+
+
+def attend_back(grads, queries, keys, values, edges, taps, keep, padded, padded_grads, blended, result, grad_taps):
     length = grads.shape[0]
+    low_marks, high_marks = mark_columns(edges)
+    low_row, high_row = mark_rows(edges)
     at = iota((length, MARKS), 0)
     member = ((low_row <= at) & (at < high_row)).astype(F32).astype(BF16)
     counts = (high_marks - low_marks).astype(F32)
@@ -227,7 +257,7 @@
         total_rows = blended[pl.ds(start, LANES), :] + jnp.where(rows < last, block, 0.0)
         result[2, pl.ds(start, LANES), :] = total_rows.astype(BF16)
 
-    convolve(padded_grads, [band(taps[2:3]), band(taps[3:4])], length, store)
+    convolve(padded_grads, [band_back(one) for one in taps], length, store)
     first = iota((LANES, LANES), 1) < HEAD_DIM
 
     def block(step, carry):
@@ -374,7 +404,7 @@
     lax.fori_loop(0, TASKS, body, 0)
 
 
-def forward_kernel(count, piece, qkv, low_col, high_col, taps, mixed_rows, slab, *refs):
+def forward_kernel(count, piece, qkv, edges, lines, mixed_rows, slab, *refs):
     keep = dict(zip(KEPT, refs))
     padded, blended, result, send_one, receive_one, send_two, receive_two = refs[len(KEPT) :]
     me = lax.axis_index("dp")
@@ -388,7 +418,7 @@
     def _():
         micro, pair = task // PAIRS, lax.rem(task, PAIRS)
         await_slab(count, piece, slab, receive_one)
-        attend(slab[0], slab[1], slab[2], low_col[micro], high_col[micro], taps[pair], keep, padded, blended, result.at[0])
+        attend(slab[0], slab[1], slab[2], edges[pl.ds(micro, 1), :], head_taps(lines, pair), keep, padded, blended, result.at[0])
         back(False)
 
     out(True)
@@ -399,7 +429,7 @@
         back(True)
 
 
-def backward_kernel(count, piece, grads, low_col, high_col, low_row, high_row, taps, slab, *refs):
+def backward_kernel(count, piece, grads, edges, lines, slab, *refs):
     keep = dict(zip(KEPT, refs))
     out_grads, grad_taps, grad_slab, padded, padded_grads, blended, result, send_one, receive_one, send_two, receive_two = refs[len(KEPT) :]
     me = lax.axis_index("dp")
@@ -415,8 +445,8 @@
         micro, pair = task // PAIRS, lax.rem(task, PAIRS)
         await_slab(count, piece, grad_slab, receive_one)
         attend_back(
-            grad_slab[0], slab[0], slab[1], slab[2], low_col[micro], high_col[micro], low_row[micro], high_row[micro],
-            taps[pair], keep, padded, padded_grads, blended, result, grad_taps.at[pair],
+            grad_slab[0], slab[0], slab[1], slab[2], edges[pl.ds(micro, 1), :], head_taps(lines, pair),
+            keep, padded, padded_grads, blended, result, grad_taps.at[pair],
         )
         back(False)
 
@@ -432,7 +462,7 @@
 DMA = pltpu.SemaphoreType.DMA
 
 
-def attention_forward(count, qkv, marks, taps, ident):
+def attention_forward(count, qkv, edges, lines, ident):
     piece = qkv.shape[2]
     length = piece * count
     shapes = kept_shapes(length)
@@ -443,7 +473,7 @@
             jax.ShapeDtypeStruct((3, length, LANES), BF16),
         ]
         + [jax.ShapeDtypeStruct(shapes[name], F32) for name in KEPT],
-        in_specs=[VMEM] * 4,
+        in_specs=[VMEM] * 3,
         out_specs=[VMEM] * (2 + len(KEPT)),
         scratch_shapes=[
             pltpu.VMEM((length + LANES, LANES), BF16),
@@ -456,11 +486,11 @@
         ],
         compiler_params=pltpu.CompilerParams(collective_id=ident, has_side_effects=True, vmem_limit_bytes=60 << 20),
         name="attend_forward",
-    )(qkv, marks[0], marks[1], taps)
+    )(qkv, edges, lines)
     return results[0][0], results[1:]
 
 
-def attention_backward(count, grads, marks, taps, kept, ident):
+def attention_backward(count, grads, edges, lines, kept, ident):
     piece = grads.shape[2]
     length = piece * count
     return pl.pallas_call(
@@ -469,7 +499,7 @@
             jax.ShapeDtypeStruct((3, MICRO, piece, D), BF16),
             jax.ShapeDtypeStruct((PAIRS, 2, 2 * LANES), F32),
         ],
-        in_specs=[VMEM] * (7 + len(KEPT)),
+        in_specs=[VMEM] * (4 + len(KEPT)),
         out_specs=[VMEM] * 2,
         scratch_shapes=[
             pltpu.VMEM((1, length, LANES), BF16),
@@ -484,10 +514,52 @@
         ],
         compiler_params=pltpu.CompilerParams(collective_id=ident, has_side_effects=True, vmem_limit_bytes=60 << 20),
         name="attend_backward",
-    )(grads, *marks, taps, *kept)
-
-
-def gather_kernel(shard, out, local_sem, z_send, z_got, x_send, x_got, y_send, y_got, core_send, core_got):
+    )(grads, edges, lines, *kept)
+
+
+def arrange(sources, targets):
+    params, first, second = sources
+    lines, ups, sliced = targets[:LAYERS], targets[LAYERS : 2 * LAYERS], targets[2 * LAYERS :]
+    for level in range(LAYERS):
+        own = slice(level, level + 1)
+        for line in range(TAP_LINE):
+            lines[level][line : line + 1, :] = params[own, line * D : (line + 1) * D]
+        lines[level][TAP_LINE:, :] = jnp.zeros((16 - TAP_LINE, D), F32)
+        lines[level][TAP_LINE : TAP_LINE + 1, : HEADS * TAPS] = params[own, TAP_LINE * D :]
+        ups[level][...] = params[own, 8 * D : 8 * D + FF]
+    for source, target in zip((first, second), sliced):
+        target[LAYERS * LINES // 2 :] = jnp.zeros((16 - LAYERS * LINES // 2, 2, D), F32)
+        for level in range(LAYERS):
+            own = slice(level, level + 1)
+            for line in range(LINES):
+                index = level * LINES + line
+                spot = slice(index % 2, index % 2 + 1)
+                if line < TAP_LINE:
+                    target[index // 2, spot, :] = source[own, line * D : (line + 1) * D]
+                else:
+                    target[index // 2, spot, :] = jnp.zeros((1, D), F32)
+                    target[index // 2, spot, : HEADS * TAPS] = source[own, TAP_LINE * D :]
+
+
+ARRANGED = (
+    [jax.ShapeDtypeStruct((16, D), F32)] * LAYERS + [jax.ShapeDtypeStruct((1, FF), F32)] * LAYERS + [jax.ShapeDtypeStruct((16, 2, D), F32)] * 2
+)
+
+
+def arrange_kernel(*refs):
+    arrange(refs[:3], refs[3:])
+
+
+def arranged(*smalls):
+    return pl.pallas_call(arrange_kernel, out_shape=ARRANGED, in_specs=[VMEM] * 3, out_specs=[VMEM] * len(ARRANGED), name="arrange")(*smalls)
+
+
+def gather_kernel(shard, params, first, second, out, *refs):
+    targets, refs = refs[: len(ARRANGED)], refs[len(ARRANGED) :]
+    gather_body(shard, out, lambda: arrange((params, first, second), targets), *refs)
+
+
+def gather_body(shard, out, aside, local_sem, z_send, z_got, x_send, x_got, y_send, y_got, core_send, core_got):
     me = lax.axis_index("dp")
     x = lax.axis_index("rep")
     core, y, z = lax.rem(me, 2), lax.rem(me // 2, 2), me // 4
@@ -553,6 +625,8 @@
     for side in range(2):
         for sub in range(2):
             move("core", z, y, side, sub, shard.at[rows(side, sub), :]).start()
+
+    aside()
 
     def at_distance(distance, act):
         for sign in (1, -1):
@@ -638,13 +712,13 @@
     pltpu.make_async_copy(column, column, core_got).wait()
 
 
-def gather(shard):
+def gather(shard, *smalls):
     block_rows = shard.shape[0]
-    return pl.pallas_call(
+    results = pl.pallas_call(
         gather_kernel,
-        out_shape=jax.ShapeDtypeStruct((4, 2, 2, block_rows, D), BF16),
-        in_specs=[VMEM],
-        out_specs=pl.BlockSpec(memory_space=pl.ANY),
+        out_shape=[jax.ShapeDtypeStruct((4, 2, 2, block_rows, D), BF16)] + ARRANGED,
+        in_specs=[VMEM] * 4,
+        out_specs=[pl.BlockSpec(memory_space=pl.ANY)] + [VMEM] * len(ARRANGED),
         scratch_shapes=[
             DMA,
             DMA((4, 2, 2)),
@@ -658,12 +732,12 @@
         ],
         compiler_params=pltpu.CompilerParams(collective_id=4, has_side_effects=True),
         name="gather",
-    )(shard).reshape(16 * block_rows, D)
-
-
-CHUNK = 48
+    )(shard, *smalls)
+    return results[0].reshape(16 * block_rows, D), results[1:]
+
+
+CHUNK = 32
 RING = 8
-LINES = 13
 MATES = ("low_in", "low_comb", "low_up", "low_act", "low_grads", "low_branch", "low_hidden", "low_down", "gain_one", "shift_one", "gain_two", "shift_two", "taps")
 
 
@@ -733,7 +807,7 @@
         put(level, 2, column_sum(mate["low_branch"][...]))
         put(level, 3, column_sum(mate["low_down"][...]))
         for line, name in enumerate(MATES[8:12]):
-            put(level, 4 + line, mate[name][...])
+            put(level, 4 + line, column_sum(mate[name][...]))
         for part in range(FF // D):
             put(level, 8 + part, column_sum(mate["low_up"][:, part * D : (part + 1) * D]))
         line = jnp.zeros((1, D), F32)
@@ -946,83 +1020,101 @@
     )(*[mate[name] for mate in mates for name in MATES], weights, first, second, small_first, small_second)
 
 
-def sliced(array):
-    wide = jnp.pad(array, ((0, 0), (0, LINES * D - array.shape[1]))).reshape(LAYERS * LINES, D)
-    return jnp.pad(wide, ((0, 32 - LAYERS * LINES), (0, 0))).reshape(16, 2, D)
-
-
-def unsliced(array, shape):
-    return array.reshape(32, D)[: LAYERS * LINES].reshape(LAYERS, LINES * D)[:, : shape[1]]
+def finish_kernel(both, params, outer, first, second, first_new, second_new, outer_new, params_new, grad, mean):
+    for level in range(LAYERS):
+        for line in range(LINES):
+            index = level * LINES + line
+            spot = slice(index % 2, index % 2 + 1)
+            for which, target in ((0, grad), (1, mean)):
+                target[level : level + 1, line * D : (line + 1) * D] = both[index // 2, which, spot, :]
+    first_new[...], second_new[...] = moments(first[...], second[...], grad[:, :SMALL])
+    momentum = MOMENTUM * outer[...] + mean[:, :SMALL]
+    outer_new[...] = momentum
+    params_new[...] = params[...] - LR_OUTER * (mean[:, :SMALL] + MOMENTUM * momentum)
+
+
+def finish(both, params, outer, first, second):
+    wide = pltpu.VMEM((LAYERS, LINES * D), F32)
+    return pl.pallas_call(
+        finish_kernel,
+        out_shape=[jax.ShapeDtypeStruct(params.shape, F32)] * 4,
+        in_specs=[VMEM] * 5,
+        out_specs=[VMEM] * 4,
+        scratch_shapes=[wide, wide],
+        name="finish",
+    )(both, params, outer, first, second)
 
 
 def dense(a, b, dims=NN):
     return mm(a, b, dims)
 
 
-def layer_norm(values, gain_vec, shift_vec):
-    row_mean = jnp.mean(values, axis=-1, keepdims=True)
-    centred = values - row_mean
-    variance = jnp.mean(centred * centred, axis=-1, keepdims=True)
-    return centred * lax.rsqrt(variance + 1e-05) * gain_vec + shift_vec
-
-
-def unpack(params):
-    blocks = [params[index * D : (index + 1) * D] for index in range(8)]
-    bias_up = params[8 * D : 8 * D + FF]
-    conv_taps = params[8 * D + FF :].reshape(HEADS, TAPS)
-    return (blocks, bias_up, conv_taps)
-
-
-def pair_taps(conv_taps):
-    both = jnp.stack([conv_taps.reshape(PAIRS, 2, TAPS), conv_taps[:, ::-1].reshape(PAIRS, 2, TAPS)], axis=1)
-    both = both.reshape(PAIRS, 4, TAPS)
-    return jnp.pad(both, ((0, 0), (0, 0), (0, 2 * LANES - TAPS)))
+def standard(values):
+    centred = values - jnp.mean(values, axis=-1, keepdims=True)
+    scale = lax.rsqrt(jnp.mean(centred * centred, axis=-1, keepdims=True) + 1e-05)
+    return centred * scale, scale
+
+
+def layer_norm(values, gain, shift):
+    return standard(values)[0] * gain + shift
+
+
+def layer_norm_back(values, gain, grad):
+    unit_values, scale = standard(values)
+    inner = grad * gain
+    along = jnp.mean(inner * unit_values, axis=-1, keepdims=True)
+    result = scale * (inner - jnp.mean(inner, axis=-1, keepdims=True) - unit_values * along)
+    return result, eighths(grad * unit_values), eighths(grad)
+
+
+def eighths(rows):
+    return jnp.sum(rows.reshape(-1, 8, D), axis=0)
 
 
 def split_rows(rows):
     return rows[: 3 * D].reshape(3, D, D), rows[3 * D : 4 * D], rows[4 * D : 4 * D + FF], rows[4 * D + FF :]
 
 
-def forward_layer(count, inputs, rows, params, marks, ident):
+def forward_layer(count, inputs, rows, small, edges, ident):
     piece = inputs.shape[0] // MICRO
-    blocks, bias_up, conv_taps = unpack(params)
+    lines, bias_up = small
     proj, out_weight, up_weight, down_weight = split_rows(rows)
     low_in = inputs.astype(BF16)
-    bias = jnp.stack([blocks[0], jnp.zeros_like(blocks[0]), blocks[1]])
-    qkv = jnp.stack([(dense(low_in, proj[part]) + bias[part]).astype(BF16) for part in range(3)])
-    low_comb, kept = attention_forward(count, qkv.reshape(3, MICRO, piece, D), marks, pair_taps(conv_taps), ident)
+    query = (dense(low_in, proj[0]) + lines[0:1]).astype(BF16)
+    key = dense(low_in, proj[1]).astype(BF16)
+    value = (dense(low_in, proj[2]) + lines[1:2]).astype(BF16)
+    qkv = jnp.stack([query, key, value])
+    low_comb, kept = attention_forward(count, qkv.reshape(3, MICRO, piece, D), edges, lines, ident)
     low_comb = low_comb.reshape(MICRO * piece, D)
-    resid_one = inputs + (dense(low_comb, out_weight) + blocks[2])
-    hidden_one = layer_norm(resid_one, blocks[4], blocks[5])
+    resid_one = inputs + (dense(low_comb, out_weight) + lines[2:3])
+    hidden_one = layer_norm(resid_one, lines[4:5], lines[5:6])
     low_hidden = hidden_one.astype(BF16)
     upward = dense(low_hidden, up_weight, NT) + bias_up
     low_act = jax.nn.gelu(upward).astype(BF16)
-    resid_two = hidden_one + (dense(low_act, down_weight) + blocks[3])
-    output = layer_norm(resid_two, blocks[6], blocks[7])
+    resid_two = hidden_one + (dense(low_act, down_weight) + lines[3:4])
+    output = layer_norm(resid_two, lines[6:7], lines[7:8])
     return output, (low_in, kept, low_comb, resid_one, low_hidden, upward, low_act, resid_two)
 
 
-def backward_layer(count, grad_output, rows, params, marks, state, ident):
+def backward_layer(count, grad_output, rows, small, edges, state, ident):
     low_in, kept, low_comb, resid_one, low_hidden, upward, low_act, resid_two = state
     total = low_in.shape[0]
     piece = total // MICRO
-    blocks, bias_up, conv_taps = unpack(params)
+    lines, _ = small
     proj, out_weight, up_weight, down_weight = split_rows(rows)
-    _, pull_two = jax.vjp(layer_norm, resid_two, blocks[6], blocks[7])
-    grad_two, grad_gain_two, grad_shift_two = pull_two(grad_output)
+    grad_two, grad_gain_two, grad_shift_two = layer_norm_back(resid_two, lines[6:7], grad_output)
     low_down = grad_two.astype(BF16)
     grad_act = dense(low_down, down_weight, NT)
     _, pull_gelu = jax.vjp(jax.nn.gelu, upward)
     low_up = pull_gelu(grad_act)[0].astype(BF16)
     grad_hidden = grad_two + dense(low_up, up_weight)
-    _, pull_one = jax.vjp(layer_norm, resid_one, blocks[4], blocks[5])
-    grad_one, grad_gain_one, grad_shift_one = pull_one(grad_hidden)
+    grad_one, grad_gain_one, grad_shift_one = layer_norm_back(resid_one, lines[4:5], grad_hidden)
     low_branch = grad_one.astype(BF16)
     grad_comb = dense(low_branch, out_weight, NT).astype(BF16)
-    low_grads, grad_taps = attention_backward(count, grad_comb.reshape(1, MICRO, piece, D), marks, pair_taps(conv_taps), kept, ident)
+    low_grads, grad_taps = attention_backward(count, grad_comb.reshape(1, MICRO, piece, D), edges, lines, kept, ident)
     low_grads = low_grads.reshape(3, total, D)
     grad_in = grad_one + sum(dense(low_grads[part], proj[part], NT) for part in range(3))
-    vectors = [vector.reshape(1, D) for vector in (grad_gain_one, grad_shift_one, grad_gain_two, grad_shift_two)]
+    vectors = (grad_gain_one, grad_shift_one, grad_gain_two, grad_shift_two)
     values = (low_in, low_comb, low_up, low_act, low_grads, low_branch, low_hidden, low_down, *vectors, grad_taps)
     return grad_in, dict(zip(MATES, values))
 
@@ -1032,7 +1124,7 @@
     parts = parts + [dense(mate[left], mate[right], TN) for left, right in (("low_comb", "low_branch"), ("low_up", "low_hidden"), ("low_act", "low_down"))]
     sums = [mate["low_grads"][0], mate["low_grads"][2], mate["low_branch"], mate["low_down"]]
     sums = [jnp.sum(one.astype(F32), axis=0) for one in sums]
-    sums = sums + [mate[name].reshape(-1) for name in MATES[8:12]]
+    sums = sums + [jnp.sum(mate[name], axis=0) for name in MATES[8:12]]
     sums = sums + [jnp.sum(mate["low_up"].astype(F32), axis=0), mate["taps"][:, :, :TAPS].reshape(-1)]
     return jnp.concatenate(parts, axis=0).astype(BF16), jnp.concatenate(sums)
 
@@ -1068,24 +1160,26 @@
     low_weights = weights.astype(BF16)
     held = [lax.all_gather(low_weights[level], "dp", axis=0, tiled=True) for level in range(LAYERS)]
     if count == 16:
-        held[0] = gather(low_weights[0])
-    edges = bounds[0, :, 0, :]
-    low_edges, high_edges = edges[:, :-1], edges[:, 1:]
-    marks = (low_edges[:, :, None], high_edges[:, :, None], low_edges[:, None, :], high_edges[:, None, :])
+        held[0], prepared = gather(low_weights[0], small_params, first_small[0], second_small[0])
+    else:
+        prepared = arranged(small_params, first_small[0], second_small[0])
+    smalls = [(prepared[level], prepared[LAYERS + level]) for level in range(LAYERS)]
+    limits = bounds[0, :, 0, :]
+    edges = jnp.pad(limits.astype(F32), ((0, 0), (0, LANES - limits.shape[1])))
     positions = lax.axis_index("dp") * piece + jnp.arange(piece, dtype=jnp.int32)
-    valid = (positions[None, :] < edges[:, -1:]).astype(F32).reshape(total, 1)
+    valid = (positions[None, :] < limits[:, -1:]).astype(F32).reshape(total, 1)
     activation = hidden[0, :, 0].reshape(total, D).astype(F32)
     states = []
     for level in range(LAYERS):
-        activation, state = forward_layer(count, activation, held[level], small_params[level], marks, 1)
+        activation, state = forward_layer(count, activation, held[level], smalls[level], edges, 1)
         states.append(state)
     gradient = cotangent[0, :, 0].reshape(total, D).astype(F32) * valid
     mates = [None] * LAYERS
     for level in reversed(range(LAYERS)):
-        gradient, mates[level] = backward_layer(count, gradient, held[level], small_params[level], marks, states[level], 2)
+        gradient, mates[level] = backward_layer(count, gradient, held[level], smalls[level], edges, states[level], 2)
     if count == 16:
-        grad_big, mean_big, small_both = settle(mates, weights, first_big[0], second_big[0], sliced(first_small[0]), sliced(second_small[0]))
-        grad_small, mean_small = [unsliced(small_both[:, which], small_params.shape) for which in range(2)]
+        grad_big, mean_big, small_both = settle(mates, weights, first_big[0], second_big[0], *prepared[2 * LAYERS :])
+        new_smalls = finish(small_both, small_params, outer_small, first_small[0], second_small[0])
     else:
         rows, sums = zip(*[plain_grads(mate) for mate in mates])
         grad_big = jnp.stack([lax.psum_scatter(one, "dp", scatter_dimension=0, tiled=True).astype(F32) for one in rows])
@@ -1095,12 +1189,12 @@
         delta_small = adam(small_params, first_small[0], second_small[0], grad_small, LR_SMALL, 0.0)[2]
         mean_big = lax.psum(delta_big.astype(BF16), "rep").astype(F32) / reps
         mean_small = lax.psum(delta_small.astype(BF16), "rep").astype(F32) / reps
+        momentum = MOMENTUM * outer_small + mean_small
+        new_smalls = (*moments(first_small[0], second_small[0], grad_small), momentum, small_params - LR_OUTER * (mean_small + MOMENTUM * momentum))
     new_first, new_second = moments(first_big[0], second_big[0], grad_big)
-    new_first_small, new_second_small = moments(first_small[0], second_small[0], grad_small)
+    new_first_small, new_second_small, outer_small_new, small_new = new_smalls
     outer_big_new = MOMENTUM * outer_big + mean_big
-    outer_small_new = MOMENTUM * outer_small + mean_small
     weights_new = weights - LR_OUTER * (mean_big + MOMENTUM * outer_big_new)
-    small_new = small_params - LR_OUTER * (mean_small + MOMENTUM * outer_small_new)
     shape = (1, MICRO, 1, piece, D)
     return (
         activation.reshape(shape),

time: 599 us -> 566 us (0.945)
  local copies, waits for them, and re-layouts: 47.7 us -> 17.4 us
    reshape x16 -> x0, local copies, waits for them, and re-layouts: 15.1 us -> none  [the longest x8 4.69 us: layer_norm(): return centred * lax.rsqrt(variance + 1e-05) * gain_vec + shift_vec]
    pallas_call x2, Pallas kernels: 85.5 us -> 78.2 us  [attention_backward(): pl.pallas_call(functools.partial(backward_kernel, count, piece), out_shap...]
    pad x6 -> x1, local copies, waits for them, and re-layouts: 7.4 us -> 1.23 us  [shards(): edges = jnp.pad(limits.astype(F32), ((0, 0), (0, LANES - limits.shape[1])))]
    pallas_call x1 -> x2, Pallas kernels: 98 us -> 101 us  [the longest x1 98.8 us: gather(): pl.pallas_call(gather_kernel, out_shape=[jax.ShapeDtypeStruct((4, 2, 2, b...]
  transfers between devices with their start and end apart: 1 -> 1, of which waited for: 0 -> 0; matrix products, arithmetic and copies ran while one was open for 8% -> 5% of each run, Pallas kernels for 23% -> 25%
where the time goes in v5:
time: 566 us; the launch traced here: 557 us
  Pallas kernels  439 us (78%)
  matrix products  57.2 us (10%)
  other arithmetic  27.6 us (5%)
  local copies, waits for them, and re-layouts  17.4 us (3%)
  between operations  15.3 us (3%)
    pallas_call x1, Pallas kernels, settle(): pl.pallas_call(functools.partial(settle_kernel, block_rows), out_shape=[j...  186 us
    pallas_call x1, Pallas kernels, gather(): pl.pallas_call(gather_kernel, out_shape=[jax.ShapeDtypeStruct((4, 2, 2, b...  98.8 us
    pallas_call x2, Pallas kernels, attention_backward(): pl.pallas_call(functools.partial(backward_kernel, count, piece), out_shap...  78.2 us
    pallas_call x2, Pallas kernels, attention_forward(): pl.pallas_call(functools.partial(forward_kernel, count, piece), out_shape...  74.4 us
    dot_general x24, matrix products, mm(): return lax.dot_general(a, b, dims, preferred_element_type=F32)  57.2 us
  transfers between devices with their start and end apart: 1, of which 0 were waited for; matrix products, arithmetic and copies ran while one was open for 5% of the time, Pallas kernels for 25%

profile of v5, /device:TPU:0, one launch (start us, length us, event | category | flops | bytes accessed | tf_op | source)
XLA Modules:
  0.0 556.7 jit_solution(189751492843281950)
XLA Ops:
  7.2 2.2 convert_element_type.116
  9.4 1.3 fusion.67
  10.7 98.8 %gather.1 = (bf16[4,2,2,576,768]{4,3,2,1,0:T(8,128)(2,1)}, f32[16,768]{1,0:T(8,128)}, f32[16,768]{1,0:T(8,128)}, f32[1,3072]{1,0:T(1,128)}, f32[1,3072]{1,0:T(1,...) custom-call(bf16[576,768]{1,0:T(8,128)(2,1)} %get-tuple-element.167.shard, f32[2,9612]{1,0:T(2,128)} %params.3, ...), custom_call_target="tpu_custom_call" | custom-call | tf_op jit(solution)/shard_map/gather/pallas_call | solution.py:717
  109.6 2.4 slice.147
  112.8 0.9 copy-done.44
  114.4 2.3 slice_reduce_fusion.1
  117.2 1.1 multiply_reduce_fusion.5
  121.0 1.3 compare_convert_fusion
  122.3 0.7 copy.25
  123.0 1.2 pad.4.edges
  124.3 1.3 convolution_convert_fusion
  126.3 0.9 pad_maximum_fusion.qkv
  127.1 41.1 %attend_forward.2 = (bf16[1,2,64,768]{3,2,1,0:T(8,128)(2,1)}, bf16[3,1024,128]{2,1,0:T(8,128)(2,1)}, f32[128,128]{1,0:T(8,128)}, f32[128,128]{1,0:T(8,128)}, f32...) custom-call(bf16[3,2,64,768]{3,2,1,0:T(8,128)(2,1)} %pad_maximum_fus, ...), custom_call_target="tpu_custom_call" | custom-call | tf_op jit(solution)/shard_map/attend_forward/pallas_call | solution.py:469
  168.9 1.8 fusion.70
  171.2 5.3 multiply_convert_fusion.1
  176.5 3.5 fusion.71
  180.4 1.6 convolution_convert_fusion.3
  182.1 1.6 fusion.50
  183.7 1.6 fusion.51
  185.3 0.9 pad_maximum_fusion.1.qkv
  186.2 33.4 %attend_forward.3 = (bf16[1,2,64,768]{3,2,1,0:T(8,128)(2,1)}, bf16[3,1024,128]{2,1,0:T(8,128)(2,1)}, f32[128,128]{1,0:T(8,128)}, f32[128,128]{1,0:T(8,128)}, f32...) custom-call(bf16[3,2,64,768]{3,2,1,0:T(8,128)(2,1)} %pad_maximum_fus, ...), custom_call_target="tpu_custom_call" | custom-call | tf_op jit(solution)/shard_map/attend_forward/pallas_call | solution.py:469
  219.6 1.8 fusion.72
  221.8 4.1 multiply_convert_fusion
  226.0 3.5 fusion.73
  229.9 0.7 bitcast_reduce_fusion.refs_23_
  230.9 1.0 fusion.66
  231.8 4.3 fusion.31.refs_15_
  236.1 3.5 multiply_reduce_fusion.12
  240.6 2.6 convolution_convert_fusion.2
  243.1 36.7 %attend_backward.2 = (bf16[3,2,64,768]{3,2,1,0:T(8,128)(2,1)}, f32[6,2,256]{2,1,0:T(2,128)}) custom-call(bf16[1,2,64,768]{3,2,1,0:T(8,128)(2,1)} %bitcast.198, f32[2,128]{1,0:T(2,128)} %pad.4.edges, f32[16,768]{1,0:T(8,128)} %get-tuple-element.61.lines, bf16[3,1024,128]{2,1,0:T(8,128)(2,1)} %get-tuple-element.64.slab, f32[128,128]{1,0:T(8,128)} %get-tuple-element.65.refs_0_, ...), custom_call_target="tpu_custom_call" | custom-call | tf_op jit(solution)/shard_map/attend_backward/pallas_call | solution.py:496
  279.9 1.2 fusion.69
  281.0 1.8 fusion.55
  282.9 1.8 convolution_add_fusion.5
  284.7 1.9 multiply_reduce_fusion.11
  288.0 4.2 fusion.24.refs_2_
  292.2 3.5 multiply_reduce_fusion.10
  296.5 0.9 fusion.63
  297.4 2.5 convolution_convert_fusion.1
  300.0 41.5 %attend_backward.3 = (bf16[3,2,64,768]{3,2,1,0:T(8,128)(2,1)}, f32[6,2,256]{2,1,0:T(2,128)}) custom-call(bf16[1,2,64,768]{3,2,1,0:T(8,128)(2,1)} %bitcast.197, f32[2,128]{1,0:T(2,128)} %pad.4.edges, f32[16,768]{1,0:T(8,128)} %get-tuple-element.58.lines, bf16[3,1024,128]{2,1,0:T(8,128)(2,1)} %get-tuple-element.78.slab, f32[128,128]{1,0:T(8,128)} %get-tuple-element.79.refs_0_, ...), custom_call_target="tpu_custom_call" | custom-call | tf_op jit(solution)/shard_map/attend_backward/pallas_call | solution.py:496
  341.5 1.9 fusion.68
  343.5 185.7 %settle.1 = (f32[2,576,768]{2,1,0:T(8,128)}, f32[2,576,768]{2,1,0:T(8,128)}, f32[16,2,2,768]{3,2,1,0:T(2,128)}) custom-call(bf16[128,768]{1,0:T(8,128)(2,1)} %bitcast.189, bf16[128,768]{1,0:T(8,128)(2,1)} %bitcast.194, bf16[128,3072]{1,0:T(8,128)(2,1)} %copy-done.18, bf16[128,3072]{1,0:T(8,128)(2,1)} %copy-done.15, bf16[3,128,768]{2,1,0:T(8,128)(2,1)} %bitcast.169, ...), custom_call_target="tpu_custom_call" | custom-call | tf_op jit(solution)/shard_map/settle/pallas_call | solution.py:978
  529.2 8.8 %fusion.17 = (f32[1,2,576,768]{3,2,1,0:T(8,128)}, f32[1,2,576,768]{3,2,1,0:T(8,128)}) fusion(f32[2,576,768]{2,1,0:T(8,128)} %get-tuple-element.96, f32[1,2,576,768]{3,2,1,0:T(8,128)} %param.17, f32[1,2,576,768]{3,2,1,0:T(8,128)} %param.16), kind=kLoop, calls=%fused_computation.18 | loop fusion | flops 6193152 | bytes 17694720 | tf_op jit(solution)/shard_map/broadcast_in_dim | solution.py:1203
  538.1 1.3 fusion.54
  539.4 0.7 copy-done.6
  540.1 4.4 fusion.62
  544.6 1.8 finish.1
  546.4 1.7 convolution_add_fusion.3
  548.1 1.3 fusion.37
  (140 shorter events, 10.8 us)
Async XLA Ops:
  7.2 173.3 %all-gather.3.cloned.1.call-start = ((), (), s32[]{:S(2)}) async-start(), calls=%async_computation | async-start | bytes 15040512 | tf_op jit(solution)/shard_map/all_gather | solution.py:1161
  109.6 2.4 copy-start.42
  112.0 13.9 %copy-start.1 = (bf16[1,2,2,576,768]{4,3,2,1,0:T(8,128)(2,1)}, bf16[1,2,2,576,768]{4,3,2,1,0:T(8,128)(2,1)S(1)}, u32[]{:S(2)}) copy-start(bf16[1,2,2,576,768]{4,3,2,1,0:T(8,128)(2,1)S(1)} %slice.147) | copy-start | bytes 10616836
  112.8 0.9 copy-start.44
  116.6 54.3 %copy-start.25 = (f32[768]{0:T(1024)}, f32[768]{0:T(1024)S(1)}, u32[]{:S(2)}) copy-start(f32[768]{0:T(1024)S(1)} %get-tuple-element.193) | copy-start | bytes 9220
  116.6 54.4 %copy-start.31 = (f32[768]{0:T(1024)}, f32[768]{0:T(1024)S(1)}, u32[]{:S(2)}) copy-start(f32[768]{0:T(1024)S(1)} %get-tuple-element.194) | copy-start | bytes 9220
  123.0 2.5 copy-start.21
  123.0 2.5 copy-start.41
  124.3 1.6 copy-start.40
  125.9 42.3 %copy-start.3 = (bf16[1,2,1,64,768]{4,3,2,1,0:T(8,128)(2,1)S(1)}, bf16[1,2,1,64,768]{4,3,2,1,0:T(8,128)(2,1)}, u32[]{:S(2)}) copy-start(bf16[1,2,1,64,768]{4,3,2,1,0:T(8,128)(2,1)} %param.13) | copy-start | bytes 589828
  125.9 43.0 %copy-start.39 = (f32[768]{0:T(1024)S(1)}, f32[768]{0:T(1024)}, u32[]{:S(2)}) copy-start(f32[768]{0:T(1024)} %get-tuple-element.192) | copy-start | bytes 9220
  168.9 2.2 copy-start.46
  171.1 5.3 copy-start.8
  171.2 5.3 copy-start.26
  171.2 5.3 copy-start.32
  171.2 5.3 copy-start.38
  176.5 3.5 copy-start.15
  176.5 3.7 copy-start.22
  176.5 3.7 copy-start.30
  180.0 2.1 copy-start.37
  180.4 3.3 copy-start.9
  180.4 3.3 copy-start.36
  183.7 35.9 %copy-start.35 = (f32[768]{0:T(1024)S(1)}, f32[768]{0:T(1024)}, u32[]{:S(2)}) copy-start(f32[768]{0:T(1024)} %get-tuple-element.142) | copy-start | bytes 9220
  186.2 35.4 %copy-start.27 = (f32[768]{0:T(1024)S(1)}, f32[768]{0:T(1024)}, u32[]{:S(2)}) copy-start(f32[768]{0:T(1024)} %get-tuple-element.141) | copy-start | bytes 9220
  186.2 35.4 %copy-start.29 = (f32[768]{0:T(1024)S(1)}, f32[768]{0:T(1024)}, u32[]{:S(2)}) copy-start(f32[768]{0:T(1024)} %get-tuple-element.140) | copy-start | bytes 9220
  219.6 2.2 copy-start.45
  221.8 4.2 copy-start.10
  221.8 4.2 copy-start.34
  226.0 3.6 copy-start.16
  226.0 3.8 copy-start.4
  226.0 3.8 copy-start.33
  226.0 4.6 copy-start.24
  229.6 1.2 copy-start.28
  229.6 1.2 copy-start.43
  231.8 4.3 copy-start.11
  236.1 3.5 copy-start.17
  240.6 39.3 %copy-start.12 = (bf16[128,768]{1,0:T(8,128)(2,1)}, bf16[128,768]{1,0:T(8,128)(2,1)S(1)}, u32[]{:S(2)}) copy-start(bf16[128,768]{1,0:T(8,128)(2,1)S(1)} %get-tuple-element.160.refs_18_) | copy-start | bytes 589828
  286.6 1.4 copy-start.47
  287.5 4.7 copy-start.13
  292.2 3.5 copy-start.18
  297.4 44.1 %copy-start.14 = (bf16[128,768]{1,0:T(8,128)(2,1)}, bf16[128,768]{1,0:T(8,128)(2,1)S(1)}, u32[]{:S(2)}) copy-start(bf16[128,768]{1,0:T(8,128)(2,1)S(1)} %get-tuple-element.156.refs_5_) | copy-start | bytes 589828
  529.2 8.9 %copy-start.2 = (bf16[1,2,2,576,768]{4,3,2,1,0:T(8,128)(2,1)S(1)}, bf16[1,2,2,576,768]{4,3,2,1,0:T(8,128)(2,1)}, u32[]{:S(2)}) copy-start(bf16[1,2,2,576,768]{4,3,2,1,0:T(8,128)(2,1)} %copy-done.1) | copy-start | bytes 10616836
  529.2 8.9 %copy-start.20 = (bf16[1,2,64,768]{3,2,1,0:T(8,128)(2,1)S(1)}, bf16[1,2,64,768]{3,2,1,0:T(8,128)(2,1)}, u32[]{:S(2)}) copy-start(bf16[1,2,64,768]{3,2,1,0:T(8,128)(2,1)} %get-tuple-element.170) | copy-start | bytes 589828
  529.2 10.2 %copy-start = (f32[2,576,768]{2,1,0:T(8,128)S(1)}, f32[2,576,768]{2,1,0:T(8,128)}, u32[]{:S(2)}) copy-start(f32[2,576,768]{2,1,0:T(8,128)} %refs_26_.1) | copy-start | bytes 10616836
  529.2 10.2 %copy-start.5 = (f32[2,576,768]{2,1,0:T(8,128)S(1)}, f32[2,576,768]{2,1,0:T(8,128)}, u32[]{:S(2)}) copy-start(f32[2,576,768]{2,1,0:T(8,128)} %param.20) | copy-start | bytes 10616836
  529.2 10.9 %copy-start.6 = (f32[2,576,768]{2,1,0:T(8,128)S(1)}, f32[2,576,768]{2,1,0:T(8,128)}, u32[]{:S(2)}) copy-start(f32[2,576,768]{2,1,0:T(8,128)} %get-tuple-element.100) | copy-start | bytes 10616836
  546.4 1.7 copy-start.7
  546.4 1.7 copy-start.19
  (1 other events, 0.6 us)
Sparse Core Ops, SparseCore 0:
  10.9 150.7 all-gather.2

commit v6 on v5

--- a/solution.py
+++ b/solution.py
@@ -141,58 +141,69 @@
     lax.fori_loop(0, length // LANES, block, 0)
 
 
-def attend(queries, keys, values, edges, taps, keep, padded, blended, result):
-    length = queries.shape[0]
-    low_marks, high_marks = mark_columns(edges)
-    at = iota((MARKS, length), 1)
-    member = ((low_marks <= at) & (at < high_marks)).astype(F32).astype(BF16)
-    counts = (high_marks - low_marks).astype(F32)
-    blocks, eye = diagonal_blocks(), unit()
-    q_marks = per_head(mm(member, queries) / counts)
-    k_marks = per_head(mm(member, keys) / counts)
-    scores = jnp.where(blocks, SCALE * exact(q_marks, k_marks, NT), NEG)
-    weights = jnp.exp(scores - jnp.max(scores, axis=1, keepdims=True))
-    kernel = weights / jnp.sum(weights, axis=1, keepdims=True)
-    total = head_sums(jnp.broadcast_to(jnp.sum(kernel * kernel, axis=1, keepdims=True), kernel.shape))
-    inverse = kernel.T / total
-    keep["q_marks"][...] = q_marks
-    keep["k_marks"][...] = k_marks
-    keep["kernel"][...] = kernel
-    keep["total"][...] = total
-    for sweep in range(NS_ITERS):
-        product = exact(kernel, inverse)
-        one = 7.0 * eye - product
-        two = 15.0 * eye - exact(product, one)
-        three = 13.0 * eye - exact(product, two)
-        keep["inverse"][sweep] = inverse
-        keep["product"][sweep] = product
-        keep["two"][sweep] = two
-        keep["three"][sweep] = three
-        inverse = 0.25 * exact(inverse, three)
-    keep["inverse"][NS_ITERS] = inverse
-    valid = at[:1] < high_marks[MARKS - 1 :]
-    key_scores = jnp.where(valid, SCALE * mm_left(q_marks, keys, NT), NEG)
-    key_exp = jnp.where(valid, jnp.exp(key_scores - jnp.max(key_scores, axis=1, keepdims=True)), 0.0)
-    key_weights = key_exp / jnp.sum(key_exp, axis=1, keepdims=True)
-    keep["key_weights"][...] = key_weights
-    summary = jnp.where(blocks, mm_left(key_weights, values), 0.0)
-    mixed = exact(inverse, summary)
-    keep["summary"][...] = summary
-    keep["mixed"][...] = mixed
-    token_scores = SCALE * mm_left(k_marks, queries, NT)
-    token_exp = jnp.exp(token_scores - head_tops(token_scores))
-    token_weights = token_exp / head_sums(token_exp)
-    keep["token_weights"][...] = token_weights
-    blended[...] = mm_both(token_weights, mixed, TN)
-    valid_column = iota((length, 1), 0) < high_marks[MARKS - 1 :]
-    padded[0:HALF, :] = jnp.zeros((HALF, LANES), BF16)
-    padded[HALF : HALF + length, :] = jnp.where(valid_column, values, jnp.zeros_like(values))
-    padded[HALF + length :, :] = jnp.zeros((LANES - HALF, LANES), BF16)
-
-    def store(start, block):
-        result[pl.ds(start, LANES), :] = (blended[pl.ds(start, LANES), :] + block).astype(BF16)
-
-    convolve(padded, [band(one) for one in taps], length, store)
+def attend(slab, edges, taps, keep, padded, blended, result):
+    length = slab.shape[1]
+
+    def begin():
+        low_marks, high_marks = mark_columns(edges())
+        at = iota((MARKS, length), 1)
+        member = ((low_marks <= at) & (at < high_marks)).astype(F32).astype(BF16)
+        counts = (high_marks - low_marks).astype(F32)
+        q_marks = per_head(mm(member, slab[0]) / counts)
+        k_marks = per_head(mm(member, slab[1]) / counts)
+        scores = jnp.where(diagonal_blocks(), SCALE * exact(q_marks, k_marks, NT), NEG)
+        weights = jnp.exp(scores - jnp.max(scores, axis=1, keepdims=True))
+        kernel = weights / jnp.sum(weights, axis=1, keepdims=True)
+        total = head_sums(jnp.broadcast_to(jnp.sum(kernel * kernel, axis=1, keepdims=True), kernel.shape))
+        keep["q_marks"][...] = q_marks
+        keep["k_marks"][...] = k_marks
+        keep["kernel"][...] = kernel
+        keep["total"][...] = total
+        keep["inverse"][0] = kernel.T / total
+
+    def sweep(at):
+        def run():
+            eye, inverse = unit(), keep["inverse"][at]
+            product = exact(keep["kernel"][...], inverse)
+            one = 7.0 * eye - product
+            two = 15.0 * eye - exact(product, one)
+            three = 13.0 * eye - exact(product, two)
+            keep["product"][at] = product
+            keep["two"][at] = two
+            keep["three"][at] = three
+            keep["inverse"][at + 1] = 0.25 * exact(inverse, three)
+
+        return run
+
+    def over_keys():
+        valid = iota((1, length), 1) < mark_columns(edges())[1][MARKS - 1 :]
+        key_scores = jnp.where(valid, SCALE * mm_left(keep["q_marks"][...], slab[1], NT), NEG)
+        key_exp = jnp.where(valid, jnp.exp(key_scores - jnp.max(key_scores, axis=1, keepdims=True)), 0.0)
+        key_weights = key_exp / jnp.sum(key_exp, axis=1, keepdims=True)
+        keep["key_weights"][...] = key_weights
+        keep["summary"][...] = jnp.where(diagonal_blocks(), mm_left(key_weights, slab[2]), 0.0)
+
+    def over_tokens():
+        token_scores = SCALE * mm_left(keep["k_marks"][...], slab[0], NT)
+        token_exp = jnp.exp(token_scores - head_tops(token_scores))
+        keep["token_weights"][...] = token_exp / head_sums(token_exp)
+
+    def close():
+        mixed = exact(keep["inverse"][NS_ITERS], keep["summary"][...])
+        keep["mixed"][...] = mixed
+        blended[...] = mm_both(keep["token_weights"][...], mixed, TN)
+        values = slab[2]
+        valid_column = iota((length, 1), 0) < mark_columns(edges())[1][MARKS - 1 :]
+        padded[0:HALF, :] = jnp.zeros((HALF, LANES), BF16)
+        padded[HALF : HALF + length, :] = jnp.where(valid_column, values, jnp.zeros_like(values))
+        padded[HALF + length :, :] = jnp.zeros((LANES - HALF, LANES), BF16)
+
+        def store(start, block):
+            result[pl.ds(start, LANES), :] = (blended[pl.ds(start, LANES), :] + block).astype(BF16)
+
+        convolve(padded, [band(one) for one in taps()], length, store)
+
+    return [begin] + [sweep(at) for at in range(NS_ITERS)] + [over_keys, over_tokens, close]
 
 
 def attend_back(grads, queries, keys, values, edges, taps, keep, padded, padded_grads, blended, result, grad_taps):
@@ -307,16 +318,18 @@
     return task, owner_of(task, count) == me
 
 
-def greet(count):
+def greet(count, across=False):
     me = lax.axis_index("dp")
     barrier = pltpu.get_barrier_semaphore()
+    if across:
+        pl.semaphore_signal(barrier, inc=1, device_id={"rep": 1 - lax.axis_index("rep")}, device_id_type=MESH)
 
     def signal(step, carry):
         pl.semaphore_signal(barrier, inc=1, device_id={"dp": lax.rem(me + step, count)}, device_id_type=MESH)
         return carry
 
     lax.fori_loop(1, count, signal, 0)
-    pl.semaphore_wait(barrier, count - 1)
+    pl.semaphore_wait(barrier, count if across else count - 1)
 
 
 def scatter_tasks(count, piece, source, slab, send, receive):
@@ -404,23 +417,41 @@
     lax.fori_loop(0, TASKS, body, 0)
 
 
-def forward_kernel(count, piece, qkv, edges, lines, mixed_rows, slab, *refs):
+def forward_kernel(count, piece, spans, qkv, edges, lines, low, mixed_rows, slab, *refs):
     keep = dict(zip(KEPT, refs))
-    padded, blended, result, send_one, receive_one, send_two, receive_two = refs[len(KEPT) :]
+    outs, refs = refs[len(KEPT) : len(KEPT) + len(spans)], refs[len(KEPT) + len(spans) :]
+    padded, blended, result, send_one, receive_one, send_two, receive_two = refs[:7]
+    begin, steps, finish = spread_all(spans, low, outs, refs[7:])
     me = lax.axis_index("dp")
     task, owns = task_of(me, count)
-    greet(count)
+    micro, pair = task // PAIRS, lax.rem(task, PAIRS)
+    greet(count, bool(spans))
     out = scatter_tasks(count, piece, qkv, slab, send_one, receive_one)
     out(False)
+    begin()
     back = return_rows(count, piece, result, mixed_rows, send_two, receive_two)
-
-    @pl.when(owns)
-    def _():
-        micro, pair = task // PAIRS, lax.rem(task, PAIRS)
-        await_slab(count, piece, slab, receive_one)
-        attend(slab[0], slab[1], slab[2], edges[pl.ds(micro, 1), :], head_taps(lines, pair), keep, padded, blended, result.at[0])
-        back(False)
-
+    phases = attend(slab, lambda: edges[pl.ds(micro, 1), :], lambda: head_taps(lines, pair), keep, padded, blended, result.at[0])
+
+    def between(at):
+        if at < len(steps):
+            steps[at]()
+
+    between(0)
+    for at, phase in enumerate(phases):
+
+        @pl.when(owns)
+        def _():
+            if at == 0:
+                await_slab(count, piece, slab, receive_one)
+            phase()
+            if at == len(phases) - 1:
+                back(False)
+
+        if at > 1:
+            between(at - 1)
+    for at in range(len(phases) - 1, len(steps)):
+        between(at)
+    finish()
     out(True)
     await_rows(mixed_rows, receive_two)
 
@@ -462,19 +493,22 @@
 DMA = pltpu.SemaphoreType.DMA
 
 
-def attention_forward(count, qkv, edges, lines, ident):
+def attention_forward(count, qkv, edges, lines, ident, low=None, spans=()):
     piece = qkv.shape[2]
     length = piece * count
     shapes = kept_shapes(length)
+    low = lines if low is None else low
+    anywhere = pl.BlockSpec(memory_space=pl.ANY)
     results = pl.pallas_call(
-        functools.partial(forward_kernel, count, piece),
+        functools.partial(forward_kernel, count, piece, spans),
         out_shape=[
             jax.ShapeDtypeStruct((1, MICRO, piece, D), BF16),
             jax.ShapeDtypeStruct((3, length, LANES), BF16),
         ]
-        + [jax.ShapeDtypeStruct(shapes[name], F32) for name in KEPT],
-        in_specs=[VMEM] * 3,
-        out_specs=[VMEM] * (2 + len(KEPT)),
+        + [jax.ShapeDtypeStruct(shapes[name], F32) for name in KEPT]
+        + [spread_shape(low, span) for span in spans],
+        in_specs=[VMEM] * 4,
+        out_specs=[VMEM] * (2 + len(KEPT)) + [anywhere] * len(spans),
         scratch_shapes=[
             pltpu.VMEM((length + LANES, LANES), BF16),
             pltpu.VMEM((length, LANES), F32),
@@ -483,11 +517,12 @@
             DMA((count,)),
             DMA((count,)),
             DMA((TASKS,)),
-        ],
+        ]
+        + [one for span in spans for one in spread_semaphores(span)],
         compiler_params=pltpu.CompilerParams(collective_id=ident, has_side_effects=True, vmem_limit_bytes=60 << 20),
         name="attend_forward",
-    )(qkv, edges, lines)
-    return results[0][0], results[1:]
+    )(qkv, edges, lines, low)
+    return results[0][0], results[1 : 2 + len(KEPT)], [flat_rows(one) for one in results[2 + len(KEPT) :]]
 
 
 def attention_backward(count, grads, edges, lines, kept, ident):
@@ -554,19 +589,72 @@
     return pl.pallas_call(arrange_kernel, out_shape=ARRANGED, in_specs=[VMEM] * 3, out_specs=[VMEM] * len(ARRANGED), name="arrange")(*smalls)
 
 
-def gather_kernel(shard, params, first, second, out, *refs):
+PLANES = 4
+
+
+def gather_kernel(spans, low, params, first, second, *refs):
+    outs, refs = refs[: len(spans)], refs[len(spans) :]
     targets, refs = refs[: len(ARRANGED)], refs[len(ARRANGED) :]
-    gather_body(shard, out, lambda: arrange((params, first, second), targets), *refs)
-
-
-def gather_body(shard, out, aside, local_sem, z_send, z_got, x_send, x_got, y_send, y_got, core_send, core_got):
+    begin, steps, finish = spread_all(spans, low, outs, refs)
+    me, x = lax.axis_index("dp"), lax.axis_index("rep")
+    core, y, z = lax.rem(me, 2), lax.rem(me // 2, 2), me // 4
+    barrier = pltpu.get_barrier_semaphore()
+    for where in ({"rep": 1 - x}, {"dp": me + 2 - 4 * y}, {"dp": me + 1 - 2 * core}):
+        pl.semaphore_signal(barrier, inc=1, device_id=where, device_id_type=MESH)
+    for sign in (1, -1):
+
+        @pl.when((z + sign >= 0) & (z + sign < PLANES))
+        def _():
+            pl.semaphore_signal(barrier, inc=1, device_id={"dp": me + 4 * sign}, device_id_type=MESH)
+
+    pl.semaphore_wait(barrier, 4 + jnp.where((z > 0) & (z < PLANES - 1), 1, 0))
+    begin()
+    arrange((params, first, second), targets)
+    for step in steps:
+        step()
+    finish()
+
+
+def spread_semaphores(span):
+    planes = span[2] - span[1]
+    return [DMA, DMA((planes, 2, 2)), DMA((planes, 2))] + [DMA((planes, 2, 2, 2))] * 5 + [DMA]
+
+
+def spread_shape(low, span):
+    return jax.ShapeDtypeStruct((span[2] - span[1], 2, 2) + low.shape[1:], BF16)
+
+
+def flat_rows(blocks):
+    return blocks.reshape(-1, D)
+
+
+def spread_all(spans, low, outs, semaphores):
+    each = len(semaphores) // max(len(spans), 1)
+    parts = [
+        spread(low.at[level], out, bottom, top, *semaphores[at * each : (at + 1) * each])
+        for at, ((level, bottom, top), out) in enumerate(zip(spans, outs))
+    ]
+
+    def together(actions):
+        def run():
+            for action in actions:
+                action()
+
+        return run
+
+    steps = [together(actions) for actions in zip(*[part[1] for part in parts])]
+    return together([part[0] for part in parts]), steps, together([part[2] for part in parts])
+
+
+def spread(shard, out, bottom, top, local_sem, z_send, z_got, x_send, x_got, y_send, y_got, core_send, core_got):
     me = lax.axis_index("dp")
     x = lax.axis_index("rep")
     core, y, z = lax.rem(me, 2), lax.rem(me // 2, 2), me // 4
     half = shard.shape[0] // 2
     part = half // 2
 
-    barrier = pltpu.get_barrier_semaphore()
+    def held(plane):
+        return (plane >= bottom) & (plane < top)
 
     def peer(axis, sign=1):
         if axis == "x":
@@ -577,73 +665,57 @@
             return {"dp": me + 1 - 2 * core}
         return {"dp": me + 4 * sign}
 
-    for axis in ("x", "y", "core"):
-        pl.semaphore_signal(barrier, inc=1, device_id=peer(axis), device_id_type=MESH)
-    for sign in (1, -1):
-
-        @pl.when((z + sign >= 0) & (z + sign < 4))
-        def _():
-            pl.semaphore_signal(barrier, inc=1, device_id=peer("z", sign), device_id_type=MESH)
-
-    pl.semaphore_wait(barrier, 4 + jnp.where((z > 0) & (z < 3), 1, 0))
-
     def rows(side, sub):
         return pl.ds(pl.multiple_of(side * half + sub * part, part), part)
 
-    def side_rows(side):
-        return pl.ds(pl.multiple_of(side * half, half), half)
-
     def remote(source, target, send, receive, where):
         return pltpu.make_async_remote_copy(source, target, send, receive, device_id=where, device_id_type=MESH)
 
     def spot(plane, row, side, sub):
-        return out.at[plane, row, core, rows(side, sub), :]
+        return out.at[plane - bottom, row, core, rows(side, sub), :]
 
     def move(axis, plane, row, side, sub, source=None):
         target = spot(plane, row, side, sub)
         source = target if source is None else source
+        at = plane - bottom
         if axis == "core":
-            return remote(source, target, core_send.at[plane, row, side, sub], core_got, peer("core"))
+            return remote(source, target, core_send.at[at, row, side, sub], core_got, peer("core"))
         send, receive = (x_send, x_got) if axis == "x" else (y_send, y_got)
-        return remote(source, target, send.at[plane, row, side, sub], receive.at[plane, row, side, sub], peer(axis))
+        return remote(source, target, send.at[at, row, side, sub], receive.at[at, row, side, sub], peer(axis))
 
     def climb(plane, sub, sign, source=None):
         target = spot(plane, y, x, sub)
         way = 0 if sign > 0 else 1
-        return remote(target if source is None else source, target, z_send.at[plane, sub, way], z_got.at[plane, sub], peer("z", sign))
-
-    own = pltpu.make_async_copy(shard, out.at[z, y, core], local_sem)
-    own.start()
-    for sub in range(2):
-        for sign in (1, -1):
-
-            @pl.when((z + sign >= 0) & (z + sign < 4))
-            def _():
-                climb(z, sub, sign, shard.at[rows(x, sub), :]).start()
-
-        move("y", z, y, x, sub, shard.at[rows(x, sub), :]).start()
-    for side in range(2):
-        for sub in range(2):
-            move("core", z, y, side, sub, shard.at[rows(side, sub), :]).start()
-
-    aside()
+        at = plane - bottom
+        return remote(target if source is None else source, target, z_send.at[at, sub, way], z_got.at[at, sub], peer("z", sign))
+
+    def inside(sign, act):
+        pl.when((z + sign >= 0) & (z + sign < PLANES))(act)
+
+    def begin():
+        @pl.when(held(z))
+        def _():
+            pltpu.make_async_copy(shard, out.at[z - bottom, y, core], local_sem).start()
+            for sub in range(2):
+                for sign in (1, -1):
+                    inside(sign, lambda: climb(z, sub, sign, shard.at[rows(x, sub), :]).start())
+                move("y", z, y, x, sub, shard.at[rows(x, sub), :]).start()
+            for side in range(2):
+                for sub in range(2):
+                    move("core", z, y, side, sub, shard.at[rows(side, sub), :]).start()
 
     def at_distance(distance, act):
         for sign in (1, -1):
             plane = z - sign * distance
 
-            @pl.when((plane >= 0) & (plane < 4))
+            @pl.when(held(plane))
             def _():
                 act(plane, sign)
 
     def from_z(plane, sign):
         for sub in range(2):
             climb(plane, sub, sign).wait_recv()
-
-            @pl.when((z + sign >= 0) & (z + sign < 4))
-            def _():
-                climb(plane, sub, sign).start()
-
+            inside(sign, lambda: climb(plane, sub, sign).start())
             for axis in ("x", "y", "core"):
                 move(axis, plane, y, x, sub).start()
 
@@ -663,77 +735,70 @@
         take("y", plane, 1 - y, 1 - x, 0)
         take("x", plane, 1 - y, 1 - x, 1)
 
-    at_distance(1, from_z)
-    for sub in range(2):
-        take("y", z, 1 - y, x, sub, "x")
-    at_distance(2, from_z)
-    at_distance(1, first_square)
-    at_distance(3, from_z)
-    at_distance(2, first_square)
-    for sub in range(2):
-        take("x", z, 1 - y, 1 - x, sub)
-    at_distance(1, second_square)
-    at_distance(3, first_square)
-    at_distance(2, second_square)
-    at_distance(3, second_square)
-    own.wait()
-
-    def finish(plane, sign):
+    def own_first():
+        @pl.when(held(z))
+        def _():
+            for sub in range(2):
+                take("y", z, 1 - y, x, sub, "x")
+
+    def own_last():
+        @pl.when(held(z))
+        def _():
+            for sub in range(2):
+                take("x", z, 1 - y, 1 - x, sub)
+
+    def stage(distance, act):
+        return lambda: at_distance(distance, act)
+
+    steps = [
+        stage(1, from_z), own_first, stage(2, from_z), stage(1, first_square), stage(3, from_z), stage(2, first_square),
+        own_last, stage(1, second_square), stage(3, first_square), stage(2, second_square), stage(3, second_square),
+    ]
+
+    def sent(plane, sign):
         for sub in range(2):
-
-            @pl.when((z + sign >= 0) & (z + sign < 4))
-            def _():
-                climb(plane, sub, sign).wait_send()
-
+            inside(sign, lambda: climb(plane, sub, sign).wait_send())
             move("x", plane, y, x, sub).wait_send()
             move("y", plane, y, x, sub).wait_send()
         move("y", plane, y, 1 - x, 0).wait_send()
         move("x", plane, 1 - y, x, 1).wait_send()
 
-    for distance in (1, 2, 3):
-        at_distance(distance, finish)
-    for sub in range(2):
-        for sign in (1, -1):
-
-            @pl.when((z + sign >= 0) & (z + sign < 4))
-            def _():
-                climb(z, sub, sign).wait_send()
-
-        move("y", z, y, x, sub).wait_send()
-        move("x", z, 1 - y, x, sub).wait_send()
-
-    def core_sent(index, carry):
-        plane, row, side, sub = index // 8, lax.rem(index // 4, 2), lax.rem(index // 2, 2), lax.rem(index, 2)
-        move("core", plane, row, side, sub).wait_send()
-        return carry
-
-    lax.fori_loop(0, 32, core_sent, 0)
-    column = out.at[:, :, 1 - core]
-    pltpu.make_async_copy(column, column, core_got).wait()
-
-
-def gather(shard, *smalls):
-    block_rows = shard.shape[0]
+    def finish():
+        for distance in (1, 2, 3):
+            at_distance(distance, sent)
+
+        @pl.when(held(z))
+        def _():
+            pltpu.make_async_copy(shard, out.at[z - bottom, y, core], local_sem).wait()
+            for sub in range(2):
+                for sign in (1, -1):
+                    inside(sign, lambda: climb(z, sub, sign).wait_send())
+                move("y", z, y, x, sub).wait_send()
+                move("x", z, 1 - y, x, sub).wait_send()
+
+        def core_sent(index, carry):
+            plane, row, side, sub = bottom + index // 8, lax.rem(index // 4, 2), lax.rem(index // 2, 2), lax.rem(index, 2)
+            move("core", plane, row, side, sub).wait_send()
+            return carry
+
+        lax.fori_loop(0, 8 * (top - bottom), core_sent, 0)
+        column = out.at[:, :, 1 - core]
+        pltpu.make_async_copy(column, column, core_got).wait()
+
+    return begin, steps, finish
+
+
+def gather(low, spans, *smalls):
     results = pl.pallas_call(
-        gather_kernel,
-        out_shape=[jax.ShapeDtypeStruct((4, 2, 2, block_rows, D), BF16)] + ARRANGED,
+        functools.partial(gather_kernel, spans),
+        out_shape=[spread_shape(low, span) for span in spans] + ARRANGED,
         in_specs=[VMEM] * 4,
-        out_specs=[pl.BlockSpec(memory_space=pl.ANY)] + [VMEM] * len(ARRANGED),
-        scratch_shapes=[
-            DMA,
-            DMA((4, 2, 2)),
-            DMA((4, 2)),
-            DMA((4, 2, 2, 2)),
-            DMA((4, 2, 2, 2)),
-            DMA((4, 2, 2, 2)),
-            DMA((4, 2, 2, 2)),
-            DMA((4, 2, 2, 2)),
-            DMA,
-        ],
+        out_specs=[pl.BlockSpec(memory_space=pl.ANY)] * len(spans) + [VMEM] * len(ARRANGED),
+        scratch_shapes=[one for span in spans for one in spread_semaphores(span)],
         compiler_params=pltpu.CompilerParams(collective_id=4, has_side_effects=True),
         name="gather",
-    )(shard, *smalls)
-    return results[0].reshape(16 * block_rows, D), results[1:]
+    )(low, *smalls)
+    return [flat_rows(one) for one in results[: len(spans)]], results[len(spans) :]
 
 
 CHUNK = 32
@@ -1071,20 +1136,22 @@
     return jnp.sum(rows.reshape(-1, 8, D), axis=0)
 
 
-def split_rows(rows):
-    return rows[: 3 * D].reshape(3, D, D), rows[3 * D : 4 * D], rows[4 * D : 4 * D + FF], rows[4 * D + FF :]
-
-
-def forward_layer(count, inputs, rows, small, edges, ident):
+def split_rows(rest):
+    return rest[:D], rest[D : D + FF], rest[D + FF :]
+
+
+def forward_layer(count, inputs, proj, rest, small, edges, ident, low=None, spans=()):
     piece = inputs.shape[0] // MICRO
     lines, bias_up = small
-    proj, out_weight, up_weight, down_weight = split_rows(rows)
+    proj = proj.reshape(3, D, D)
     low_in = inputs.astype(BF16)
     query = (dense(low_in, proj[0]) + lines[0:1]).astype(BF16)
     key = dense(low_in, proj[1]).astype(BF16)
     value = (dense(low_in, proj[2]) + lines[1:2]).astype(BF16)
     qkv = jnp.stack([query, key, value])
-    low_comb, kept = attention_forward(count, qkv.reshape(3, MICRO, piece, D), edges, lines, ident)
+    low_comb, kept, fetched = attention_forward(count, qkv.reshape(3, MICRO, piece, D), edges, lines, ident, low, spans)
+    rest = fetched[0] if fetched else rest
+    out_weight, up_weight, down_weight = split_rows(rest)
     low_comb = low_comb.reshape(MICRO * piece, D)
     resid_one = inputs + (dense(low_comb, out_weight) + lines[2:3])
     hidden_one = layer_norm(resid_one, lines[4:5], lines[5:6])
@@ -1093,15 +1160,15 @@
     low_act = jax.nn.gelu(upward).astype(BF16)
     resid_two = hidden_one + (dense(low_act, down_weight) + lines[3:4])
     output = layer_norm(resid_two, lines[6:7], lines[7:8])
-    return output, (low_in, kept, low_comb, resid_one, low_hidden, upward, low_act, resid_two)
-
-
-def backward_layer(count, grad_output, rows, small, edges, state, ident):
-    low_in, kept, low_comb, resid_one, low_hidden, upward, low_act, resid_two = state
+    return output, (proj, rest, low_in, kept, low_comb, resid_one, low_hidden, upward, low_act, resid_two), fetched[1:]
+
+
+def backward_layer(count, grad_output, small, edges, state, ident):
+    proj, rest, low_in, kept, low_comb, resid_one, low_hidden, upward, low_act, resid_two = state
     total = low_in.shape[0]
     piece = total // MICRO
     lines, _ = small
-    proj, out_weight, up_weight, down_weight = split_rows(rows)
+    out_weight, up_weight, down_weight = split_rows(rest)
     grad_two, grad_gain_two, grad_shift_two = layer_norm_back(resid_two, lines[6:7], grad_output)
     low_down = grad_two.astype(BF16)
     grad_act = dense(low_down, down_weight, NT)
@@ -1158,25 +1225,29 @@
     piece = hidden.shape[3]
     total = MICRO * piece
     low_weights = weights.astype(BF16)
-    held = [lax.all_gather(low_weights[level], "dp", axis=0, tiled=True) for level in range(LAYERS)]
+    limits = bounds[0, :, 0, :]
+    edges = jnp.pad(limits.astype(F32), ((0, 0), (0, LANES - limits.shape[1])))
+    positions = lax.axis_index("dp") * piece + lax.broadcasted_iota(jnp.int32, (MICRO, piece, 1), 1)
+    valid = positions < limits[:, -1].reshape(MICRO, 1, 1)
+    activation = hidden[0, :, 0].reshape(total, D).astype(F32)
+    states = [None] * LAYERS
     if count == 16:
-        held[0], prepared = gather(low_weights[0], small_params, first_small[0], second_small[0])
+        (proj,), prepared = gather(low_weights, ((0, 0, 1),), small_params, first_small[0], second_small[0])
     else:
         prepared = arranged(small_params, first_small[0], second_small[0])
     smalls = [(prepared[level], prepared[LAYERS + level]) for level in range(LAYERS)]
-    limits = bounds[0, :, 0, :]
-    edges = jnp.pad(limits.astype(F32), ((0, 0), (0, LANES - limits.shape[1])))
-    positions = lax.axis_index("dp") * piece + jnp.arange(piece, dtype=jnp.int32)
-    valid = (positions[None, :] < limits[:, -1:]).astype(F32).reshape(total, 1)
-    activation = hidden[0, :, 0].reshape(total, D).astype(F32)
-    states = []
     for level in range(LAYERS):
-        activation, state = forward_layer(count, activation, held[level], smalls[level], edges, 1)
-        states.append(state)
-    gradient = cotangent[0, :, 0].reshape(total, D).astype(F32) * valid
+        if count == 16:
+            spans = ((level, 1, PLANES),) + (((level + 1, 0, 1),) if level + 1 < LAYERS else ())
+            activation, states[level], more = forward_layer(count, activation, proj, None, smalls[level], edges, 1 + 4 * level, low_weights, spans)
+            proj = more[0] if more else None
+        else:
+            rows = lax.all_gather(low_weights[level], "dp", axis=0, tiled=True)
+            activation, states[level], _ = forward_layer(count, activation, rows[: 3 * D], rows[3 * D :], smalls[level], edges, 1)
+    gradient = jnp.where(valid, cotangent[0, :, 0].astype(F32), 0.0).reshape(total, D)
     mates = [None] * LAYERS
     for level in reversed(range(LAYERS)):
-        gradient, mates[level] = backward_layer(count, gradient, held[level], smalls[level], edges, states[level], 2)
+        gradient, mates[level] = backward_layer(count, gradient, smalls[level], edges, states[level], 2)
     if count == 16:
         grad_big, mean_big, small_both = settle(mates, weights, first_big[0], second_big[0], *prepared[2 * LAYERS :])
         new_smalls = finish(small_both, small_params, outer_small, first_small[0], second_small[0])

time: 566 us -> 559 us (0.988)
  Pallas kernels: 439 us -> 466 us
  between operations: 15.3 us -> 1.72 us
  local copies, waits for them, and re-layouts: 17.4 us -> 5.91 us
    pallas_call x3, Pallas kernels: 173 us -> 202 us  [the longest x2 176 us: attention_forward(): pl.pallas_call(functools.partial(forward_kernel, count, piece, spans), ou...]
  transfers between devices with their start and end apart: 1 -> 0, of which waited for: 0 -> 0; matrix products, arithmetic and copies ran while one was open for 5% -> 0% of each run, Pallas kernels for 25% -> 0%
where the time goes in v6:
time: 559 us; the launch traced here: 552 us
  Pallas kernels  466 us (83%)
  matrix products  52.6 us (9%)
  other arithmetic  26.1 us (5%)
  local copies, waits for them, and re-layouts  5.91 us (1%)
    pallas_call x1, Pallas kernels, settle(): pl.pallas_call(functools.partial(settle_kernel, block_rows), out_shape=[j...  185 us
    pallas_call x2, Pallas kernels, attention_forward(): pl.pallas_call(functools.partial(forward_kernel, count, piece, spans), ou...  176 us
    pallas_call x2, Pallas kernels, attention_backward(): pl.pallas_call(functools.partial(backward_kernel, count, piece), out_shap...  77.4 us
    dot_general x24, matrix products, mm(): return lax.dot_general(a, b, dims, preferred_element_type=F32)  52.6 us
    pallas_call x1, Pallas kernels, gather(): pl.pallas_call(functools.partial(gather_kernel, spans), out_shape=[spread...  25.6 us

profile of v6, /device:TPU:0, one launch (start us, length us, event | category | flops | bytes accessed | tf_op | source)
XLA Modules:
  0.0 551.8 jit_solution(6328826294210826054)
XLA Ops:
  0.6 3.4 convert_element_type.102.low
  4.0 25.6 %gather.1 = (bf16[1,2,2,576,768]{4,3,2,1,0:T(8,128)(2,1)}, f32[16,768]{1,0:T(8,128)}, f32[16,768]{1,0:T(8,128)}, f32[1,3072]{1,0:T(1,128)}, f32[1,3072]{1,0:T(1,...) custom-call(bf16[2,576,768]{2,1,0:T(8,128)(2,1)} %convert_element_type.102.low, f32[2,9612]{1,0:T(2,128)} %params.3, ...), custom_call_target="tpu_custom_call" | custom-call | tf_op jit(solution)/shard_map/gather/pallas_call | solution.py:792
  29.6 1.4 slice_reduce_fusion.1
  31.0 1.6 fusion.66
  32.6 1.6 fusion.67
  34.3 1.6 convolution_convert_fusion
  35.9 0.9 pad_maximum_fusion.qkv
  36.8 0.6 pad.4.edges
  37.4 102.3 %attend_forward.2 = (bf16[1,2,64,768]{3,2,1,0:T(8,128)(2,1)}, bf16[3,1024,128]{2,1,0:T(8,128)(2,1)}, f32[128,128]{1,0:T(8,128)}, f32[128,128]{1,0:T(8,128)}, f32...) custom-call(bf16[3,2,64,768]{3,2,1,0:T(8,128)(2,1)} %pad_maximum_fus, ...), custom_call_target="tpu_custom_call" | custom-call | tf_op jit(solution)/shard_map/attend_forward/pallas_call | solution.py:502
  139.7 1.8 fusion.85
  141.9 5.3 multiply_convert_fusion.1
  147.2 3.5 fusion.86
  151.1 0.3 fusion.64
  151.4 0.3 convolution_convert_fusion.3
  151.8 0.3 fusion.65
  152.1 0.9 pad_maximum_fusion.1.qkv
  153.0 73.8 %attend_forward.3 = (bf16[1,2,64,768]{3,2,1,0:T(8,128)(2,1)}, bf16[3,1024,128]{2,1,0:T(8,128)(2,1)}, f32[128,128]{1,0:T(8,128)}, f32[128,128]{1,0:T(8,128)}, f32...) custom-call(bf16[3,2,64,768]{3,2,1,0:T(8,128)(2,1)} %pad_maximum_fus, ...), custom_call_target="tpu_custom_call" | custom-call | tf_op jit(solution)/shard_map/attend_forward/pallas_call | solution.py:502
  226.8 1.8 fusion.87
  229.0 5.3 multiply_convert_fusion
  234.3 3.5 fusion.88
  238.5 0.8 bitcast_reduce_fusion.refs_23_
  239.9 1.0 fusion.82
  240.9 4.8 fusion.37.refs_15_
  245.7 3.5 multiply_reduce_fusion.11
  249.2 0.7 bitcast_reduce_fusion.1
  250.1 2.6 convolution_convert_fusion.2
  252.7 35.4 %attend_backward.2 = (bf16[3,2,64,768]{3,2,1,0:T(8,128)(2,1)}, f32[6,2,256]{2,1,0:T(2,128)}) custom-call(bf16[1,2,64,768]{3,2,1,0:T(8,128)(2,1)} %bitcast.170, f32[2,128]{1,0:T(2,128)} %pad.4.edges, f32[16,768]{1,0:T(8,128)} %get-tuple-element.66.lines, bf16[3,1024,128]{2,1,0:T(8,128)(2,1)} %get-tuple-element.70.slab, f32[128,128]{1,0:T(8,128)} %get-tuple-element.71.refs_0_, ...), custom_call_target="tpu_custom_call" | custom-call | tf_op jit(solution)/shard_map/attend_backward/pallas_call | solution.py:531
  288.1 1.2 fusion.84
  289.3 1.8 fusion.69
  291.1 2.0 convolution_add_fusion.5
  293.1 1.9 multiply_reduce_fusion.10
  295.0 0.7 bitcast_reduce_fusion.3
  295.9 0.5 copy-done.22
  296.4 4.6 fusion.30.refs_2_
  301.1 0.9 multiply_reduce_fusion.9
  302.0 0.7 bitcast_reduce_fusion.5
  302.8 0.9 fusion.79
  303.7 1.2 convolution_convert_fusion.1
  304.9 42.0 %attend_backward.3 = (bf16[3,2,64,768]{3,2,1,0:T(8,128)(2,1)}, f32[6,2,256]{2,1,0:T(2,128)}) custom-call(bf16[1,2,64,768]{3,2,1,0:T(8,128)(2,1)} %bitcast.169, f32[2,128]{1,0:T(2,128)} %pad.4.edges, f32[16,768]{1,0:T(8,128)} %get-tuple-element.61.lines, bf16[3,1024,128]{2,1,0:T(8,128)(2,1)} %get-tuple-element.84.slab, f32[128,128]{1,0:T(8,128)} %get-tuple-element.85.refs_0_, ...), custom_call_target="tpu_custom_call" | custom-call | tf_op jit(solution)/shard_map/attend_backward/pallas_call | solution.py:531
  347.2 0.7 select_reduce_fusion.refs_24_
  347.9 184.5 %settle.1 = (f32[2,576,768]{2,1,0:T(8,128)}, f32[2,576,768]{2,1,0:T(8,128)}, f32[16,2,2,768]{3,2,1,0:T(2,128)}) custom-call(bf16[128,768]{1,0:T(8,128)(2,1)} %bitcast.160, bf16[128,768]{1,0:T(8,128)(2,1)} %bitcast.166, bf16[128,3072]{1,0:T(8,128)(2,1)} %copy-done.17, bf16[128,3072]{1,0:T(8,128)(2,1)} %copy-done.14, bf16[3,128,768]{2,1,0:T(8,128)(2,1)} %bitcast.147, ...), custom_call_target="tpu_custom_call" | custom-call | tf_op jit(solution)/shard_map/settle/pallas_call | solution.py:1043
  532.5 9.2 %fusion.78 = (bf16[2,576,768]{2,1,0:T(8,128)(2,1)}, f32[2,576,768]{2,1,0:T(8,128)}, f32[2,576,768]{2,1,0:T(8,128)}) fusion(f32[2,576,768]{2,1,0:T(8,128)} %refs_26_.1, f32[2,576,768]{2,1,0:T(8,128)} %get-tuple-element.106, f32[2,576,768]{2,1,0:T(8,128)} %param.20), kind=kLoop, calls=%fused_computation.159 | loop fusion | flops 6193152 | bytes 19464192 | tf_op jit(solution)/shard_map/convert_element_type | solution.py:1281
  541.9 4.0 fusion.23
  545.9 1.8 finish.1
  547.8 1.2 fusion.83
  548.9 0.5 fusion.68
  549.5 0.5 convolution_add_fusion.3
  550.0 1.3 fusion.45
  (93 shorter events, 3.3 us)
Async XLA Ops:
  4.0 27.0 %copy-start.18 = (bf16[1,2,1,64,768]{4,3,2,1,0:T(8,128)(2,1)S(1)}, bf16[1,2,1,64,768]{4,3,2,1,0:T(8,128)(2,1)}, u32[]{:S(2)}) copy-start(bf16[1,2,1,64,768]{4,3,2,1,0:T(8,128)(2,1)} %param.11) | copy-start | bytes 589828
  34.3 2.5 copy-start.19
  139.7 2.2 copy-start.21
  141.9 5.3 copy-start.7
  147.2 3.6 copy-start.14
  147.2 3.9 copy-start.4
  151.1 0.7 copy-start.8
  226.8 2.2 copy-start.20
  229.0 5.3 copy-start.9
  234.3 3.5 copy-start.15
  234.3 4.2 copy-start.2
  240.9 4.8 copy-start.10
  245.7 3.5 copy-start.16
  250.1 38.0 %copy-start.11 = (bf16[128,768]{1,0:T(8,128)(2,1)}, bf16[128,768]{1,0:T(8,128)(2,1)S(1)}, u32[]{:S(2)}) copy-start(bf16[128,768]{1,0:T(8,128)(2,1)S(1)} %get-tuple-element.166.refs_18_) | copy-start | bytes 589828
  291.1 10.0 %slice-start = ((s8[10616832]{0:T(1024)(128)(4,1)}), s8[4194304]{0:T(1024)(128)(4,1)S(1)}, s32[]{:S(2)}) async-start(s8[10616832]{0:T(1024)(128)(4,1)} %bitcast.183), calls=%async_computation | async-start | bytes 8388608
  295.0 1.4 copy-start.22
  295.8 5.3 slice-start.1
  295.9 5.1 copy-start.12
  296.4 4.7 slice-start.2
  301.1 1.0 copy-start.17
  303.7 43.2 %copy-start.13 = (bf16[128,768]{1,0:T(8,128)(2,1)}, bf16[128,768]{1,0:T(8,128)(2,1)S(1)}, u32[]{:S(2)}) copy-start(bf16[128,768]{1,0:T(8,128)(2,1)S(1)} %get-tuple-element.162.refs_5_) | copy-start | bytes 589828
  532.5 9.2 %copy-start = (f32[1,2,576,768]{3,2,1,0:T(8,128)S(1)}, f32[1,2,576,768]{3,2,1,0:T(8,128)}, u32[]{:S(2)}) copy-start(f32[1,2,576,768]{3,2,1,0:T(8,128)} %param.16) | copy-start | bytes 10616836
  532.5 9.2 %copy-start.1 = (f32[1,2,576,768]{3,2,1,0:T(8,128)S(1)}, f32[1,2,576,768]{3,2,1,0:T(8,128)}, u32[]{:S(2)}) copy-start(f32[1,2,576,768]{3,2,1,0:T(8,128)} %param.17) | copy-start | bytes 10616836
  532.5 9.4 %copy-start.5 = (f32[2,576,768]{2,1,0:T(8,128)S(1)}, f32[2,576,768]{2,1,0:T(8,128)}, u32[]{:S(2)}) copy-start(f32[2,576,768]{2,1,0:T(8,128)} %get-tuple-element.102) | copy-start | bytes 10616836
  541.9 7.0 %copy-start.3 = (bf16[1,2,2,576,768]{4,3,2,1,0:T(8,128)(2,1)S(1)}, bf16[1,2,2,576,768]{4,3,2,1,0:T(8,128)(2,1)}, u32[]{:S(2)}) copy-start(bf16[1,2,2,576,768]{4,3,2,1,0:T(8,128)(2,1)} %get-tuple-element.60) | copy-start | bytes 10616836
  548.9 1.1 copy-start.6

commit v7 on v6

--- a/solution.py
+++ b/solution.py
@@ -141,16 +141,25 @@
     lax.fori_loop(0, length // LANES, block, 0)
 
 
+def put_rows(ref, at, start, rows):
+    half = ref.shape[2]
+    ref[at, start // half, pl.ds(pl.multiple_of(lax.rem(start, half), LANES), LANES), :] = rows
+
+
+def whole(ref, at):
+    return ref[at].reshape(-1, LANES)
+
+
 def attend(slab, edges, taps, keep, padded, blended, result):
-    length = slab.shape[1]
+    length = slab.shape[1] * slab.shape[2]
 
     def begin():
         low_marks, high_marks = mark_columns(edges())
         at = iota((MARKS, length), 1)
         member = ((low_marks <= at) & (at < high_marks)).astype(F32).astype(BF16)
         counts = (high_marks - low_marks).astype(F32)
-        q_marks = per_head(mm(member, slab[0]) / counts)
-        k_marks = per_head(mm(member, slab[1]) / counts)
+        q_marks = per_head(mm(member, whole(slab, 0)) / counts)
+        k_marks = per_head(mm(member, whole(slab, 1)) / counts)
         scores = jnp.where(diagonal_blocks(), SCALE * exact(q_marks, k_marks, NT), NEG)
         weights = jnp.exp(scores - jnp.max(scores, axis=1, keepdims=True))
         kernel = weights / jnp.sum(weights, axis=1, keepdims=True)
@@ -177,14 +186,14 @@
 
     def over_keys():
         valid = iota((1, length), 1) < mark_columns(edges())[1][MARKS - 1 :]
-        key_scores = jnp.where(valid, SCALE * mm_left(keep["q_marks"][...], slab[1], NT), NEG)
+        key_scores = jnp.where(valid, SCALE * mm_left(keep["q_marks"][...], whole(slab, 1), NT), NEG)
         key_exp = jnp.where(valid, jnp.exp(key_scores - jnp.max(key_scores, axis=1, keepdims=True)), 0.0)
         key_weights = key_exp / jnp.sum(key_exp, axis=1, keepdims=True)
         keep["key_weights"][...] = key_weights
-        keep["summary"][...] = jnp.where(diagonal_blocks(), mm_left(key_weights, slab[2]), 0.0)
+        keep["summary"][...] = jnp.where(diagonal_blocks(), mm_left(key_weights, whole(slab, 2)), 0.0)
 
     def over_tokens():
-        token_scores = SCALE * mm_left(keep["k_marks"][...], slab[0], NT)
+        token_scores = SCALE * mm_left(keep["k_marks"][...], whole(slab, 0), NT)
         token_exp = jnp.exp(token_scores - head_tops(token_scores))
         keep["token_weights"][...] = token_exp / head_sums(token_exp)
 
@@ -192,14 +201,14 @@
         mixed = exact(keep["inverse"][NS_ITERS], keep["summary"][...])
         keep["mixed"][...] = mixed
         blended[...] = mm_both(keep["token_weights"][...], mixed, TN)
-        values = slab[2]
+        values = whole(slab, 2)
         valid_column = iota((length, 1), 0) < mark_columns(edges())[1][MARKS - 1 :]
         padded[0:HALF, :] = jnp.zeros((HALF, LANES), BF16)
         padded[HALF : HALF + length, :] = jnp.where(valid_column, values, jnp.zeros_like(values))
         padded[HALF + length :, :] = jnp.zeros((LANES - HALF, LANES), BF16)
 
         def store(start, block):
-            result[pl.ds(start, LANES), :] = (blended[pl.ds(start, LANES), :] + block).astype(BF16)
+            put_rows(result, 0, start, (blended[pl.ds(start, LANES), :] + block).astype(BF16))
 
         convolve(padded, [band(one) for one in taps()], length, store)
 
@@ -250,9 +259,9 @@
     grad_q_marks = (grad_q_marks[:MARKS] + grad_q_marks[MARKS:]) / counts
     grad_k_marks = (grad_k_marks[:MARKS] + grad_k_marks[MARKS:]) / counts
     high, rest = halves(grad_q_marks)
-    result[0] = (mm_both(grad_token, k_marks, TN) + mm(member, high) + mm(member, rest)).astype(BF16)
+    result[0] = (mm_both(grad_token, k_marks, TN) + mm(member, high) + mm(member, rest)).astype(BF16).reshape(result.shape[1:])
     high, rest = halves(grad_k_marks)
-    result[1] = (mm_both(grad_key, q_marks, TN) + mm(member, high) + mm(member, rest)).astype(BF16)
+    result[1] = (mm_both(grad_key, q_marks, TN) + mm(member, high) + mm(member, rest)).astype(BF16).reshape(result.shape[1:])
     blended[...] = mm_both(key_weights, grad_summary, TN)
     last = high_marks[MARKS - 1 :]
     valid_column = iota((length, 1), 0) < last
@@ -266,7 +275,7 @@
     def store(start, block):
         rows = start + iota((LANES, 1), 0)
         total_rows = blended[pl.ds(start, LANES), :] + jnp.where(rows < last, block, 0.0)
-        result[2, pl.ds(start, LANES), :] = total_rows.astype(BF16)
+        put_rows(result, 2, start, total_rows.astype(BF16))
 
     convolve(padded_grads, [band_back(one) for one in taps], length, store)
     first = iota((LANES, LANES), 1) < HEAD_DIM
@@ -295,7 +304,6 @@
         grad_taps[head : head + 1, :] = line
 
 
-TASKS = MICRO * PAIRS
 KEPT = ("q_marks", "k_marks", "kernel", "total", "inverse", "product", "two", "three", "key_weights", "summary", "mixed", "token_weights")
 
 
@@ -309,112 +317,138 @@
     return shapes
 
 
-def owner_of(task, count):
-    return task * count // TASKS
-
-
-def task_of(me, count):
-    task = (me * TASKS + count - 1) // count
-    return task, owner_of(task, count) == me
-
-
-def greet(count, across=False):
-    me = lax.axis_index("dp")
+class Layout:
+    def __init__(self, count):
+        self.count = count
+        self.groups = MICRO if count == 16 else 1
+        self.members = count // self.groups
+        self.tasks = PAIRS * MICRO // self.groups
+
+    def place(self):
+        me = lax.axis_index("dp")
+        self.me, self.group, self.index = me, me // self.members, lax.rem(me, self.members)
+        self.task = (self.index * self.tasks + self.members - 1) // self.members
+        self.owns = self.owner(self.task) == self.index
+        self.micro = self.micro_of(self.task)
+        self.pair = lax.rem(self.task, PAIRS)
+        return self
+
+    def owner(self, task):
+        return task * self.members // self.tasks
+
+    def micro_of(self, task):
+        return self.group if self.groups > 1 else task // PAIRS
+
+    def device(self, index):
+        return {"dp": self.group * self.members + index}
+
+    def block(self, array, task):
+        lanes = pl.ds(pl.multiple_of(lax.rem(task, PAIRS) * LANES, LANES), LANES)
+        return array.at[:, :, :, lanes] if self.groups > 1 else array.at[:, pl.ds(task // PAIRS, 1), :, lanes]
+
+    def rows(self, slab, index, piece):
+        return slab.at[:, :, pl.ds(pl.multiple_of(index * piece, piece), piece), :]
+
+    def mate(self):
+        return {"dp": lax.rem(self.me + self.members, self.count)}
+
+
+def greet(at, everyone=False, mate=False):
     barrier = pltpu.get_barrier_semaphore()
-    if across:
+    size, index = (at.count, at.me) if everyone else (at.members, at.index)
+    if everyone:
         pl.semaphore_signal(barrier, inc=1, device_id={"rep": 1 - lax.axis_index("rep")}, device_id_type=MESH)
+    if mate:
+        pl.semaphore_signal(barrier, inc=1, device_id=at.mate(), device_id_type=MESH)
 
     def signal(step, carry):
-        pl.semaphore_signal(barrier, inc=1, device_id={"dp": lax.rem(me + step, count)}, device_id_type=MESH)
+        other = lax.rem(index + step, size)
+        pl.semaphore_signal(barrier, inc=1, device_id={"dp": other} if everyone else at.device(other), device_id_type=MESH)
         return carry
 
-    lax.fori_loop(1, count, signal, 0)
-    pl.semaphore_wait(barrier, count if across else count - 1)
-
-
-def scatter_tasks(count, piece, source, slab, send, receive):
-    me = lax.axis_index("dp")
-
+    lax.fori_loop(1, size, signal, 0)
+    pl.semaphore_wait(barrier, size - 1 + int(everyone) + int(mate))
+
+
+def scatter_tasks(at, piece, source, slab, send, receive):
     def one(step, finish):
-        task = lax.rem(task_of(me, count)[0] + step, TASKS)
-        owner = owner_of(task, count)
-        micro = task // PAIRS
-        lanes = pl.ds(pl.multiple_of(lax.rem(task, PAIRS) * LANES, LANES), LANES)
-        rows = pl.ds(pl.multiple_of(me * piece, piece), piece)
-        outgoing = source.at[:, micro, :, lanes]
-        landing = slab.at[:, rows, :]
-
-        @pl.when(owner != me)
+        task = lax.rem(at.task + step, at.tasks)
+        owner = at.owner(task)
+        outgoing, landing = at.block(source, task), at.rows(slab, at.index, piece)
+
+        @pl.when(owner != at.index)
         def _():
-            copy = pltpu.make_async_remote_copy(outgoing, landing, send.at[task], receive.at[me], device_id={"dp": owner}, device_id_type=MESH)
+            copy = pltpu.make_async_remote_copy(
+                outgoing, landing, send.at[task], receive.at[at.index], device_id=at.device(owner), device_id_type=MESH
+            )
             if finish:
                 copy.wait_send()
             else:
                 copy.start()
 
-        @pl.when((owner == me) & (not finish))
+        @pl.when((owner == at.index) & (not finish))
         def _():
-            pltpu.make_async_copy(outgoing, landing, receive.at[me]).start()
+            pltpu.make_async_copy(outgoing, landing, receive.at[at.index]).start()
 
     def run(finish):
         def body(step, carry):
             one(step, finish)
             return carry
 
-        lax.fori_loop(0, TASKS, body, 0)
+        lax.fori_loop(0, at.tasks, body, 0)
 
     return run
 
 
-def await_slab(count, piece, slab, receive):
+def await_slab(at, piece, slab, receive):
     def body(origin, carry):
-        landing = slab.at[:, pl.ds(pl.multiple_of(origin * piece, piece), piece), :]
+        landing = at.rows(slab, origin, piece)
         pltpu.make_async_copy(landing, landing, receive.at[origin]).wait()
         return carry
 
-    lax.fori_loop(0, count, body, 0)
-
-
-def return_rows(count, piece, result, target, send, receive):
-    me = lax.axis_index("dp")
-    task = task_of(me, count)[0]
-    micro = task // PAIRS
-    lanes = pl.ds(pl.multiple_of(lax.rem(task, PAIRS) * LANES, LANES), LANES)
-
+    lax.fori_loop(0, at.members, body, 0)
+
+
+def return_rows(at, piece, result, target, send, receive):
     def run(finish):
         def body(step, carry):
-            peer = lax.rem(me + step, count)
-            rows = pl.ds(pl.multiple_of(peer * piece, piece), piece)
-            outgoing = result.at[:, rows, :]
-            landing = target.at[:, micro, :, lanes]
-
-            @pl.when(peer != me)
+            peer = lax.rem(at.index + step, at.members)
+            outgoing, landing = at.rows(result, peer, piece), at.block(target, at.task)
+
+            @pl.when(peer != at.index)
             def _():
-                copy = pltpu.make_async_remote_copy(outgoing, landing, send.at[peer], receive.at[task], device_id={"dp": peer}, device_id_type=MESH)
+                copy = pltpu.make_async_remote_copy(
+                    outgoing, landing, send.at[peer], receive.at[at.task], device_id=at.device(peer), device_id_type=MESH
+                )
                 if finish:
                     copy.wait_send()
                 else:
                     copy.start()
 
-            @pl.when((peer == me) & (not finish))
+            @pl.when((peer == at.index) & (not finish))
             def _():
-                pltpu.make_async_copy(outgoing, landing, receive.at[task]).start()
+                pltpu.make_async_copy(outgoing, landing, receive.at[at.task]).start()
 
             return carry
 
-        lax.fori_loop(0, count, body, 0)
+        lax.fori_loop(0, at.members, body, 0)
 
     return run
 
 
-def await_rows(target, receive):
+def await_rows(at, target, receive):
     def body(task, carry):
-        lanes = pl.ds(pl.multiple_of(lax.rem(task, PAIRS) * LANES, LANES), LANES)
-        landing = target.at[:, task // PAIRS, :, lanes]
+        landing = at.block(target, task)
         pltpu.make_async_copy(landing, landing, receive.at[task]).wait()
         return carry
 
-    lax.fori_loop(0, TASKS, body, 0)
+    lax.fori_loop(0, at.tasks, body, 0)
+
+
+def swap(at, source, target, send, receive):
+    return pltpu.make_async_remote_copy(
+        source.at[1 - at.group], target.at[at.group], send, receive, device_id=at.mate(), device_id_type=MESH
+    )
 
 
 def forward_kernel(count, piece, spans, qkv, edges, lines, low, mixed_rows, slab, *refs):
@@ -422,69 +456,75 @@
     outs, refs = refs[len(KEPT) : len(KEPT) + len(spans)], refs[len(KEPT) + len(spans) :]
     padded, blended, result, send_one, receive_one, send_two, receive_two = refs[:7]
     begin, steps, finish = spread_all(spans, low, outs, refs[7:])
-    me = lax.axis_index("dp")
-    task, owns = task_of(me, count)
-    micro, pair = task // PAIRS, lax.rem(task, PAIRS)
-    greet(count, bool(spans))
-    out = scatter_tasks(count, piece, qkv, slab, send_one, receive_one)
+    at = Layout(count).place()
+    greet(at, bool(spans))
+    out = scatter_tasks(at, piece, qkv, slab, send_one, receive_one)
     out(False)
     begin()
-    back = return_rows(count, piece, result, mixed_rows, send_two, receive_two)
-    phases = attend(slab, lambda: edges[pl.ds(micro, 1), :], lambda: head_taps(lines, pair), keep, padded, blended, result.at[0])
-
-    def between(at):
-        if at < len(steps):
-            steps[at]()
+    back = return_rows(at, piece, result, mixed_rows, send_two, receive_two)
+    phases = attend(slab, lambda: edges[pl.ds(at.micro, 1), :], lambda: head_taps(lines, at.pair), keep, padded, blended, result)
+
+    def between(turn):
+        if turn < len(steps):
+            steps[turn]()
 
     between(0)
-    for at, phase in enumerate(phases):
-
-        @pl.when(owns)
+    for turn, phase in enumerate(phases):
+
+        @pl.when(at.owns)
         def _():
-            if at == 0:
-                await_slab(count, piece, slab, receive_one)
+            if turn == 0:
+                await_slab(at, piece, slab, receive_one)
             phase()
-            if at == len(phases) - 1:
+            if turn == len(phases) - 1:
                 back(False)
 
-        if at > 1:
-            between(at - 1)
-    for at in range(len(phases) - 1, len(steps)):
-        between(at)
+        if turn > 1:
+            between(turn - 1)
+    for turn in range(len(phases) - 1, len(steps)):
+        between(turn)
     finish()
     out(True)
-    await_rows(mixed_rows, receive_two)
-
-    @pl.when(owns)
+    await_rows(at, mixed_rows, receive_two)
+
+    @pl.when(at.owns)
     def _():
         back(True)
 
 
-def backward_kernel(count, piece, grads, edges, lines, slab, *refs):
+def backward_kernel(count, piece, carries, grads, edges, lines, *refs):
+    carried, refs = refs[:carries], refs[carries:]
+    slab, refs = refs[0], refs[1:]
     keep = dict(zip(KEPT, refs))
-    out_grads, grad_taps, grad_slab, padded, padded_grads, blended, result, send_one, receive_one, send_two, receive_two = refs[len(KEPT) :]
-    me = lax.axis_index("dp")
-    task, owns = task_of(me, count)
-    greet(count)
-    out = scatter_tasks(count, piece, grads, grad_slab, send_one, receive_one)
+    out_grads, grad_taps, refs = refs[len(KEPT)], refs[len(KEPT) + 1], refs[len(KEPT) + 2 :]
+    swapped, refs = refs[:carries], refs[carries:]
+    grad_slab, padded, padded_grads, blended, result, send_one, receive_one, send_two, receive_two, send_swap, receive_swap = refs
+    at = Layout(count).place()
+    greet(at, mate=bool(carries))
+    out = scatter_tasks(at, piece, grads, grad_slab, send_one, receive_one)
     out(False)
-    back = return_rows(count, piece, result, out_grads, send_two, receive_two)
+    swaps = [swap(at, one, two, send_swap, receive_swap) for one, two in zip(carried, swapped)]
+    for one, source, target in zip(swaps, carried, swapped):
+        one.start()
+        target[pl.ds(at.group, 1)] = source[pl.ds(at.group, 1)]
+    back = return_rows(at, piece, result, out_grads, send_two, receive_two)
     grad_taps[...] = jnp.zeros(grad_taps.shape, F32)
 
-    @pl.when(owns)
+    @pl.when(at.owns)
     def _():
-        micro, pair = task // PAIRS, lax.rem(task, PAIRS)
-        await_slab(count, piece, grad_slab, receive_one)
+        await_slab(at, piece, grad_slab, receive_one)
         attend_back(
-            grad_slab[0], slab[0], slab[1], slab[2], edges[pl.ds(micro, 1), :], head_taps(lines, pair),
-            keep, padded, padded_grads, blended, result, grad_taps.at[pair],
+            whole(grad_slab, 0), whole(slab, 0), whole(slab, 1), whole(slab, 2), edges[pl.ds(at.micro, 1), :], head_taps(lines, at.pair),
+            keep, padded, padded_grads, blended, result, grad_taps.at[at.pair],
         )
         back(False)
 
     out(True)
-    await_rows(out_grads, receive_two)
-
-    @pl.when(owns)
+    await_rows(at, out_grads, receive_two)
+    for one in swaps:
+        one.wait()
+
+    @pl.when(at.owns)
     def _():
         back(True)
 
@@ -497,13 +537,15 @@
     piece = qkv.shape[2]
     length = piece * count
     shapes = kept_shapes(length)
-    low = lines if low is None else low
+    low = low if spans else lines
+    at = Layout(count)
+    halved = (at.groups, length // at.groups, LANES)
     anywhere = pl.BlockSpec(memory_space=pl.ANY)
     results = pl.pallas_call(
         functools.partial(forward_kernel, count, piece, spans),
         out_shape=[
             jax.ShapeDtypeStruct((1, MICRO, piece, D), BF16),
-            jax.ShapeDtypeStruct((3, length, LANES), BF16),
+            jax.ShapeDtypeStruct((3,) + halved, BF16),
         ]
         + [jax.ShapeDtypeStruct(shapes[name], F32) for name in KEPT]
         + [spread_shape(low, span) for span in spans],
@@ -512,11 +554,11 @@
         scratch_shapes=[
             pltpu.VMEM((length + LANES, LANES), BF16),
             pltpu.VMEM((length, LANES), F32),
-            pltpu.VMEM((1, length, LANES), BF16),
-            DMA((TASKS,)),
-            DMA((count,)),
-            DMA((count,)),
-            DMA((TASKS,)),
+            pltpu.VMEM((1,) + halved, BF16),
+            DMA((at.tasks,)),
+            DMA((at.members,)),
+            DMA((at.members,)),
+            DMA((at.tasks,)),
         ]
         + [one for span in spans for one in spread_semaphores(span)],
         compiler_params=pltpu.CompilerParams(collective_id=ident, has_side_effects=True, vmem_limit_bytes=60 << 20),
@@ -525,31 +567,37 @@
     return results[0][0], results[1 : 2 + len(KEPT)], [flat_rows(one) for one in results[2 + len(KEPT) :]]
 
 
-def attention_backward(count, grads, edges, lines, kept, ident):
+def attention_backward(count, grads, edges, lines, kept, ident, carried=()):
     piece = grads.shape[2]
     length = piece * count
-    return pl.pallas_call(
-        functools.partial(backward_kernel, count, piece),
+    at = Layout(count)
+    halved = (at.groups, length // at.groups, LANES)
+    results = pl.pallas_call(
+        functools.partial(backward_kernel, count, piece, len(carried)),
         out_shape=[
             jax.ShapeDtypeStruct((3, MICRO, piece, D), BF16),
             jax.ShapeDtypeStruct((PAIRS, 2, 2 * LANES), F32),
-        ],
-        in_specs=[VMEM] * (4 + len(KEPT)),
-        out_specs=[VMEM] * 2,
+        ]
+        + [jax.ShapeDtypeStruct(one.shape, one.dtype) for one in carried],
+        in_specs=[VMEM] * (4 + len(carried) + len(KEPT)),
+        out_specs=[VMEM] * (2 + len(carried)),
         scratch_shapes=[
-            pltpu.VMEM((1, length, LANES), BF16),
+            pltpu.VMEM((1,) + halved, BF16),
             pltpu.VMEM((length + LANES, LANES), BF16),
             pltpu.VMEM((length + LANES, LANES), BF16),
             pltpu.VMEM((length, LANES), F32),
-            pltpu.VMEM((3, length, LANES), BF16),
-            DMA((TASKS,)),
-            DMA((count,)),
-            DMA((count,)),
-            DMA((TASKS,)),
+            pltpu.VMEM((3,) + halved, BF16),
+            DMA((at.tasks,)),
+            DMA((at.members,)),
+            DMA((at.members,)),
+            DMA((at.tasks,)),
+            DMA,
+            DMA,
         ],
         compiler_params=pltpu.CompilerParams(collective_id=ident, has_side_effects=True, vmem_limit_bytes=60 << 20),
         name="attend_backward",
-    )(grads, edges, lines, *kept)
+    )(grads, edges, lines, *carried, *kept)
+    return results[0], results[1], results[2:]
 
 
 def arrange(sources, targets):
@@ -590,16 +638,20 @@
 
 
 PLANES = 4
-
-
-def gather_kernel(spans, low, params, first, second, *refs):
+SUBS = 2
+EVEN, ODD = range(0, SUBS, 2), range(1, SUBS, 2)
+
+
+def gather_kernel(spans, low, params, first, second, hidden, cotangent, *refs):
     outs, refs = refs[: len(spans)], refs[len(spans) :]
     targets, refs = refs[: len(ARRANGED)], refs[len(ARRANGED) :]
+    swapped, swap_sems, refs = refs[:2], refs[2], refs[3:]
     begin, steps, finish = spread_all(spans, low, outs, refs)
+    at = Layout(16).place()
     me, x = lax.axis_index("dp"), lax.axis_index("rep")
     core, y, z = lax.rem(me, 2), lax.rem(me // 2, 2), me // 4
     barrier = pltpu.get_barrier_semaphore()
-    for where in ({"rep": 1 - x}, {"dp": me + 2 - 4 * y}, {"dp": me + 1 - 2 * core}):
+    for where in ({"rep": 1 - x}, {"dp": me + 2 - 4 * y}, {"dp": me + 1 - 2 * core}, at.mate()):
         pl.semaphore_signal(barrier, inc=1, device_id=where, device_id_type=MESH)
     for sign in (1, -1):
 
@@ -607,17 +659,23 @@
         def _():
             pl.semaphore_signal(barrier, inc=1, device_id={"dp": me + 4 * sign}, device_id_type=MESH)
 
-    pl.semaphore_wait(barrier, 4 + jnp.where((z > 0) & (z < PLANES - 1), 1, 0))
+    pl.semaphore_wait(barrier, 5 + jnp.where((z > 0) & (z < PLANES - 1), 1, 0))
     begin()
+    swaps = [swap(at, one, two, swap_sems.at[0, which], swap_sems.at[1, which]) for which, (one, two) in enumerate(zip((hidden, cotangent), swapped))]
+    for one, source, target in zip(swaps, (hidden, cotangent), swapped):
+        one.start()
+        target[pl.ds(at.group, 1)] = source[pl.ds(at.group, 1)]
     arrange((params, first, second), targets)
     for step in steps:
         step()
     finish()
+    for one in swaps:
+        one.wait()
 
 
 def spread_semaphores(span):
     planes = span[2] - span[1]
-    return [DMA, DMA((planes, 2, 2)), DMA((planes, 2))] + [DMA((planes, 2, 2, 2))] * 5 + [DMA]
+    return [DMA, DMA((planes, SUBS, 2)), DMA((planes, SUBS))] + [DMA((planes, 2, 2, SUBS))] * 5 + [DMA]
 
 
 def spread_shape(low, span):
@@ -651,7 +709,7 @@
     x = lax.axis_index("rep")
     core, y, z = lax.rem(me, 2), lax.rem(me // 2, 2), me // 4
     half = shard.shape[0] // 2
-    part = half // 2
+    part = half // SUBS
 
     def held(plane):
         return (plane >= bottom) & (plane < top)
@@ -696,12 +754,12 @@
         @pl.when(held(z))
         def _():
             pltpu.make_async_copy(shard, out.at[z - bottom, y, core], local_sem).start()
-            for sub in range(2):
+            for sub in range(SUBS):
                 for sign in (1, -1):
                     inside(sign, lambda: climb(z, sub, sign, shard.at[rows(x, sub), :]).start())
                 move("y", z, y, x, sub, shard.at[rows(x, sub), :]).start()
             for side in range(2):
-                for sub in range(2):
+                for sub in range(SUBS):
                     move("core", z, y, side, sub, shard.at[rows(side, sub), :]).start()
 
     def at_distance(distance, act):
@@ -713,7 +771,7 @@
                 act(plane, sign)
 
     def from_z(plane, sign):
-        for sub in range(2):
+        for sub in range(SUBS):
             climb(plane, sub, sign).wait_recv()
             inside(sign, lambda: climb(plane, sub, sign).start())
             for axis in ("x", "y", "core"):
@@ -726,25 +784,27 @@
         move("core", plane, row, side, sub).start()
 
     def first_square(plane, sign):
-        take("x", plane, y, 1 - x, 0, "y")
-        take("y", plane, 1 - y, x, 1, "x")
-        take("y", plane, 1 - y, x, 0)
-        take("x", plane, y, 1 - x, 1)
+        for even, odd in zip(EVEN, ODD):
+            take("x", plane, y, 1 - x, even, "y")
+            take("y", plane, 1 - y, x, odd, "x")
+            take("y", plane, 1 - y, x, even)
+            take("x", plane, y, 1 - x, odd)
 
     def second_square(plane, sign):
-        take("y", plane, 1 - y, 1 - x, 0)
-        take("x", plane, 1 - y, 1 - x, 1)
+        for even, odd in zip(EVEN, ODD):
+            take("y", plane, 1 - y, 1 - x, even)
+            take("x", plane, 1 - y, 1 - x, odd)
 
     def own_first():
         @pl.when(held(z))
         def _():
-            for sub in range(2):
+            for sub in range(SUBS):
                 take("y", z, 1 - y, x, sub, "x")
 
     def own_last():
         @pl.when(held(z))
         def _():
-            for sub in range(2):
+            for sub in range(SUBS):
                 take("x", z, 1 - y, 1 - x, sub)
 
     def stage(distance, act):
@@ -756,12 +816,13 @@
     ]
 
     def sent(plane, sign):
-        for sub in range(2):
+        for sub in range(SUBS):
             inside(sign, lambda: climb(plane, sub, sign).wait_send())
             move("x", plane, y, x, sub).wait_send()
             move("y", plane, y, x, sub).wait_send()
-        move("y", plane, y, 1 - x, 0).wait_send()
-        move("x", plane, 1 - y, x, 1).wait_send()
+        for even, odd in zip(EVEN, ODD):
+            move("y", plane, y, 1 - x, even).wait_send()
+            move("x", plane, 1 - y, x, odd).wait_send()
 
     def finish():
         for distance in (1, 2, 3):
@@ -770,35 +831,36 @@
         @pl.when(held(z))
         def _():
             pltpu.make_async_copy(shard, out.at[z - bottom, y, core], local_sem).wait()
-            for sub in range(2):
+            for sub in range(SUBS):
                 for sign in (1, -1):
                     inside(sign, lambda: climb(z, sub, sign).wait_send())
                 move("y", z, y, x, sub).wait_send()
                 move("x", z, 1 - y, x, sub).wait_send()
 
         def core_sent(index, carry):
-            plane, row, side, sub = bottom + index // 8, lax.rem(index // 4, 2), lax.rem(index // 2, 2), lax.rem(index, 2)
+            plane, row = bottom + index // (4 * SUBS), lax.rem(index // (2 * SUBS), 2)
+            side, sub = lax.rem(index // SUBS, 2), lax.rem(index, SUBS)
             move("core", plane, row, side, sub).wait_send()
             return carry
 
-        lax.fori_loop(0, 8 * (top - bottom), core_sent, 0)
+        lax.fori_loop(0, 4 * SUBS * (top - bottom), core_sent, 0)
         column = out.at[:, :, 1 - core]
         pltpu.make_async_copy(column, column, core_got).wait()
 
     return begin, steps, finish
 
 
-def gather(low, spans, *smalls):
+def gather(low, spans, hidden, cotangent, *smalls):
     results = pl.pallas_call(
         functools.partial(gather_kernel, spans),
-        out_shape=[spread_shape(low, span) for span in spans] + ARRANGED,
-        in_specs=[VMEM] * 4,
-        out_specs=[pl.BlockSpec(memory_space=pl.ANY)] * len(spans) + [VMEM] * len(ARRANGED),
-        scratch_shapes=[one for span in spans for one in spread_semaphores(span)],
+        out_shape=[spread_shape(low, span) for span in spans] + ARRANGED + [jax.ShapeDtypeStruct(hidden.shape, BF16)] * 2,
+        in_specs=[VMEM] * 6,
+        out_specs=[pl.BlockSpec(memory_space=pl.ANY)] * len(spans) + [VMEM] * (len(ARRANGED) + 2),
+        scratch_shapes=[DMA((2, 2))] + [one for span in spans for one in spread_semaphores(span)],
         compiler_params=pltpu.CompilerParams(collective_id=4, has_side_effects=True),
         name="gather",
-    )(low, *smalls)
-    return [flat_rows(one) for one in results[: len(spans)]], results[len(spans) :]
+    )(low, *smalls, hidden, cotangent)
+    return [flat_rows(one) for one in results[: len(spans)]], results[len(spans) : -2], results[-2:]
 
 
 CHUNK = 32
@@ -816,9 +878,9 @@
     count = len(MATES)
     mates = [dict(zip(MATES, refs[level * count : (level + 1) * count])) for level in range(LAYERS)]
     (
-        weights, first, second, small_first, small_second, grad_out, mean_out, small_out,
+        weights, first, second, small_first, small_second, grad_in, grad_out, mean_out, small_out, grad_in_out,
         turned, right, staged, own, got_core, got_y, got_z, inner, step_own, step_got, small, small_got, small_own, small_step, small_step_got,
-        core_send, core_got, y_send, y_got, z_send, z_got, inner_sem, rep_send, rep_got, small_send, small_sem, back_send, back_sem, small_rep,
+        core_send, core_got, y_send, y_got, z_send, z_got, inner_sem, rep_send, rep_got, small_send, small_sem, back_send, back_sem, small_rep, swap_sems,
     ) = refs[LAYERS * count :]
     me = lax.axis_index("dp")
     other_rep = 1 - lax.axis_index("rep")
@@ -886,6 +948,11 @@
 
     pl.semaphore_wait(barrier, devices)
 
+    at_layout = Layout(16).place()
+    swapping = swap(at_layout, grad_in, grad_in_out, swap_sems.at[0], swap_sems.at[1])
+    swapping.start()
+    grad_in_out[pl.ds(at_layout.group, 1)] = grad_in[pl.ds(at_layout.group, 1)]
+
     def small_copy(step):
         peer = lax.rem(me + step, devices)
         return to_dp(small.at[peer], small_got.at[me], small_send.at[peer], small_sem.at[me], peer)
@@ -1032,9 +1099,10 @@
 
     lax.fori_loop(1, devices, small_drain, 0)
     small_rep_copy().wait_send()
-
-
-def settle(mates, weights, first, second, small_first, small_second):
+    swapping.wait()
+
+
+def settle(mates, weights, first, second, small_first, small_second, grad_in):
     block_rows = weights.shape[1]
     anywhere = pl.BlockSpec(memory_space=pl.ANY)
     devices = 16
@@ -1046,9 +1114,10 @@
             jax.ShapeDtypeStruct(weights.shape, F32),
             jax.ShapeDtypeStruct(weights.shape, F32),
             jax.ShapeDtypeStruct((devices, 2, 2, D), F32),
+            jax.ShapeDtypeStruct(grad_in.shape, F32),
         ],
-        in_specs=[VMEM] * (LAYERS * len(MATES)) + [anywhere] * 3 + [VMEM] * 2,
-        out_specs=[VMEM] * 3,
+        in_specs=[VMEM] * (LAYERS * len(MATES)) + [anywhere] * 3 + [VMEM] * 3,
+        out_specs=[VMEM] * 4,
         scratch_shapes=[
             pltpu.VMEM((LAYERS * 2 * (D + FF), tokens), BF16),
             pltpu.VMEM((LAYERS * 6, tokens, D), BF16),
@@ -1079,10 +1148,11 @@
             DMA((devices,)),
             DMA((devices,)),
             DMA((2,)),
+            DMA((2,)),
         ],
         compiler_params=pltpu.CompilerParams(collective_id=3, has_side_effects=True, vmem_limit_bytes=63 << 20),
         name="settle",
-    )(*[mate[name] for mate in mates for name in MATES], weights, first, second, small_first, small_second)
+    )(*[mate[name] for mate in mates for name in MATES], weights, first, second, small_first, small_second, grad_in)
 
 
 def finish_kernel(both, params, outer, first, second, first_new, second_new, outer_new, params_new, grad, mean):
@@ -1150,7 +1220,6 @@
     value = (dense(low_in, proj[2]) + lines[1:2]).astype(BF16)
     qkv = jnp.stack([query, key, value])
     low_comb, kept, fetched = attention_forward(count, qkv.reshape(3, MICRO, piece, D), edges, lines, ident, low, spans)
-    rest = fetched[0] if fetched else rest
     out_weight, up_weight, down_weight = split_rows(rest)
     low_comb = low_comb.reshape(MICRO * piece, D)
     resid_one = inputs + (dense(low_comb, out_weight) + lines[2:3])
@@ -1160,10 +1229,10 @@
     low_act = jax.nn.gelu(upward).astype(BF16)
     resid_two = hidden_one + (dense(low_act, down_weight) + lines[3:4])
     output = layer_norm(resid_two, lines[6:7], lines[7:8])
-    return output, (proj, rest, low_in, kept, low_comb, resid_one, low_hidden, upward, low_act, resid_two), fetched[1:]
-
-
-def backward_layer(count, grad_output, small, edges, state, ident):
+    return output, (proj, rest, low_in, kept, low_comb, resid_one, low_hidden, upward, low_act, resid_two), fetched
+
+
+def backward_layer(count, grad_output, small, edges, state, ident, carried=()):
     proj, rest, low_in, kept, low_comb, resid_one, low_hidden, upward, low_act, resid_two = state
     total = low_in.shape[0]
     piece = total // MICRO
@@ -1178,12 +1247,12 @@
     grad_one, grad_gain_one, grad_shift_one = layer_norm_back(resid_one, lines[4:5], grad_hidden)
     low_branch = grad_one.astype(BF16)
     grad_comb = dense(low_branch, out_weight, NT).astype(BF16)
-    low_grads, grad_taps = attention_backward(count, grad_comb.reshape(1, MICRO, piece, D), edges, lines, kept, ident)
+    low_grads, grad_taps, swapped = attention_backward(count, grad_comb.reshape(1, MICRO, piece, D), edges, lines, kept, ident, carried)
     low_grads = low_grads.reshape(3, total, D)
     grad_in = grad_one + sum(dense(low_grads[part], proj[part], NT) for part in range(3))
     vectors = (grad_gain_one, grad_shift_one, grad_gain_two, grad_shift_two)
     values = (low_in, low_comb, low_up, low_act, low_grads, low_branch, low_hidden, low_down, *vectors, grad_taps)
-    return grad_in, dict(zip(MATES, values))
+    return grad_in, dict(zip(MATES, values)), swapped
 
 
 def plain_grads(mate):
@@ -1227,29 +1296,43 @@
     low_weights = weights.astype(BF16)
     limits = bounds[0, :, 0, :]
     edges = jnp.pad(limits.astype(F32), ((0, 0), (0, LANES - limits.shape[1])))
-    positions = lax.axis_index("dp") * piece + lax.broadcasted_iota(jnp.int32, (MICRO, piece, 1), 1)
-    valid = positions < limits[:, -1].reshape(MICRO, 1, 1)
-    activation = hidden[0, :, 0].reshape(total, D).astype(F32)
-    states = [None] * LAYERS
+    own_hidden, own_cotangent = hidden[0, :, 0], cotangent[0, :, 0]
+    me = lax.axis_index("dp")
+    start, last = me * piece, limits[:, -1].reshape(MICRO, 1, 1)
     if count == 16:
-        (proj,), prepared = gather(low_weights, ((0, 0, 1),), small_params, first_small[0], second_small[0])
+        (rows,), prepared, (own_hidden, own_cotangent) = gather(
+            low_weights, ((0, 0, PLANES),), own_hidden, own_cotangent, small_params, first_small[0], second_small[0]
+        )
+        half = count // MICRO
+        start = (lax.broadcasted_iota(jnp.int32, (MICRO, 1, 1), 0) * half + lax.rem(me, half)) * piece
+        last = jnp.where(me < half, limits[0, -1], limits[1, -1])
     else:
         prepared = arranged(small_params, first_small[0], second_small[0])
+    positions = start + lax.broadcasted_iota(jnp.int32, (MICRO, piece, 1), 1)
+    valid = positions < last
+    activation = own_hidden.reshape(total, D).astype(F32)
+    states = [None] * LAYERS
     smalls = [(prepared[level], prepared[LAYERS + level]) for level in range(LAYERS)]
     for level in range(LAYERS):
         if count == 16:
-            spans = ((level, 1, PLANES),) + (((level + 1, 0, 1),) if level + 1 < LAYERS else ())
-            activation, states[level], more = forward_layer(count, activation, proj, None, smalls[level], edges, 1 + 4 * level, low_weights, spans)
-            proj = more[0] if more else None
+            spans = ((level + 1, 0, PLANES),) if level + 1 < LAYERS else ()
+            activation, states[level], more = forward_layer(
+                count, activation, rows[: 3 * D], rows[3 * D :], smalls[level], edges, 1 + 4 * level, low_weights, spans
+            )
+            rows = more[0] if more else None
         else:
             rows = lax.all_gather(low_weights[level], "dp", axis=0, tiled=True)
             activation, states[level], _ = forward_layer(count, activation, rows[: 3 * D], rows[3 * D :], smalls[level], edges, 1)
-    gradient = jnp.where(valid, cotangent[0, :, 0].astype(F32), 0.0).reshape(total, D)
+    gradient = jnp.where(valid, own_cotangent.astype(F32), 0.0).reshape(total, D)
     mates = [None] * LAYERS
     for level in reversed(range(LAYERS)):
-        gradient, mates[level] = backward_layer(count, gradient, smalls[level], edges, states[level], 2)
+        carried = (activation.reshape(MICRO, piece, D),) if count == 16 and level == LAYERS - 1 else ()
+        gradient, mates[level], swapped = backward_layer(count, gradient, smalls[level], edges, states[level], 2 + 4 * level, carried)
+        activation = swapped[0] if carried else activation
     if count == 16:
-        grad_big, mean_big, small_both = settle(mates, weights, first_big[0], second_big[0], *prepared[2 * LAYERS :])
+        grad_big, mean_big, small_both, gradient = settle(
+            mates, weights, first_big[0], second_big[0], *prepared[2 * LAYERS :], gradient.reshape(MICRO, piece, D)
+        )
         new_smalls = finish(small_both, small_params, outer_small, first_small[0], second_small[0])
     else:
         rows, sums = zip(*[plain_grads(mate) for mate in mates])

time: 559 us -> 530 us (0.948)
  Pallas kernels: 466 us -> 423 us
  local copies, waits for them, and re-layouts: 5.91 us -> 30.5 us
  matrix products: 52.6 us -> 39.3 us
    pallas_call x2, Pallas kernels: 176 us -> 105 us  [attention_forward(): pl.pallas_call(functools.partial(forward_kernel, count, piece, spans), ou...]
    pallas_call x1, Pallas kernels: 25.6 us -> 70.8 us  [gather(): pl.pallas_call(functools.partial(gather_kernel, spans), out_shape=[spread...]
    slice x1 -> x5, local copies, waits for them, and re-layouts: 0.18 us -> 18.6 us  [the longest x2 14.8 us: shards(): rows[3 * D:]]
    pallas_call x2, Pallas kernels: 77.4 us -> 62.8 us  [attention_backward(): pl.pallas_call(functools.partial(backward_kernel, count, piece, len(carri...]
    dot_general x24, matrix products: 52.6 us -> 39.3 us  [mm(): return lax.dot_general(a, b, dims, preferred_element_type=F32)]
where the time goes in v7:
time: 530 us; the launch traced here: 523 us
  Pallas kernels  423 us (80%)
  matrix products  39.3 us (7%)
  local copies, waits for them, and re-layouts  30.5 us (6%)
  other arithmetic  27.3 us (5%)
    pallas_call x1, Pallas kernels, settle(): pl.pallas_call(functools.partial(settle_kernel, block_rows), out_shape=[j...  183 us
    pallas_call x2, Pallas kernels, attention_forward(): pl.pallas_call(functools.partial(forward_kernel, count, piece, spans), ou...  105 us
    pallas_call x1, Pallas kernels, gather(): pl.pallas_call(functools.partial(gather_kernel, spans), out_shape=[spread...  70.8 us
    pallas_call x2, Pallas kernels, attention_backward(): pl.pallas_call(functools.partial(backward_kernel, count, piece, len(carri...  62.8 us
    dot_general x24, matrix products, mm(): return lax.dot_general(a, b, dims, preferred_element_type=F32)  39.3 us
    slice x2, local copies, waits for them, and re-layouts, shards(): rows[3 * D:]  14.8 us

profile of v7, /device:TPU:0, one launch (start us, length us, event | category | flops | bytes accessed | tf_op | source)
XLA Modules:
  0.0 523.0 jit_solution(7879288717691483899)
XLA Ops:
  0.7 0.7 convert_element_type.80
  1.9 1.3 fusion.84
  4.6 3.4 convert_element_type.75.low
  8.0 70.8 %gather.1 = (bf16[4,2,2,576,768]{4,3,2,1,0:T(8,128)(2,1)}, f32[16,768]{1,0:T(8,128)}, f32[16,768]{1,0:T(8,128)}, f32[1,3072]{1,0:T(1,128)}, f32[1,3072]{1,0:T(1,...) custom-call(bf16[2,576,768]{2,1,0:T(8,128)(2,1)} %convert_element_ty, ...), custom_call_target="tpu_custom_call" | custom-call | tf_op jit(solution)/shard_map/gather/pallas_call | solution.py:854
  78.8 2.2 slice_reduce_fusion
  81.6 1.1 multiply_reduce_fusion.4
  82.7 0.7 div.67
  84.1 2.2 slice.150
  86.3 9.3 %slice.156 = bf16[3,2,2,576,768]{4,3,2,1,0:T(8,128)(2,1)} slice(bf16[4,2,2,576,768]{4,3,2,1,0:T(8,128)(2,1)} %get-tuple-element.63), slice={[1:4], [0:2], [0:2], [0:576], [0:768]} | slice | bytes 21233664 | tf_op jit(solution)/shard_map/slice | solution.py:1320
  96.6 0.9 pad_maximum_fusion.qkv
  97.5 77.6 %attend_forward.2 = (bf16[1,2,64,768]{3,2,1,0:T(8,128)(2,1)}, bf16[3,2,512,128]{3,2,1,0:T(8,128)(2,1)}, f32[128,128]{1,0:T(8,128)}, f32[128,128]{1,0:T(8,128)}, ...) custom-call(bf16[3,2,64,768]{3,2,1,0:T(8,128)(2,1)} %pad_maximum_fus, ...), custom_call_target="tpu_custom_call" | custom-call | tf_op jit(solution)/shard_map/attend_forward/pallas_call | solution.py:544
  175.1 1.8 fusion.85
  177.4 5.4 %multiply_convert_fusion.1 = (bf16[128,3072]{1,0:T(8,128)(2,1)S(1)}, f32[128,3072]{1,0:T(8,128)}) fusion(f32[3072]{0:T(1024)S(1)} %bitcast.194, bf16[128,768]{1,0:T(8,128)(2,1)S(1)} %fusion.74.refs_6_, bf16[6912,768]{1,0:T(8,128)(2,1)} %bitcast.140), kind=kOutput, calls=%fused_computation.43 | convolution fusion | flops 607911936 | bytes 7286784 | tf_op jit(solution)/shard_map/dot_general | solution.py:48
  182.8 4.2 fusion.86
  188.6 5.5 %slice.173 = bf16[3,2,2,576,768]{4,3,2,1,0:T(8,128)(2,1)} slice(bf16[4,2,2,576,768]{4,3,2,1,0:T(8,128)(2,1)S(1)} %copy-done.2), slice={[1:4], [0:2], [0:2], [0:576], [0:768]} | slice | bytes 21233664 | tf_op jit(solution)/shard_map/slice | solution.py:1320
  195.5 0.9 pad_maximum_fusion.1.qkv
  196.4 27.0 %attend_forward.3 = (bf16[1,2,64,768]{3,2,1,0:T(8,128)(2,1)}, bf16[3,2,512,128]{3,2,1,0:T(8,128)(2,1)}, f32[128,128]{1,0:T(8,128)}, f32[128,128]{1,0:T(8,128)}, ...) custom-call(bf16[3,2,64,768]{3,2,1,0:T(8,128)(2,1)} %pad_maximum_fus, ...), custom_call_target="tpu_custom_call" | custom-call | tf_op jit(solution)/shard_map/attend_forward/pallas_call | solution.py:544
  223.4 1.8 fusion.87
  225.7 4.2 multiply_convert_fusion
  229.9 1.3 copy-done.3
  231.2 0.9 fusion.88
  232.6 0.7 bitcast_reduce_fusion.refs_23_
  233.3 1.0 fusion.81
  234.3 2.1 fusion.37.refs_15_
  236.4 0.9 multiply_reduce_fusion.11
  237.4 0.7 bitcast_reduce_fusion.1
  238.1 0.9 fusion.80
  239.0 1.2 convolution_convert_fusion.1
  240.2 32.1 %attend_backward.2 = (bf16[3,2,64,768]{3,2,1,0:T(8,128)(2,1)}, f32[6,2,256]{2,1,0:T(2,128)}, f32[2,64,768]{2,1,0:T(8,128)}) custom-call(bf16[1,2,64,768]{3,2,1,0:T(8,128)(2,1)} %bitcast.179, f32[2,128]{1,0:T(2,128)} %pad.4.edges, f32[16,768]{1,0:T(8,128)} %get-tuple-element.68.lines.low, f32[2,64,768]{2,1,0:T(8,128)} %bitcast.156, ...), custom_call_target="tpu_custom_call" | custom-call | tf_op jit(solution)/shard_map/attend_backward/pallas_call | solution.py:575
  272.3 1.2 fusion.83
  273.5 1.8 fusion.69
  275.4 2.0 convolution_add_fusion.3
  277.4 1.9 multiply_reduce_fusion.10
  279.3 0.7 bitcast_reduce_fusion.3
  280.7 4.7 fusion.30.refs_2_
  285.5 0.9 multiply_reduce_fusion.9
  286.4 0.7 bitcast_reduce_fusion.5
  287.4 1.2 convolution_convert_fusion
  288.6 30.8 %attend_backward.3 = (bf16[3,2,64,768]{3,2,1,0:T(8,128)(2,1)}, f32[6,2,256]{2,1,0:T(2,128)}) custom-call(bf16[1,2,64,768]{3,2,1,0:T(8,128)(2,1)} %bitcast.180, f32[2,128]{1,0:T(2,128)} %pad.4.edges, f32[16,768]{1,0:T(8,128)} %get-tuple-element.64.lines, bf16[3,2,512,128]{3,2,1,0:T(8,128)(2,1)} %get-tuple-element.87.refs_0_, ...), custom_call_target="tpu_custom_call" | custom-call | tf_op jit(solution)/shard_map/attend_backward/pallas_call | solution.py:575
  319.4 1.2 fusion.82
  321.6 1.3 fusion.45
  322.9 182.6 %settle.1 = (f32[2,576,768]{2,1,0:T(8,128)}, f32[2,576,768]{2,1,0:T(8,128)}, f32[16,2,2,768]{3,2,1,0:T(2,128)}, f32[2,64,768]{2,1,0:T(8,128)}) custom-call(bf16[128,768]{1,0:T(8,128)(2,1)} %bitcast.170, bf16[128,768]{1,0:T(8,128)(2,1)} %bitcast.176, bf16[128,3072]{1,0:T(8,128)(2,1)} %copy-done.21, bf16[128,3072]{1,0:T(8,128)(2,1)} %copy-done.18, ...), custom_call_target="tpu_custom_call" | custom-call | tf_op jit(solution)/shard_map/settle/pallas_call | solution.py:1111
  505.5 1.8 finish.1
  507.4 8.7 %fusion.23 = (f32[1,2,576,768]{3,2,1,0:T(8,128)}, f32[1,2,576,768]{3,2,1,0:T(8,128)}) fusion(f32[2,576,768]{2,1,0:T(8,128)} %get-tuple-element.106, f32[1,2,576,768]{3,2,1,0:T(8,128)} %param.17, f32[1,2,576,768]{3,2,1,0:T(8,128)} %param.16), kind=kLoop, calls=%fused_computation.20 | loop fusion | flops 6193152 | bytes 17694720 | tf_op jit(solution)/shard_map/broadcast_in_dim | solution.py:1357
  516.1 0.7 copy-done.9
  516.8 4.4 fusion.77
  521.2 0.7 copy.26
  522.0 0.7 copy.27
  (158 shorter events, 9.0 us)
Async XLA Ops:
  81.0 96.2 %copy-start.30 = (f32[768]{0:T(1024)}, f32[768]{0:T(1024)S(1)}, u32[]{:S(2)}) copy-start(f32[768]{0:T(1024)S(1)} %get-tuple-element.194) | copy-start | bytes 9220
  81.0 96.2 %copy-start.37 = (f32[768]{0:T(1024)}, f32[768]{0:T(1024)S(1)}, u32[]{:S(2)}) copy-start(f32[768]{0:T(1024)S(1)} %get-tuple-element.195) | copy-start | bytes 9220
  86.3 9.3 %copy-start.24 = (bf16[2,64,768]{2,1,0:T(8,128)(2,1)S(1)}, bf16[2,64,768]{2,1,0:T(8,128)(2,1)}, u32[]{:S(2)}) copy-start(bf16[2,64,768]{2,1,0:T(8,128)(2,1)} %get-tuple-element.62) | copy-start | bytes 589828
  175.1 2.2 copy-start.55
  176.9 5.8 %copy-start.6 = (f32[128,768]{1,0:T(8,128)}, f32[128,768]{1,0:T(8,128)S(1)}, u32[]{:S(2)}) copy-start(f32[128,768]{1,0:T(8,128)S(1)} %get-tuple-element.177) | copy-start | bytes 1179652
  177.0 5.8 %copy-start.41 = (f32[128]{0:T(128)}, f32[128]{0:T(128)S(1)}, u32[]{:S(2)}) copy-start(f32[128]{0:T(128)S(1)} %broadcast_multiply_fusion.11) | copy-start | bytes 1540
  177.2 5.6 %copy-start.46 = (f32[128]{0:T(128)}, f32[128]{0:T(128)S(1)}, u32[]{:S(2)}) copy-start(f32[128]{0:T(128)S(1)} %add_rsqrt_fusion.3) | copy-start | bytes 1540
  177.2 5.6 %copy-start.52 = (f32[768]{0:T(1024)S(1)}, f32[768]{0:T(1024)}, u32[]{:S(2)}) copy-start(f32[768]{0:T(1024)} %get-tuple-element.196) | copy-start | bytes 9220
  177.4 5.4 %copy-start.11 = (bf16[128,768]{1,0:T(8,128)(2,1)}, bf16[128,768]{1,0:T(8,128)(2,1)S(1)}, u32[]{:S(2)}) copy-start(bf16[128,768]{1,0:T(8,128)(2,1)S(1)} %fusion.74.refs_6_) | copy-start | bytes 589828
  177.4 10.9 %copy-start.2 = (bf16[4,2,2,576,768]{4,3,2,1,0:T(8,128)(2,1)S(1)}, bf16[4,2,2,576,768]{4,3,2,1,0:T(8,128)(2,1)}, u32[]{:S(2)}) copy-start(bf16[4,2,2,576,768]{4,3,2,1,0:T(8,128)(2,1)} %get-tuple-element.67) | copy-start | bytes 42467332
  182.7 4.2 copy-start.18
  182.8 5.4 %copy-start.25 = (f32[768]{0:T(1024)S(1)}, f32[768]{0:T(1024)}, u32[]{:S(2)}) copy-start(f32[768]{0:T(1024)} %get-tuple-element.198) | copy-start | bytes 9220
  182.8 5.4 %copy-start.35 = (f32[768]{0:T(1024)S(1)}, f32[768]{0:T(1024)}, u32[]{:S(2)}) copy-start(f32[768]{0:T(1024)} %get-tuple-element.197) | copy-start | bytes 9220
  188.3 6.8 %copy-start.12 = (bf16[128,768]{1,0:T(8,128)(2,1)}, bf16[128,768]{1,0:T(8,128)(2,1)S(1)}, u32[]{:S(2)}) copy-start(bf16[128,768]{1,0:T(8,128)(2,1)S(1)} %fusion.75.refs_13_) | copy-start | bytes 589828
  188.6 6.5 %copy-start.1 = (bf16[1,2,2,576,768]{4,3,2,1,0:T(8,128)(2,1)}, bf16[1,2,2,576,768]{4,3,2,1,0:T(8,128)(2,1)S(1)}, u32[]{:S(2)}) copy-start(bf16[1,2,2,576,768]{4,3,2,1,0:T(8,128)(2,1)S(1)} %slice.167) | copy-start | bytes 10616836
  188.6 5.5 %copy-start.51 = (f32[768]{0:T(1024)S(1)}, f32[768]{0:T(1024)}, u32[]{:S(2)}) copy-start(f32[768]{0:T(1024)} %get-tuple-element.142) | copy-start | bytes 9220
  195.4 27.9 %copy-start.26 = (f32[768]{0:T(1024)S(1)}, f32[768]{0:T(1024)}, u32[]{:S(2)}) copy-start(f32[768]{0:T(1024)} %get-tuple-element.198) | copy-start | bytes 9220
  195.5 27.9 %copy-start.36 = (f32[768]{0:T(1024)S(1)}, f32[768]{0:T(1024)}, u32[]{:S(2)}) copy-start(f32[768]{0:T(1024)} %get-tuple-element.197) | copy-start | bytes 9220
  195.5 27.9 %copy-start.39 = (f32[128]{0:T(128)S(1)}, f32[128]{0:T(128)}, u32[]{:S(2)}) copy-start(f32[128]{0:T(128)} %copy-done.38) | copy-start | bytes 1540
  195.5 27.9 %copy-start.44 = (f32[128]{0:T(128)S(1)}, f32[128]{0:T(128)}, u32[]{:S(2)}) copy-start(f32[128]{0:T(128)} %copy-done.43) | copy-start | bytes 1540
  195.5 27.9 %copy-start.49 = (f32[768]{0:T(1024)S(1)}, f32[768]{0:T(1024)}, u32[]{:S(2)}) copy-start(f32[768]{0:T(1024)} %get-tuple-element.141) | copy-start | bytes 9220
  223.4 2.1 copy-start.32
  223.4 2.1 copy-start.34
  223.4 2.2 copy-start.54
  225.5 5.7 %copy-start.3 = (bf16[3,2,2,576,768]{4,3,2,1,0:T(8,128)(2,1)S(1)}, bf16[3,2,2,576,768]{4,3,2,1,0:T(8,128)(2,1)}, u32[]{:S(2)}) copy-start(bf16[3,2,2,576,768]{4,3,2,1,0:T(8,128)(2,1)} %slice.173) | copy-start | bytes 31850500
  225.7 4.2 copy-start.13
  225.7 5.5 %copy-start.48 = (f32[768]{0:T(1024)S(1)}, f32[768]{0:T(1024)}, u32[]{:S(2)}) copy-start(f32[768]{0:T(1024)} %get-tuple-element.138) | copy-start | bytes 9220
  229.9 2.2 copy-start.19
  234.2 2.2 copy-start.14
  239.0 33.3 %copy-start.15 = (bf16[128,768]{1,0:T(8,128)(2,1)}, bf16[128,768]{1,0:T(8,128)(2,1)S(1)}, u32[]{:S(2)}) copy-start(bf16[128,768]{1,0:T(8,128)(2,1)S(1)} %get-tuple-element.159.refs_18_) | copy-start | bytes 589828
  273.5 3.9 copy-start.10
  273.5 3.9 copy-start.27
  273.5 3.9 copy-start.40
  273.5 3.9 copy-start.45
  275.4 10.1 %slice-start = ((s8[10616832]{0:T(1024)(128)(4,1)}), s8[4194304]{0:T(1024)(128)(4,1)S(1)}, s32[]{:S(2)}) async-start(s8[10616832]{0:T(1024)(128)(4,1)} %bitcast.143), calls=%async_computation | async-start | bytes 8388608
  280.1 5.4 %slice-start.1 = ((s8[10616832]{0:T(1024)(128)(4,1)}), s8[4194304]{0:T(1024)(128)(4,1)S(1)}, s32[]{:S(2)}) async-start(s8[10616832]{0:T(1024)(128)(4,1)} %bitcast.143), calls=%async_computation.1 | async-start | bytes 8388608
  280.2 5.2 copy-start.16
  280.7 4.7 slice-start.2
  280.7 4.7 copy-start.7
  280.7 4.7 copy-start.31
  280.7 4.8 copy-start.42
  280.7 4.8 copy-start.47
  287.3 32.0 %copy-start.17 = (bf16[128,768]{1,0:T(8,128)(2,1)}, bf16[128,768]{1,0:T(8,128)(2,1)S(1)}, u32[]{:S(2)}) copy-start(bf16[128,768]{1,0:T(8,128)(2,1)S(1)} %get-tuple-element.155.refs_5_) | copy-start | bytes 589828
  507.4 8.7 %copy-start = (f32[2,576,768]{2,1,0:T(8,128)S(1)}, f32[2,576,768]{2,1,0:T(8,128)}, u32[]{:S(2)}) copy-start(f32[2,576,768]{2,1,0:T(8,128)} %refs_26_.1) | copy-start | bytes 10616836
  507.4 8.7 %copy-start.8 = (f32[2,576,768]{2,1,0:T(8,128)S(1)}, f32[2,576,768]{2,1,0:T(8,128)}, u32[]{:S(2)}) copy-start(f32[2,576,768]{2,1,0:T(8,128)} %param.20) | copy-start | bytes 10616836
  507.4 9.4 %copy-start.9 = (f32[2,576,768]{2,1,0:T(8,128)S(1)}, f32[2,576,768]{2,1,0:T(8,128)}, u32[]{:S(2)}) copy-start(f32[2,576,768]{2,1,0:T(8,128)} %get-tuple-element.110) | copy-start | bytes 10616836
  516.8 4.4 copy-start.22
  516.8 5.2 copy-start.23
  (12 other events, 11.2 us)

commit v8 on v7

--- a/solution.py
+++ b/solution.py
@@ -864,7 +864,8 @@
 
 
 CHUNK = 32
-RING = 8
+RING = 12
+CYCLE = 6
 MATES = ("low_in", "low_comb", "low_up", "low_act", "low_grads", "low_branch", "low_hidden", "low_down", "gain_one", "shift_one", "gain_two", "shift_two", "taps")
 
 
@@ -879,8 +880,8 @@
     mates = [dict(zip(MATES, refs[level * count : (level + 1) * count])) for level in range(LAYERS)]
     (
         weights, first, second, small_first, small_second, grad_in, grad_out, mean_out, small_out, grad_in_out,
-        turned, right, staged, own, got_core, got_y, got_z, inner, step_own, step_got, small, small_got, small_own, small_step, small_step_got,
-        core_send, core_got, y_send, y_got, z_send, z_got, inner_sem, rep_send, rep_got, small_send, small_sem, back_send, back_sem, small_rep, swap_sems,
+        turned, right, staged, own, got_core, got_y, got_near, got_far, inner, step_own, step_got, small, small_got, small_own, small_step, small_step_got,
+        core_send, core_got, y_send, y_got, near_send, near_got, far_send, far_got, inner_sem, rep_send, rep_got, small_send, small_sem, back_send, back_sem, small_rep, swap_sems,
     ) = refs[LAYERS * count :]
     me = lax.axis_index("dp")
     other_rep = 1 - lax.axis_index("rep")
@@ -966,13 +967,30 @@
     def core_copy(chunk):
         return to_dp(staged.at[lax.rem(chunk, 2)], got_core.at[spot(chunk)], core_send.at[lax.rem(chunk, 2)], core_got.at[spot(chunk)], me + 1 - 2 * core)
 
-    def y_copy(chunk):
-        return to_dp(own.at[spot(chunk), :, 1 - y], got_y.at[spot(chunk)], y_send.at[spot(chunk)], y_got.at[spot(chunk)], me + 2 - 4 * y)
-
-    def z_copy(chunk, hop):
-        there = lax.rem(z + hop, 4)
+    near, far = z + 1 - 2 * lax.rem(z, 2), 3 - z
+
+    def plane_device(plane):
+        return plane * 4 + lax.rem(me, 4)
+
+    def y_copy(chunk, full):
         slot = spot(chunk)
-        return to_dp(own.at[slot, there, y], got_z.at[slot, hop - 1], z_send.at[slot, hop - 1], z_got.at[slot, hop - 1], there * 4 + lax.rem(me, 4))
+        source, target = (own.at[slot, :, 1 - y], got_y.at[slot]) if full else (own.at[slot, z, 1 - y], got_y.at[slot, 0])
+        return to_dp(source, target, y_send.at[slot], y_got.at[slot], me + 2 - 4 * y)
+
+    def near_copy(chunk, which, full):
+        slot, block = spot(chunk), 3 - near if which else near
+        source, target = (own.at[slot, block], got_near.at[slot, which]) if full else (own.at[slot, block, y], got_near.at[slot, which, 0])
+        return to_dp(source, target, near_send.at[slot, which], near_got.at[slot, which], plane_device(near))
+
+    def far_copy(chunk, full):
+        slot = spot(chunk)
+        source, target = (own.at[slot, far], got_far.at[slot]) if full else (own.at[slot, far, y], got_far.at[slot, 0])
+        return to_dp(source, target, far_send.at[slot], far_got.at[slot], plane_device(far))
+
+    def by_order(chunk, y_first, z_first):
+        turn_z = lax.rem(chunk, CYCLE) == CYCLE // 2
+        pl.when(jnp.logical_not(turn_z))(y_first)
+        pl.when(turn_z)(z_first)
 
     def place(chunk):
         return LAYERS - 1 - chunk // per_layer, pl.ds(pl.multiple_of(lax.rem(chunk, per_layer) * CHUNK, CHUNK), CHUNK)
@@ -1013,27 +1031,60 @@
         for there in range(4):
             for side in range(2):
                 own[slot, there, side] = own[slot, there, side] + got_core[slot, there, side]
-        y_copy(chunk).start()
-
-    def stage_y(chunk):
-        y_copy(chunk).wait_recv()
+
+        def z_first():
+            for which in range(2):
+                near_copy(chunk, which, True).start()
+
+        by_order(chunk, lambda: y_copy(chunk, True).start(), z_first)
+
+    def stage_second(chunk):
         slot = spot(chunk)
-        for there in range(4):
-            own[slot, there, y] = own[slot, there, y] + got_y[slot, there]
-        for hop in range(1, 4):
-            z_copy(chunk, hop).start()
+
+        def y_first():
+            y_copy(chunk, True).wait()
+            for there in range(4):
+                own[slot, there, y] = own[slot, there, y] + got_y[slot, there]
+            for which in range(2):
+                near_copy(chunk, which, False).start()
+
+        def z_first():
+            for which in range(2):
+                near_copy(chunk, which, True).wait()
+            for row in range(2):
+                own[slot, far, row] = own[slot, far, row] + got_near[slot, 1, row]
+                own[slot, z, row] = own[slot, z, row] + got_near[slot, 0, row]
+            far_copy(chunk, True).start()
+
+        by_order(chunk, y_first, z_first)
+
+    def stage_third(chunk):
+        slot = spot(chunk)
+
+        def y_first():
+            for which in range(2):
+                near_copy(chunk, which, False).wait()
+            own[slot, far, y] = own[slot, far, y] + got_near[slot, 1, 0]
+            own[slot, z, y] = own[slot, z, y] + got_near[slot, 0, 0]
+            far_copy(chunk, False).start()
+
+        def z_first():
+            far_copy(chunk, True).wait()
+            for row in range(2):
+                own[slot, z, row] = own[slot, z, row] + got_far[slot, row]
+            y_copy(chunk, False).start()
+
+        by_order(chunk, y_first, z_first)
         for copy in inner_copies(chunk):
             copy.start()
 
-    def stage_z(chunk):
-        y_copy(chunk).wait_send()
-        for hop in range(1, 4):
-            z_copy(chunk, hop).wait_recv()
+    def stage_last(chunk):
         for copy in inner_copies(chunk):
             copy.wait()
-        total = own[spot(chunk), z, y].astype(F32)
-        for hop in range(3):
-            total = total + got_z[spot(chunk), hop].astype(F32)
+        by_order(chunk, lambda: far_copy(chunk, False).wait(), lambda: y_copy(chunk, False).wait())
+        slot = spot(chunk)
+        turn_z = lax.rem(chunk, CYCLE) == CYCLE // 2
+        total = own[slot, z, y].astype(F32) + jnp.where(turn_z, got_y[slot, 0].astype(F32), got_far[slot, 0].astype(F32))
         level, rows = place(chunk)
         grad_out[level, rows, :] = total
         slot = lax.rem(chunk, 4)
@@ -1042,8 +1093,6 @@
         rep_copy(chunk).start()
 
     def stage_rep(chunk):
-        for hop in range(1, 4):
-            z_copy(chunk, hop).wait_send()
         rep_copy(chunk).wait()
         level, rows = place(chunk)
         mean_out[level, rows, :] = 0.5 * (step_own[spot(chunk)].astype(F32) + step_got[spot(chunk)].astype(F32))
@@ -1078,7 +1127,7 @@
         lax.fori_loop(1, devices, send, 0)
 
     def turn(now, carry):
-        for lag, stage in ((0, stage_product), (1, stage_core), (3, stage_y), (5, stage_z), (7, stage_rep)):
+        for lag, stage in ((0, stage_product), (1, stage_core), (3, stage_second), (5, stage_third), (7, stage_last), (9, stage_rep)):
 
             @pl.when((now >= lag) & (now < chunks + lag))
             def _():
@@ -1088,7 +1137,7 @@
         pl.when(now == 7)(small_spread)
         return carry
 
-    lax.fori_loop(0, chunks + 7, turn, 0)
+    lax.fori_loop(0, chunks + 9, turn, 0)
 
     def small_drain(step, carry):
         peer = lax.rem(me + step, devices)
@@ -1125,7 +1174,8 @@
             pltpu.VMEM((RING, 4, 2) + piece, BF16),
             pltpu.VMEM((RING, 4, 2) + piece, BF16),
             pltpu.VMEM((RING, 4) + piece, BF16),
-            pltpu.VMEM((RING, 3) + piece, BF16),
+            pltpu.VMEM((RING, 2, 2) + piece, BF16),
+            pltpu.VMEM((RING, 2) + piece, BF16),
             pltpu.VMEM((4, 3) + piece, F32),
             pltpu.VMEM((RING,) + piece, BF16),
             pltpu.VMEM((RING,) + piece, BF16),
@@ -1138,8 +1188,10 @@
             DMA((RING,)),
             DMA((RING,)),
             DMA((RING,)),
-            DMA((RING, 3)),
-            DMA((RING, 3)),
+            DMA((RING, 2)),
+            DMA((RING, 2)),
+            DMA((RING,)),
+            DMA((RING,)),
             DMA((4, 3)),
             DMA((RING,)),
             DMA((RING,)),
@@ -1300,8 +1352,8 @@
     me = lax.axis_index("dp")
     start, last = me * piece, limits[:, -1].reshape(MICRO, 1, 1)
     if count == 16:
-        (rows,), prepared, (own_hidden, own_cotangent) = gather(
-            low_weights, ((0, 0, PLANES),), own_hidden, own_cotangent, small_params, first_small[0], second_small[0]
+        (proj, rest), prepared, (own_hidden, own_cotangent) = gather(
+            low_weights, ((0, 0, 1), (0, 1, PLANES)), own_hidden, own_cotangent, small_params, first_small[0], second_small[0]
         )
         half = count // MICRO
         start = (lax.broadcasted_iota(jnp.int32, (MICRO, 1, 1), 0) * half + lax.rem(me, half)) * piece
@@ -1315,11 +1367,11 @@
     smalls = [(prepared[level], prepared[LAYERS + level]) for level in range(LAYERS)]
     for level in range(LAYERS):
         if count == 16:
-            spans = ((level + 1, 0, PLANES),) if level + 1 < LAYERS else ()
+            spans = ((level + 1, 0, 1), (level + 1, 1, PLANES)) if level + 1 < LAYERS else ()
             activation, states[level], more = forward_layer(
-                count, activation, rows[: 3 * D], rows[3 * D :], smalls[level], edges, 1 + 4 * level, low_weights, spans
+                count, activation, proj, rest, smalls[level], edges, 1 + 4 * level, low_weights, spans
             )
-            rows = more[0] if more else None
+            proj, rest = more or (None, None)
         else:
             rows = lax.all_gather(low_weights[level], "dp", axis=0, tiled=True)
             activation, states[level], _ = forward_layer(count, activation, rows[: 3 * D], rows[3 * D :], smalls[level], edges, 1)

time: 530 us -> 494 us (0.932)
  local copies, waits for them, and re-layouts: 30.5 us -> 8.03 us
  Pallas kernels: 423 us -> 406 us
    slice x4 -> x0, local copies, waits for them, and re-layouts: 17.3 us -> none  [the longest x2 14.8 us: shards(): rows[3 * D:]]
    pallas_call x1, Pallas kernels: 183 us -> 166 us  [settle(): pl.pallas_call(functools.partial(settle_kernel, block_rows), out_shape=[j...]
where the time goes in v8:
time: 494 us; the launch traced here: 486 us
  Pallas kernels  406 us (82%)
  matrix products  43.8 us (9%)
  other arithmetic  25.7 us (5%)
  local copies, waits for them, and re-layouts  8.03 us (2%)
    pallas_call x1, Pallas kernels, settle(): pl.pallas_call(functools.partial(settle_kernel, block_rows), out_shape=[j...  166 us
    pallas_call x2, Pallas kernels, attention_forward(): pl.pallas_call(functools.partial(forward_kernel, count, piece, spans), ou...  104 us
    pallas_call x1, Pallas kernels, gather(): pl.pallas_call(functools.partial(gather_kernel, spans), out_shape=[spread...  70.8 us
    pallas_call x2, Pallas kernels, attention_backward(): pl.pallas_call(functools.partial(backward_kernel, count, piece, len(carri...  62.9 us
    dot_general x24, matrix products, mm(): return lax.dot_general(a, b, dims, preferred_element_type=F32)  43.8 us

profile of v8, /device:TPU:0, one launch (start us, length us, event | category | flops | bytes accessed | tf_op | source)
XLA Modules:
  0.0 486.2 jit_solution(15926296961297642068)
XLA Ops:
  0.7 0.7 convert_element_type.80
  1.3 0.6 pad.4.edges
  1.9 1.3 fusion.84
  4.6 3.4 convert_element_type.75.low
  8.0 70.8 %gather.1 = (bf16[1,2,2,576,768]{4,3,2,1,0:T(8,128)(2,1)}, bf16[3,2,2,576,768]{4,3,2,1,0:T(8,128)(2,1)}, f32[16,768]{1,0:T(8,128)}, f32[16,768]{1,0:T(8,128)}, f...) custom-call(bf16[2,576,768]{2,1,0:T(8,128)(2,1)} %convert_element_ty, ...), custom_call_target="tpu_custom_call" | custom-call | tf_op jit(solution)/shard_map/gather/pallas_call | solution.py:854
  78.8 1.4 slice_reduce_fusion
  80.3 1.7 fusion.64
  82.0 1.6 fusion.65
  83.6 1.6 convolution_convert_fusion.3
  85.3 0.9 pad_maximum_fusion.qkv
  86.4 0.6 reduce_sum.271.refs_24_
  87.1 77.5 %attend_forward.2 = (bf16[1,2,64,768]{3,2,1,0:T(8,128)(2,1)}, bf16[3,2,512,128]{3,2,1,0:T(8,128)(2,1)}, f32[128,128]{1,0:T(8,128)}, f32[128,128]{1,0:T(8,128)}, ...) custom-call(bf16[3,2,64,768]{3,2,1,0:T(8,128)(2,1)} %pad_maximum_fus, ...), custom_call_target="tpu_custom_call" | custom-call | tf_op jit(solution)/shard_map/attend_forward/pallas_call | solution.py:544
  164.5 1.8 fusion.85
  166.8 4.1 multiply_convert_fusion.1
  170.9 3.5 fusion.86
  175.9 0.9 pad_maximum_fusion.1.qkv
  176.8 27.0 %attend_forward.3 = (bf16[1,2,64,768]{3,2,1,0:T(8,128)(2,1)}, bf16[3,2,512,128]{3,2,1,0:T(8,128)(2,1)}, f32[128,128]{1,0:T(8,128)}, f32[128,128]{1,0:T(8,128)}, ...) custom-call(bf16[3,2,64,768]{3,2,1,0:T(8,128)(2,1)} %pad_maximum_fus, ...), custom_call_target="tpu_custom_call" | custom-call | tf_op jit(solution)/shard_map/attend_forward/pallas_call | solution.py:544
  203.8 1.8 fusion.87
  206.0 4.2 multiply_convert_fusion
  210.3 3.5 fusion.88
  214.3 0.7 bitcast_reduce_fusion.refs_23_
  215.0 1.0 fusion.81
  216.0 2.1 fusion.37.refs_15_
  218.1 0.9 multiply_reduce_fusion.11
  219.1 0.7 bitcast_reduce_fusion.1
  220.0 1.2 convolution_convert_fusion.1
  221.2 32.0 %attend_backward.2 = (bf16[3,2,64,768]{3,2,1,0:T(8,128)(2,1)}, f32[6,2,256]{2,1,0:T(2,128)}, f32[2,64,768]{2,1,0:T(8,128)}) custom-call(bf16[1,2,64,768]{3,2,1,0:T(8,128)(2,1)} %bitcast.165, f32[2,128]{1,0:T(2,128)} %pad.4.edges, f32[16,768]{1,0:T(8,128)} %get-tuple-element.71.lines.low, f32[2,64,768]{2,1,0:T(8,128)} %bitcast.142, ...), custom_call_target="tpu_custom_call" | custom-call | tf_op jit(solution)/shard_map/attend_backward/pallas_call | solution.py:575
  253.2 1.2 fusion.83
  254.4 1.8 fusion.69
  256.2 2.0 convolution_add_fusion.3
  258.2 1.9 multiply_reduce_fusion.10
  260.1 0.7 bitcast_reduce_fusion.3
  261.0 4.4 fusion.30.refs_2_
  265.5 0.9 multiply_reduce_fusion.9
  266.4 0.7 bitcast_reduce_fusion.5
  267.3 1.2 convolution_convert_fusion
  268.5 30.9 %attend_backward.3 = (bf16[3,2,64,768]{3,2,1,0:T(8,128)(2,1)}, f32[6,2,256]{2,1,0:T(2,128)}) custom-call(bf16[1,2,64,768]{3,2,1,0:T(8,128)(2,1)} %bitcast.166, f32[2,128]{1,0:T(2,128)} %pad.4.edges, f32[16,768]{1,0:T(8,128)} %get-tuple-element.66.lines, bf16[3,2,512,128]{3,2,1,0:T(8,128)(2,1)} %get-tuple-element.91.refs_0_, ...), custom_call_target="tpu_custom_call" | custom-call | tf_op jit(solution)/shard_map/attend_backward/pallas_call | solution.py:575
  299.5 1.2 fusion.82
  300.6 0.5 fusion.68
  301.2 0.5 convolution_add_fusion.1
  301.7 1.3 fusion.45
  303.0 165.9 %settle.1 = (f32[2,576,768]{2,1,0:T(8,128)}, f32[2,576,768]{2,1,0:T(8,128)}, f32[16,2,2,768]{3,2,1,0:T(2,128)}, f32[2,64,768]{2,1,0:T(8,128)}) custom-call(bf16[128,768]{1,0:T(8,128)(2,1)} %bitcast.157, bf16[128,768]{1,0:T(8,128)(2,1)} %bitcast.162, bf16[128,3072]{1,0:T(8,128)(2,1)} %copy-done.15, bf16[128,3072]{1,0:T(8,128)(2,1)} %copy-done.12, ...), custom_call_target="tpu_custom_call" | custom-call | tf_op jit(solution)/shard_map/settle/pallas_call | solution.py:1160
  468.9 1.8 finish.1
  470.7 8.7 %fusion.23 = (f32[1,2,576,768]{3,2,1,0:T(8,128)}, f32[1,2,576,768]{3,2,1,0:T(8,128)}) fusion(f32[2,576,768]{2,1,0:T(8,128)} %get-tuple-element.110, f32[1,2,576,768]{3,2,1,0:T(8,128)} %param.17, f32[1,2,576,768]{3,2,1,0:T(8,128)} %param.16), kind=kLoop, calls=%fused_computation.20 | loop fusion | flops 6193152 | bytes 17694720 | tf_op jit(solution)/shard_map/broadcast_in_dim | solution.py:1409
  479.4 0.7 copy-done.4
  480.1 4.4 fusion.77
  484.5 0.7 copy.26
  485.3 0.7 copy.27
  (91 shorter events, 3.5 us)
Async XLA Ops:
  78.8 3.2 copy-start.18
  83.6 2.5 copy-start.19
  164.5 2.2 copy-start.21
  166.7 4.2 copy-start.5
  170.9 3.6 copy-start.12
  170.9 3.9 copy-start.3
  174.9 0.7 copy-start.6
  203.8 2.2 copy-start.20
  206.0 4.3 copy-start.7
  206.0 10.0 %slice-start.3 = ((s8[10616832]{0:T(1024)(128)(4,1)}), s8[4194304]{0:T(1024)(128)(4,1)S(1)}, s32[]{:S(2)}) async-start(s8[10616832]{0:T(1024)(128)(4,1)} %bitcast.188), calls=%async_computation.3 | async-start | bytes 8388608
  206.0 10.0 %slice-start.4 = ((s8[10616832]{0:T(1024)(128)(4,1)}), s8[4194304]{0:T(1024)(128)(4,1)S(1)}, s32[]{:S(2)}) async-start(s8[10616832]{0:T(1024)(128)(4,1)} %bitcast.188), calls=%async_computation.4 | async-start | bytes 8388608
  210.3 3.6 copy-start.13
  210.3 5.7 %slice-start.5 = ((s8[10616832]{0:T(1024)(128)(4,1)}), s8[2228224]{0:T(1024)(128)(4,1)S(1)}, s32[]{:S(2)}) async-start(s8[10616832]{0:T(1024)(128)(4,1)} %bitcast.188), calls=%async_computation.5 | async-start | bytes 4456448
  216.0 2.1 copy-start.8
  218.1 0.9 copy-start.14
  220.0 33.2 %copy-start.9 = (bf16[128,768]{1,0:T(8,128)(2,1)}, bf16[128,768]{1,0:T(8,128)(2,1)S(1)}, u32[]{:S(2)}) copy-start(bf16[128,768]{1,0:T(8,128)(2,1)S(1)} %get-tuple-element.163.refs_18_) | copy-start | bytes 589828
  256.2 9.2 %slice-start = ((s8[10616832]{0:T(1024)(128)(4,1)}), s8[4194304]{0:T(1024)(128)(4,1)S(1)}, s32[]{:S(2)}) async-start(s8[10616832]{0:T(1024)(128)(4,1)} %bitcast.181), calls=%async_computation | async-start | bytes 8388608
  260.8 4.6 slice-start.1
  261.0 4.4 copy-start.10
  261.0 4.4 slice-start.2
  265.4 1.0 copy-start.15
  267.3 32.1 %copy-start.11 = (bf16[128,768]{1,0:T(8,128)(2,1)}, bf16[128,768]{1,0:T(8,128)(2,1)S(1)}, u32[]{:S(2)}) copy-start(bf16[128,768]{1,0:T(8,128)(2,1)S(1)} %get-tuple-element.159.refs_5_) | copy-start | bytes 589828
  268.5 32.1 %copy-start.2 = (bf16[1,2,2,576,768]{4,3,2,1,0:T(8,128)(2,1)S(1)}, bf16[1,2,2,576,768]{4,3,2,1,0:T(8,128)(2,1)}, u32[]{:S(2)}) copy-start(bf16[1,2,2,576,768]{4,3,2,1,0:T(8,128)(2,1)} %get-tuple-element.65) | copy-start | bytes 10616836
  470.7 8.7 %copy-start = (f32[2,576,768]{2,1,0:T(8,128)S(1)}, f32[2,576,768]{2,1,0:T(8,128)}, u32[]{:S(2)}) copy-start(f32[2,576,768]{2,1,0:T(8,128)} %refs_26_.1) | copy-start | bytes 10616836
  470.7 8.7 %copy-start.1 = (f32[2,576,768]{2,1,0:T(8,128)S(1)}, f32[2,576,768]{2,1,0:T(8,128)}, u32[]{:S(2)}) copy-start(f32[2,576,768]{2,1,0:T(8,128)} %param.20) | copy-start | bytes 10616836
  470.7 9.4 %copy-start.4 = (f32[2,576,768]{2,1,0:T(8,128)S(1)}, f32[2,576,768]{2,1,0:T(8,128)}, u32[]{:S(2)}) copy-start(f32[2,576,768]{2,1,0:T(8,128)} %get-tuple-element.114) | copy-start | bytes 10616836
  480.1 4.4 copy-start.16
  480.1 5.2 %copy-start.17 = (f32[2,64,768]{2,1,0:T(8,128)S(1)}, f32[2,64,768]{2,1,0:T(8,128)}, u32[]{:S(2)}) copy-start(f32[2,64,768]{2,1,0:T(8,128)} %get-tuple-element.109) | copy-start | bytes 1179652

commit v9 on v8

--- a/solution.py
+++ b/solution.py
@@ -867,6 +867,7 @@
 RING = 12
 CYCLE = 6
 MATES = ("low_in", "low_comb", "low_up", "low_act", "low_grads", "low_branch", "low_hidden", "low_down", "gain_one", "shift_one", "gain_two", "shift_two", "taps")
+LATE = ("low_grads", "taps")
 
 
 def change(grad, first_old, second_old):
@@ -875,14 +876,21 @@
     return new_first * (1.0 / (1.0 - ADAM_ONE**STEP_COUNT)) / (jnp.sqrt(new_second * (1.0 / (1.0 - ADAM_TWO**STEP_COUNT))) + ADAM_EPSILON)
 
 
-def settle_kernel(block_rows, *refs):
-    count = len(MATES)
-    mates = [dict(zip(MATES, refs[level * count : (level + 1) * count])) for level in range(LAYERS)]
+def settle_kernel(block_rows, tokens, *refs):
+    early = [name for name in MATES if name not in LATE]
+    mates = [dict(zip(early, refs)), dict(zip(MATES, refs[len(early) :]))]
+    refs = refs[len(early) + len(MATES) :]
+    grads, edges, lines, proj, grad_one, slab = refs[:6]
+    keep = dict(zip(KEPT, refs[6:]))
+    refs = refs[6 + len(KEPT) :]
     (
-        weights, first, second, small_first, small_second, grad_in, grad_out, mean_out, small_out, grad_in_out,
+        weights, first, second, small_first, small_second, grad_out, mean_out, small_out, grad_in_out,
         turned, right, staged, own, got_core, got_y, got_near, got_far, inner, step_own, step_got, small, small_got, small_own, small_step, small_step_got,
         core_send, core_got, y_send, y_got, near_send, near_got, far_send, far_got, inner_sem, rep_send, rep_got, small_send, small_sem, back_send, back_sem, small_rep, swap_sems,
-    ) = refs[LAYERS * count :]
+        low_grads, taps, grad_slab, padded, padded_grads, blended, result, grad_in, send_one, receive_one, send_two, receive_two,
+    ) = refs
+    mates[0].update(low_grads=low_grads, taps=taps)
+    piece = grads.shape[2]
     me = lax.axis_index("dp")
     other_rep = 1 - lax.axis_index("rep")
     core, y, z = lax.rem(me, 2), lax.rem(me // 2, 2), me // 4
@@ -909,17 +917,20 @@
         return lax.rem(slot, RING)
 
     features = D * 2 + FF * 2
-    for order, level in enumerate(reversed(range(LAYERS))):
-        mate = mates[level]
-        at = order * features
+
+    def prepare(level):
+        order = LAYERS - 1 - level
+        mate, at = mates[level], order * features
         for name in MATES[:4]:
             for part in range(mate[name].shape[1] // LANES):
                 turned[at : at + LANES, :] = mate[name][:, part * LANES : (part + 1) * LANES].T
                 at += LANES
         for part in range(3):
-            right[order * 6 + part] = mate["low_grads"][part]
+            right[order * 6 + part] = mate["low_grads"][part].reshape(tokens, D)
         for part, name in enumerate(MATES[5:8]):
             right[order * 6 + 3 + part] = mate[name][...]
+
+    prepare(LAYERS - 1)
 
     def put(level, line, row):
         index = level * LINES + line
@@ -928,31 +939,58 @@
     def column_sum(array):
         return jnp.sum(array.astype(F32), axis=0, keepdims=True)
 
-    for level in range(LAYERS):
-        mate = mates[level]
-        put(level, 0, column_sum(mate["low_grads"][0]))
-        put(level, 1, column_sum(mate["low_grads"][2]))
-        put(level, 2, column_sum(mate["low_branch"][...]))
-        put(level, 3, column_sum(mate["low_down"][...]))
-        for line, name in enumerate(MATES[8:12]):
-            put(level, 4 + line, column_sum(mate[name][...]))
-        for part in range(FF // D):
-            put(level, 8 + part, column_sum(mate["low_up"][:, part * D : (part + 1) * D]))
-        line = jnp.zeros((1, D), F32)
-        for head in range(HEADS):
-            taps = jnp.concatenate([mate["taps"][head // 2][head % 2 : head % 2 + 1], jnp.zeros((1, D - 2 * LANES), F32)], axis=1)
-            taps = jnp.where(iota((1, D), 1) < TAPS, taps, 0.0)
-            line = line + (pltpu.roll(taps, TAPS * head, 1) if head else taps)
-        put(level, 12, line)
-    for index in range(LAYERS * LINES, 2 * devices):
-        small[index // 2, index % 2 : index % 2 + 1, :] = jnp.zeros((1, D), F32)
+    def small_rows():
+        for level in range(LAYERS):
+            mate = mates[level]
+            put(level, 0, column_sum(right[(LAYERS - 1 - level) * 6]))
+            put(level, 1, column_sum(right[(LAYERS - 1 - level) * 6 + 2]))
+            put(level, 2, column_sum(mate["low_branch"][...]))
+            put(level, 3, column_sum(mate["low_down"][...]))
+            for line, name in enumerate(MATES[8:12]):
+                put(level, 4 + line, column_sum(mate[name][...]))
+            for part in range(FF // D):
+                put(level, 8 + part, column_sum(mate["low_up"][:, part * D : (part + 1) * D]))
+            line = jnp.zeros((1, D), F32)
+            for head in range(HEADS):
+                taps = jnp.concatenate([mate["taps"][head // 2][head % 2 : head % 2 + 1], jnp.zeros((1, D - 2 * LANES), F32)], axis=1)
+                taps = jnp.where(iota((1, D), 1) < TAPS, taps, 0.0)
+                line = line + (pltpu.roll(taps, TAPS * head, 1) if head else taps)
+            put(level, 12, line)
+        for index in range(LAYERS * LINES, 2 * devices):
+            small[index // 2, index % 2 : index % 2 + 1, :] = jnp.zeros((1, D), F32)
 
     pl.semaphore_wait(barrier, devices)
 
-    at_layout = Layout(16).place()
-    swapping = swap(at_layout, grad_in, grad_in_out, swap_sems.at[0], swap_sems.at[1])
-    swapping.start()
-    grad_in_out[pl.ds(at_layout.group, 1)] = grad_in[pl.ds(at_layout.group, 1)]
+    at = Layout(16).place()
+    out = scatter_tasks(at, piece, grads, grad_slab, send_one, receive_one)
+    back = return_rows(at, piece, result, low_grads, send_two, receive_two)
+    swapping = swap(at, grad_in, grad_in_out, swap_sems.at[0], swap_sems.at[1])
+    out(False)
+
+    def attention():
+        taps[...] = jnp.zeros(taps.shape, F32)
+
+        @pl.when(at.owns)
+        def _():
+            await_slab(at, piece, grad_slab, receive_one)
+            attend_back(
+                whole(grad_slab, 0), whole(slab, 0), whole(slab, 1), whole(slab, 2), edges[pl.ds(at.micro, 1), :], head_taps(lines, at.pair),
+                keep, padded, padded_grads, blended, result, taps.at[at.pair],
+            )
+            back(False)
+
+    def collect():
+        out(True)
+        await_rows(at, low_grads, receive_two)
+        pl.when(at.owns)(lambda: back(True))
+
+    def input_grads():
+        total = grad_one[...]
+        for part in range(3):
+            total = total + mm(low_grads[part].reshape(tokens, D), proj[part], NT)
+        grad_in[...] = total.reshape(grad_in.shape)
+        swapping.start()
+        grad_in_out[pl.ds(at.group, 1)] = grad_in[pl.ds(at.group, 1)]
 
     def small_copy(step):
         peer = lax.rem(me + step, devices)
@@ -962,7 +1000,9 @@
         small_copy(step).start()
         return carry
 
-    lax.fori_loop(1, devices, small_begin, 0)
+    def small_start():
+        small_rows()
+        lax.fori_loop(1, devices, small_begin, 0)
 
     def core_copy(chunk):
         return to_dp(staged.at[lax.rem(chunk, 2)], got_core.at[spot(chunk)], core_send.at[lax.rem(chunk, 2)], core_got.at[spot(chunk)], me + 1 - 2 * core)
@@ -1133,8 +1173,10 @@
             def _():
                 stage(now - lag)
 
-        pl.when(now == 4)(small_sum)
-        pl.when(now == 7)(small_spread)
+        for when, act in (
+            (2, attention), (6, collect), (7, lambda: prepare(0)), (8, input_grads), (9, small_start), (13, small_sum), (16, small_spread),
+        ):
+            pl.when(now == when)(act)
         return carry
 
     lax.fori_loop(0, chunks + 9, turn, 0)
@@ -1151,21 +1193,26 @@
     swapping.wait()
 
 
-def settle(mates, weights, first, second, small_first, small_second, grad_in):
+def settle(mates, attention, weights, first, second, small_first, small_second):
     block_rows = weights.shape[1]
     anywhere = pl.BlockSpec(memory_space=pl.ANY)
     devices = 16
     piece = (CHUNK, D)
     tokens = mates[0]["low_in"].shape[0]
+    share = attention[0].shape[2]
+    at = Layout(devices)
+    length = share * devices
+    halved = (at.groups, length // at.groups, LANES)
+    early = [mates[0][name] for name in MATES if name not in LATE] + [mates[1][name] for name in MATES] + list(attention)
     return pl.pallas_call(
-        functools.partial(settle_kernel, block_rows),
+        functools.partial(settle_kernel, block_rows, tokens),
         out_shape=[
             jax.ShapeDtypeStruct(weights.shape, F32),
             jax.ShapeDtypeStruct(weights.shape, F32),
             jax.ShapeDtypeStruct((devices, 2, 2, D), F32),
-            jax.ShapeDtypeStruct(grad_in.shape, F32),
+            jax.ShapeDtypeStruct((MICRO, share, D), F32),
         ],
-        in_specs=[VMEM] * (LAYERS * len(MATES)) + [anywhere] * 3 + [VMEM] * 3,
+        in_specs=[VMEM] * len(early) + [anywhere] * 3 + [VMEM] * 2,
         out_specs=[VMEM] * 4,
         scratch_shapes=[
             pltpu.VMEM((LAYERS * 2 * (D + FF), tokens), BF16),
@@ -1201,10 +1248,22 @@
             DMA((devices,)),
             DMA((2,)),
             DMA((2,)),
+            pltpu.VMEM((3, MICRO, share, D), BF16),
+            pltpu.VMEM((PAIRS, 2, 2 * LANES), F32),
+            pltpu.VMEM((1,) + halved, BF16),
+            pltpu.VMEM((length + LANES, LANES), BF16),
+            pltpu.VMEM((length + LANES, LANES), BF16),
+            pltpu.VMEM((length, LANES), F32),
+            pltpu.VMEM((3,) + halved, BF16),
+            pltpu.VMEM((MICRO, share, D), F32),
+            DMA((at.tasks,)),
+            DMA((at.members,)),
+            DMA((at.members,)),
+            DMA((at.tasks,)),
         ],
         compiler_params=pltpu.CompilerParams(collective_id=3, has_side_effects=True, vmem_limit_bytes=63 << 20),
         name="settle",
-    )(*[mate[name] for mate in mates for name in MATES], weights, first, second, small_first, small_second, grad_in)
+    )(*early, weights, first, second, small_first, small_second)
 
 
 def finish_kernel(both, params, outer, first, second, first_new, second_new, outer_new, params_new, grad, mean):
@@ -1284,7 +1343,7 @@
     return output, (proj, rest, low_in, kept, low_comb, resid_one, low_hidden, upward, low_act, resid_two), fetched
 
 
-def backward_layer(count, grad_output, small, edges, state, ident, carried=()):
+def backward_layer(count, grad_output, small, edges, state, ident, carried=(), later=False):
     proj, rest, low_in, kept, low_comb, resid_one, low_hidden, upward, low_act, resid_two = state
     total = low_in.shape[0]
     piece = total // MICRO
@@ -1299,10 +1358,14 @@
     grad_one, grad_gain_one, grad_shift_one = layer_norm_back(resid_one, lines[4:5], grad_hidden)
     low_branch = grad_one.astype(BF16)
     grad_comb = dense(low_branch, out_weight, NT).astype(BF16)
+    vectors = (grad_gain_one, grad_shift_one, grad_gain_two, grad_shift_two)
+    if later:
+        names = [name for name in MATES if name not in LATE]
+        values = (low_in, low_comb, low_up, low_act, low_branch, low_hidden, low_down, *vectors)
+        return None, dict(zip(names, values)), (grad_comb.reshape(1, MICRO, piece, D), edges, lines, proj, grad_one, *kept)
     low_grads, grad_taps, swapped = attention_backward(count, grad_comb.reshape(1, MICRO, piece, D), edges, lines, kept, ident, carried)
     low_grads = low_grads.reshape(3, total, D)
     grad_in = grad_one + sum(dense(low_grads[part], proj[part], NT) for part in range(3))
-    vectors = (grad_gain_one, grad_shift_one, grad_gain_two, grad_shift_two)
     values = (low_in, low_comb, low_up, low_act, low_grads, low_branch, low_hidden, low_down, *vectors, grad_taps)
     return grad_in, dict(zip(MATES, values)), swapped
 
@@ -1379,11 +1442,12 @@
     mates = [None] * LAYERS
     for level in reversed(range(LAYERS)):
         carried = (activation.reshape(MICRO, piece, D),) if count == 16 and level == LAYERS - 1 else ()
-        gradient, mates[level], swapped = backward_layer(count, gradient, smalls[level], edges, states[level], 2 + 4 * level, carried)
+        later = count == 16 and level == 0
+        gradient, mates[level], swapped = backward_layer(count, gradient, smalls[level], edges, states[level], 2 + 4 * level, carried, later)
         activation = swapped[0] if carried else activation
     if count == 16:
         grad_big, mean_big, small_both, gradient = settle(
-            mates, weights, first_big[0], second_big[0], *prepared[2 * LAYERS :], gradient.reshape(MICRO, piece, D)
+            mates, swapped, weights, first_big[0], second_big[0], *prepared[2 * LAYERS :]
         )
         new_smalls = finish(small_both, small_params, outer_small, first_small[0], second_small[0])
     else:

time: 494 us -> 484 us (0.980)
  Pallas kernels: 406 us -> 398 us
    pallas_call x2 -> x1, Pallas kernels: 62.9 us -> 31.8 us  [attention_backward(): pl.pallas_call(functools.partial(backward_kernel, count, piece, len(carri...]
    pallas_call x1, Pallas kernels: 166 us -> 189 us  [settle(): pl.pallas_call(functools.partial(settle_kernel, block_rows, tokens), out_...]
    dot_general x24 -> x21, matrix products: 43.8 us -> 41.7 us  [mm(): return lax.dot_general(a, b, dims, preferred_element_type=F32)]
where the time goes in v9:
time: 484 us; the launch traced here: 476 us
  Pallas kernels  398 us (82%)
  matrix products  41.7 us (9%)
  other arithmetic  26.5 us (5%)
  local copies, waits for them, and re-layouts  6.86 us (1%)
    pallas_call x1, Pallas kernels, settle(): pl.pallas_call(functools.partial(settle_kernel, block_rows, tokens), out_...  189 us
    pallas_call x2, Pallas kernels, attention_forward(): pl.pallas_call(functools.partial(forward_kernel, count, piece, spans), ou...  104 us
    pallas_call x1, Pallas kernels, gather(): pl.pallas_call(functools.partial(gather_kernel, spans), out_shape=[spread...  70.8 us
    dot_general x21, matrix products, mm(): return lax.dot_general(a, b, dims, preferred_element_type=F32)  41.7 us
    pallas_call x1, Pallas kernels, attention_backward(): pl.pallas_call(functools.partial(backward_kernel, count, piece, len(carri...  31.8 us

profile of v9, /device:TPU:0, one launch (start us, length us, event | category | flops | bytes accessed | tf_op | source)
XLA Modules:
  0.0 475.6 jit_solution(9345663623521684348)
XLA Ops:
  0.7 0.7 convert_element_type.80
  1.3 0.6 pad.4.edges.refs_25_
  1.9 1.3 fusion.83
  4.6 3.4 convert_element_type.75.low
  8.0 70.8 %gather.1 = (bf16[1,2,2,576,768]{4,3,2,1,0:T(8,128)(2,1)}, bf16[3,2,2,576,768]{4,3,2,1,0:T(8,128)(2,1)}, f32[16,768]{1,0:T(8,128)}, f32[16,768]{1,0:T(8,128)}, f...) custom-call(bf16[2,576,768]{2,1,0:T(8,128)(2,1)} %convert_element_ty, ...), custom_call_target="tpu_custom_call" | custom-call | tf_op jit(solution)/shard_map/gather/pallas_call | solution.py:854
  78.8 1.4 slice_reduce_fusion
  80.3 1.7 fusion.65
  82.0 1.6 fusion.66
  83.6 1.6 fusion.64
  85.3 0.9 pad_maximum_fusion.qkv
  86.4 0.6 reduce_sum.271.refs_22_
  87.1 77.5 %attend_forward.2 = (bf16[1,2,64,768]{3,2,1,0:T(8,128)(2,1)}, bf16[3,2,512,128]{3,2,1,0:T(8,128)(2,1)}, f32[128,128]{1,0:T(8,128)}, f32[128,128]{1,0:T(8,128)}, ...) custom-call(bf16[3,2,64,768]{3,2,1,0:T(8,128)(2,1)} %pad_maximum_fus, ...), custom_call_target="tpu_custom_call" | custom-call | tf_op jit(solution)/shard_map/attend_forward/pallas_call | solution.py:544
  164.6 1.8 fusion.84
  166.8 4.1 multiply_convert_fusion.1
  170.9 3.6 fusion.85
  174.9 0.3 fusion.68
  175.2 0.3 fusion.67
  175.6 0.3 convolution_convert_fusion.2
  175.9 0.9 pad_maximum_fusion.1.qkv
  176.8 27.0 %attend_forward.3 = (bf16[1,2,64,768]{3,2,1,0:T(8,128)(2,1)}, bf16[3,2,512,128]{3,2,1,0:T(8,128)(2,1)}, f32[128,128]{1,0:T(8,128)}, f32[128,128]{1,0:T(8,128)}, ...) custom-call(bf16[3,2,64,768]{3,2,1,0:T(8,128)(2,1)} %pad_maximum_fus, ...), custom_call_target="tpu_custom_call" | custom-call | tf_op jit(solution)/shard_map/attend_forward/pallas_call | solution.py:544
  203.9 1.8 fusion.86
  206.1 4.2 multiply_convert_fusion
  210.4 3.6 fusion.87
  214.1 0.2 multiply_reduce_fusion.3
  214.4 0.7 bitcast_reduce_fusion.refs_21_
  215.1 1.0 fusion.81
  216.1 2.2 fusion.37.refs_13_
  218.3 0.9 multiply_reduce_fusion.11
  219.3 0.7 bitcast_reduce_fusion.1
  220.2 1.2 convolution_convert_fusion.1
  221.4 31.8 %attend_backward.1 = (bf16[3,2,64,768]{3,2,1,0:T(8,128)(2,1)}, f32[6,2,256]{2,1,0:T(2,128)}, f32[2,64,768]{2,1,0:T(8,128)}) custom-call(bf16[1,2,64,768]{3,2,1,0:T(8,128)(2,1)} %bitcast.154, f32[2,128]{1,0:T(2,128)} %pad.4.edges.refs_25_, f32[16,768]{1,0:T(8,128)} %get-tuple-element.69.lines.low, f32[2,64,768]{2,1,0:T(8,128)} %bitcast.134, ...), custom_call_target="tpu_custom_call" | custom-call | tf_op jit(solution)/shard_map/attend_backward/pallas_call | solution.py:575
  253.2 1.2 fusion.82
  254.4 1.8 fusion.69
  256.2 2.0 convolution_add_fusion.1
  258.1 1.9 multiply_reduce_fusion.10
  260.1 0.7 bitcast_reduce_fusion.3
  261.0 4.5 fusion.30.refs_2_
  265.6 0.9 multiply_reduce_fusion.9
  266.5 0.7 bitcast_reduce_fusion.5
  267.3 0.9 fusion.78
  268.2 1.2 convolution_convert_fusion
  269.4 188.8 %settle.1 = (f32[2,576,768]{2,1,0:T(8,128)}, f32[2,576,768]{2,1,0:T(8,128)}, f32[16,2,2,768]{3,2,1,0:T(2,128)}, f32[2,64,768]{2,1,0:T(8,128)}) custom-call(bf16[128,768]{1,0:T(8,128)(2,1)} %bitcast.145, bf16[128,768]{1,0:T(8,128)(2,1)} %bitcast.150, bf16[128,3072]{1,0:T(8,128)(2,1)} %copy-done.14, bf16[128,3072]{1,0:T(8,128)(2,1)} %copy-done.11, ...), custom_call_target="tpu_custom_call" | custom-call | tf_op jit(solution)/shard_map/settle/pallas_call | solution.py:1207
  458.2 1.8 finish.1
  460.1 8.7 %fusion.23 = (f32[1,2,576,768]{3,2,1,0:T(8,128)}, f32[1,2,576,768]{3,2,1,0:T(8,128)}) fusion(f32[2,576,768]{2,1,0:T(8,128)} %get-tuple-element.106, f32[1,2,576,768]{3,2,1,0:T(8,128)} %param.17, f32[1,2,576,768]{3,2,1,0:T(8,128)} %param.16), kind=kLoop, calls=%fused_computation.20 | loop fusion | flops 6193152 | bytes 17694720 | tf_op jit(solution)/shard_map/broadcast_in_dim | solution.py:1473
  468.8 0.7 copy-done.3
  469.4 4.4 fusion.77
  473.9 0.7 copy.26
  474.6 0.7 copy.27
  (84 shorter events, 2.1 us)
Async XLA Ops:
  78.8 3.2 copy-start.17
  83.6 2.5 copy-start.18
  164.5 2.2 copy-start.20
  166.8 4.2 copy-start.4
  170.9 3.6 copy-start.11
  170.9 4.0 copy-start.2
  174.9 0.7 copy-start.5
  203.8 2.2 copy-start.19
  206.1 4.3 copy-start.6
  206.1 10.0 %slice-start.3 = ((s8[10616832]{0:T(1024)(128)(4,1)}), s8[4194304]{0:T(1024)(128)(4,1)S(1)}, s32[]{:S(2)}) async-start(s8[10616832]{0:T(1024)(128)(4,1)} %bitcast.176), calls=%async_computation.3 | async-start | bytes 8388608
  206.1 10.0 %slice-start.4 = ((s8[10616832]{0:T(1024)(128)(4,1)}), s8[4194304]{0:T(1024)(128)(4,1)S(1)}, s32[]{:S(2)}) async-start(s8[10616832]{0:T(1024)(128)(4,1)} %bitcast.176), calls=%async_computation.4 | async-start | bytes 8388608
  210.3 3.6 copy-start.12
  210.3 5.7 %slice-start.5 = ((s8[10616832]{0:T(1024)(128)(4,1)}), s8[2228224]{0:T(1024)(128)(4,1)S(1)}, s32[]{:S(2)}) async-start(s8[10616832]{0:T(1024)(128)(4,1)} %bitcast.176), calls=%async_computation.5 | async-start | bytes 4456448
  216.1 2.2 copy-start.7
  218.3 1.0 copy-start.13
  220.2 33.0 %copy-start.8 = (bf16[128,768]{1,0:T(8,128)(2,1)}, bf16[128,768]{1,0:T(8,128)(2,1)S(1)}, u32[]{:S(2)}) copy-start(bf16[128,768]{1,0:T(8,128)(2,1)S(1)} %get-tuple-element.159.refs_16_) | copy-start | bytes 589828
  256.2 9.4 %slice-start = ((s8[10616832]{0:T(1024)(128)(4,1)}), s8[4194304]{0:T(1024)(128)(4,1)S(1)}, s32[]{:S(2)}) async-start(s8[10616832]{0:T(1024)(128)(4,1)} %bitcast.169), calls=%async_computation | async-start | bytes 8388608
  260.8 4.7 slice-start.1
  261.0 4.5 copy-start.9
  261.0 4.5 slice-start.2
  265.5 1.0 copy-start.14
  268.2 1.2 copy-start.10
  460.1 8.7 %copy-start = (f32[2,576,768]{2,1,0:T(8,128)S(1)}, f32[2,576,768]{2,1,0:T(8,128)}, u32[]{:S(2)}) copy-start(f32[2,576,768]{2,1,0:T(8,128)} %refs_42_.1) | copy-start | bytes 10616836
  460.1 8.7 %copy-start.1 = (f32[2,576,768]{2,1,0:T(8,128)S(1)}, f32[2,576,768]{2,1,0:T(8,128)}, u32[]{:S(2)}) copy-start(f32[2,576,768]{2,1,0:T(8,128)} %param.20) | copy-start | bytes 10616836
  460.1 9.4 %copy-start.3 = (f32[2,576,768]{2,1,0:T(8,128)S(1)}, f32[2,576,768]{2,1,0:T(8,128)}, u32[]{:S(2)}) copy-start(f32[2,576,768]{2,1,0:T(8,128)} %get-tuple-element.110) | copy-start | bytes 10616836
  469.4 4.4 copy-start.15
  469.4 5.2 %copy-start.16 = (f32[2,64,768]{2,1,0:T(8,128)S(1)}, f32[2,64,768]{2,1,0:T(8,128)}, u32[]{:S(2)}) copy-start(f32[2,64,768]{2,1,0:T(8,128)} %get-tuple-element.105) | copy-start | bytes 1179652

commit v10 on v9

--- a/solution.py
+++ b/solution.py
@@ -68,6 +68,14 @@
     return mm_both(a, b, dims)
 
 
+def sweep_all(body, carry, rolled):
+    if rolled:
+        return lax.fori_loop(0, NS_ITERS, body, carry)
+    for step in range(NS_ITERS):
+        carry = body(step, carry)
+    return carry
+
+
 def iota(shape, dim):
     return lax.broadcasted_iota(jnp.int32, shape, dim)
 
@@ -170,8 +178,8 @@
         keep["total"][...] = total
         keep["inverse"][0] = kernel.T / total
 
-    def sweep(at):
-        def run():
+    def sweeps():
+        def run(at, carry):
             eye, inverse = unit(), keep["inverse"][at]
             product = exact(keep["kernel"][...], inverse)
             one = 7.0 * eye - product
@@ -181,8 +189,9 @@
             keep["two"][at] = two
             keep["three"][at] = three
             keep["inverse"][at + 1] = 0.25 * exact(inverse, three)
-
-        return run
+            return carry
+
+        sweep_all(run, 0, length <= 8 * LANES)
 
     def over_keys():
         valid = iota((1, length), 1) < mark_columns(edges())[1][MARKS - 1 :]
@@ -212,7 +221,7 @@
 
         convolve(padded, [band(one) for one in taps()], length, store)
 
-    return [begin] + [sweep(at) for at in range(NS_ITERS)] + [over_keys, over_tokens, close]
+    return [begin, sweeps, over_keys, over_tokens, close]
 
 
 def attend_back(grads, queries, keys, values, edges, taps, keep, padded, padded_grads, blended, result, grad_taps):
@@ -233,8 +242,10 @@
     grad_token = SCALE * (grad_token - token_weights * head_sums(grad_token))
     grad_summary = exact(inverse, grad_mixed, TN)
     grad_inverse = exact(grad_mixed, summary, NT)
-    grad_kernel = jnp.zeros_like(kernel)
-    for sweep in reversed(range(NS_ITERS)):
+
+    def sweep_back(step, carry):
+        grad_kernel, grad_inverse = carry
+        sweep = NS_ITERS - 1 - step
         before, product = keep["inverse"][sweep], keep["product"][sweep]
         one = 7.0 * eye - product
         two, three = keep["two"][sweep], keep["three"][sweep]
@@ -244,6 +255,9 @@
         grad_product = -(exact(grad_three, two, NT) + exact(grad_two, one, NT) + grad_one)
         grad_kernel = grad_kernel + exact(grad_product, before, NT)
         grad_inverse = 0.25 * exact(grad_inverse, three, NT) + exact(kernel, grad_product, TN)
+        return grad_kernel, grad_inverse
+
+    grad_kernel, grad_inverse = sweep_all(sweep_back, (jnp.zeros_like(kernel), grad_inverse), length <= 8 * LANES)
     total = keep["total"][...]
     turned = grad_inverse.T / total
     weighted = jnp.sum(jnp.where(blocks, turned * kernel, 0.0), axis=1, keepdims=True)
@@ -328,12 +342,16 @@
         me = lax.axis_index("dp")
         self.me, self.group, self.index = me, me // self.members, lax.rem(me, self.members)
         self.task = (self.index * self.tasks + self.members - 1) // self.members
+        if self.groups > 1:
+            self.task = jnp.where(self.index < 3, self.index, jnp.where(self.index < 6, 3, self.index - 2))
         self.owns = self.owner(self.task) == self.index
         self.micro = self.micro_of(self.task)
         self.pair = lax.rem(self.task, PAIRS)
         return self
 
     def owner(self, task):
+        if self.groups > 1:
+            return jnp.where(task < 3, task, jnp.where(task < 4, 4, task + 2))
         return task * self.members // self.tasks
 
     def micro_of(self, task):
@@ -743,7 +761,7 @@
 
     def climb(plane, sub, sign, source=None):
         target = spot(plane, y, x, sub)
-        way = 0 if sign > 0 else 1
+        way = (1 - sign) // 2
         at = plane - bottom
         return remote(target if source is None else source, target, z_send.at[at, sub, way], z_got.at[at, sub], peer("z", sign))
 
@@ -763,19 +781,29 @@
                     move("core", z, y, side, sub, shard.at[rows(side, sub), :]).start()
 
     def at_distance(distance, act):
-        for sign in (1, -1):
+        def side(step, carry):
+            sign = 1 - 2 * step
             plane = z - sign * distance
-
-            @pl.when(held(plane))
-            def _():
-                act(plane, sign)
+            pl.when(held(plane))(lambda: act(plane, sign))
+            return carry
+
+        lax.fori_loop(0, 2, side, 0)
+
+    def for_subs(act):
+        def one(sub, carry):
+            act(sub)
+            return carry
+
+        lax.fori_loop(0, SUBS, one, 0)
 
     def from_z(plane, sign):
-        for sub in range(SUBS):
+        def one(sub):
             climb(plane, sub, sign).wait_recv()
             inside(sign, lambda: climb(plane, sub, sign).start())
             for axis in ("x", "y", "core"):
                 move(axis, plane, y, x, sub).start()
+
+        for_subs(one)
 
     def take(axis, plane, row, side, sub, onward=None):
         move(axis, plane, row, side, sub).wait_recv()
@@ -816,17 +844,22 @@
     ]
 
     def sent(plane, sign):
-        for sub in range(SUBS):
+        def one(sub):
             inside(sign, lambda: climb(plane, sub, sign).wait_send())
             move("x", plane, y, x, sub).wait_send()
             move("y", plane, y, x, sub).wait_send()
+
+        for_subs(one)
         for even, odd in zip(EVEN, ODD):
             move("y", plane, y, 1 - x, even).wait_send()
             move("x", plane, 1 - y, x, odd).wait_send()
 
     def finish():
-        for distance in (1, 2, 3):
+        def distant(distance, carry):
             at_distance(distance, sent)
+            return carry
+
+        lax.fori_loop(1, 4, distant, 0)
 
         @pl.when(held(z))
         def _():
@@ -922,9 +955,16 @@
         order = LAYERS - 1 - level
         mate, at = mates[level], order * features
         for name in MATES[:4]:
-            for part in range(mate[name].shape[1] // LANES):
-                turned[at : at + LANES, :] = mate[name][:, part * LANES : (part + 1) * LANES].T
-                at += LANES
+            source, base = mate[name], at
+
+            def transpose(step, carry):
+                for part in range(D // LANES):
+                    lanes = pl.multiple_of(step * D + part * LANES, LANES)
+                    turned[pl.ds(pl.multiple_of(base + lanes, LANES), LANES), :] = source[:, pl.ds(lanes, LANES)].T
+                return carry
+
+            lax.fori_loop(0, source.shape[1] // D, transpose, 0)
+            at += source.shape[1]
         for part in range(3):
             right[order * 6 + part] = mate["low_grads"][part].reshape(tokens, D)
         for part, name in enumerate(MATES[5:8]):

time: 484 us -> 476 us (0.983); the launches traced: 476 us -> 475 us
  no operation moved by 1% of the time
where the time goes in v10:
time: 476 us; the launch traced here: 475 us
  Pallas kernels  398 us (84%)
  matrix products  41.7 us (9%)
  other arithmetic  26.5 us (6%)
  local copies, waits for them, and re-layouts  6.86 us (1%)
    pallas_call x1, Pallas kernels, settle(): pl.pallas_call(functools.partial(settle_kernel, block_rows, tokens), out_...  188 us
    pallas_call x2, Pallas kernels, attention_forward(): pl.pallas_call(functools.partial(forward_kernel, count, piece, spans), ou...  103 us
    pallas_call x1, Pallas kernels, gather(): pl.pallas_call(functools.partial(gather_kernel, spans), out_shape=[spread...  70.8 us
    dot_general x21, matrix products, mm(): return lax.dot_general(a, b, dims, preferred_element_type=F32)  41.7 us
    pallas_call x1, Pallas kernels, attention_backward(): pl.pallas_call(functools.partial(backward_kernel, count, piece, len(carri...  33.4 us

profile of v10, /device:TPU:0, one launch (start us, length us, event | category | flops | bytes accessed | tf_op | source)
XLA Modules:
  0.0 475.2 jit_solution(9475620095223134914)
XLA Ops:
  0.7 0.7 convert_element_type.80
  1.3 0.6 pad.4.edges.refs_25_
  1.9 1.3 fusion.83
  4.6 3.4 convert_element_type.75.low
  8.0 70.8 %gather.1 = (bf16[1,2,2,576,768]{4,3,2,1,0:T(8,128)(2,1)}, bf16[3,2,2,576,768]{4,3,2,1,0:T(8,128)(2,1)}, f32[16,768]{1,0:T(8,128)}, f32[16,768]{1,0:T(8,128)}, f...) custom-call(bf16[2,576,768]{2,1,0:T(8,128)(2,1)} %convert_element_ty, ...), custom_call_target="tpu_custom_call" | custom-call | tf_op jit(solution)/shard_map/gather/pallas_call | solution.py:887
  78.8 1.4 slice_reduce_fusion
  80.3 1.7 fusion.65
  82.0 1.6 fusion.66
  83.6 1.6 fusion.64
  85.3 0.9 pad_maximum_fusion.qkv
  86.4 0.6 reduce_sum.271.refs_22_
  87.1 77.5 %attend_forward.2 = (bf16[1,2,64,768]{3,2,1,0:T(8,128)(2,1)}, bf16[3,2,512,128]{3,2,1,0:T(8,128)(2,1)}, f32[128,128]{1,0:T(8,128)}, f32[128,128]{1,0:T(8,128)}, ...) custom-call(bf16[3,2,64,768]{3,2,1,0:T(8,128)(2,1)} %pad_maximum_fus, ...), custom_call_target="tpu_custom_call" | custom-call | tf_op jit(solution)/shard_map/attend_forward/pallas_call | solution.py:562
  164.6 1.8 fusion.84
  166.8 4.1 multiply_convert_fusion.1
  171.0 3.6 fusion.85
  174.9 0.3 fusion.68
  175.3 0.3 fusion.67
  175.6 0.3 convolution_convert_fusion.2
  175.9 0.9 pad_maximum_fusion.1.qkv
  176.8 26.0 %attend_forward.3 = (bf16[1,2,64,768]{3,2,1,0:T(8,128)(2,1)}, bf16[3,2,512,128]{3,2,1,0:T(8,128)(2,1)}, f32[128,128]{1,0:T(8,128)}, f32[128,128]{1,0:T(8,128)}, ...) custom-call(bf16[3,2,64,768]{3,2,1,0:T(8,128)(2,1)} %pad_maximum_fus, ...), custom_call_target="tpu_custom_call" | custom-call | tf_op jit(solution)/shard_map/attend_forward/pallas_call | solution.py:562
  202.8 1.8 fusion.86
  205.1 4.2 multiply_convert_fusion
  209.3 3.6 fusion.87
  213.1 0.2 multiply_reduce_fusion.3
  213.3 0.7 bitcast_reduce_fusion.refs_21_
  214.1 1.0 fusion.81
  215.1 2.2 fusion.37.refs_13_
  217.3 0.9 multiply_reduce_fusion.11
  218.2 0.7 bitcast_reduce_fusion.1
  219.1 1.2 convolution_convert_fusion.1
  220.4 33.4 %attend_backward.1 = (bf16[3,2,64,768]{3,2,1,0:T(8,128)(2,1)}, f32[6,2,256]{2,1,0:T(2,128)}, f32[2,64,768]{2,1,0:T(8,128)}) custom-call(bf16[1,2,64,768]{3,2,1,0:T(8,128)(2,1)} %bitcast.154, f32[2,128]{1,0:T(2,128)} %pad.4.edges.refs_25_, f32[16,768]{1,0:T(8,128)} %get-tuple-element.69.lines.low, f32[2,64,768]{2,1,0:T(8,128)} %bitcast.134, ...), custom_call_target="tpu_custom_call" | custom-call | tf_op jit(solution)/shard_map/attend_backward/pallas_call | solution.py:593
  253.8 1.2 fusion.82
  254.9 1.8 fusion.69
  256.8 2.0 convolution_add_fusion.1
  258.7 1.9 multiply_reduce_fusion.10
  260.7 0.7 bitcast_reduce_fusion.3
  261.6 4.5 fusion.30.refs_2_
  266.2 0.9 multiply_reduce_fusion.9
  267.1 0.7 bitcast_reduce_fusion.5
  267.9 0.9 fusion.78
  268.8 1.2 convolution_convert_fusion
  270.0 188.1 %settle.1 = (f32[2,576,768]{2,1,0:T(8,128)}, f32[2,576,768]{2,1,0:T(8,128)}, f32[16,2,2,768]{3,2,1,0:T(2,128)}, f32[2,64,768]{2,1,0:T(8,128)}) custom-call(bf16[128,768]{1,0:T(8,128)(2,1)} %bitcast.145, bf16[128,768]{1,0:T(8,128)(2,1)} %bitcast.150, bf16[128,3072]{1,0:T(8,128)(2,1)} %copy-done.14, bf16[128,3072]{1,0:T(8,128)(2,1)} %copy-done.11, ...), custom_call_target="tpu_custom_call" | custom-call | tf_op jit(solution)/shard_map/settle/pallas_call | solution.py:1247
  458.1 1.8 finish.1
  460.0 8.7 %fusion.23 = (f32[1,2,576,768]{3,2,1,0:T(8,128)}, f32[1,2,576,768]{3,2,1,0:T(8,128)}) fusion(f32[2,576,768]{2,1,0:T(8,128)} %get-tuple-element.106, f32[1,2,576,768]{3,2,1,0:T(8,128)} %param.17, f32[1,2,576,768]{3,2,1,0:T(8,128)} %param.16), kind=kLoop, calls=%fused_computation.20 | loop fusion | flops 6193152 | bytes 17694720 | tf_op jit(solution)/shard_map/broadcast_in_dim | solution.py:1513
  468.6 0.7 copy-done.3
  469.3 4.4 fusion.77
  473.8 0.7 copy.26
  474.5 0.7 copy.27
  (84 shorter events, 2.1 us)
Async XLA Ops:
  78.8 3.2 copy-start.17
  83.6 2.5 copy-start.18
  164.6 2.2 copy-start.20
  166.8 4.2 copy-start.4
  170.9 3.6 copy-start.11
  170.9 4.0 copy-start.2
  174.9 0.7 copy-start.5
  202.8 2.2 copy-start.19
  205.0 4.3 copy-start.6
  205.1 10.0 %slice-start.3 = ((s8[10616832]{0:T(1024)(128)(4,1)}), s8[4194304]{0:T(1024)(128)(4,1)S(1)}, s32[]{:S(2)}) async-start(s8[10616832]{0:T(1024)(128)(4,1)} %bitcast.176), calls=%async_computation.3 | async-start | bytes 8388608
  205.1 10.0 %slice-start.4 = ((s8[10616832]{0:T(1024)(128)(4,1)}), s8[4194304]{0:T(1024)(128)(4,1)S(1)}, s32[]{:S(2)}) async-start(s8[10616832]{0:T(1024)(128)(4,1)} %bitcast.176), calls=%async_computation.4 | async-start | bytes 8388608
  209.3 3.6 copy-start.12
  209.3 5.7 %slice-start.5 = ((s8[10616832]{0:T(1024)(128)(4,1)}), s8[2228224]{0:T(1024)(128)(4,1)S(1)}, s32[]{:S(2)}) async-start(s8[10616832]{0:T(1024)(128)(4,1)} %bitcast.176), calls=%async_computation.5 | async-start | bytes 4456448
  215.0 2.2 copy-start.7
  217.3 1.0 copy-start.13
  219.1 34.6 %copy-start.8 = (bf16[128,768]{1,0:T(8,128)(2,1)}, bf16[128,768]{1,0:T(8,128)(2,1)S(1)}, u32[]{:S(2)}) copy-start(bf16[128,768]{1,0:T(8,128)(2,1)S(1)} %get-tuple-element.159.refs_16_) | copy-start | bytes 589828
  256.8 9.4 %slice-start = ((s8[10616832]{0:T(1024)(128)(4,1)}), s8[4194304]{0:T(1024)(128)(4,1)S(1)}, s32[]{:S(2)}) async-start(s8[10616832]{0:T(1024)(128)(4,1)} %bitcast.169), calls=%async_computation | async-start | bytes 8388608
  261.4 4.7 slice-start.1
  261.6 4.5 copy-start.9
  261.6 4.5 slice-start.2
  266.1 1.0 copy-start.14
  268.8 1.2 copy-start.10
  459.9 8.7 %copy-start = (f32[2,576,768]{2,1,0:T(8,128)S(1)}, f32[2,576,768]{2,1,0:T(8,128)}, u32[]{:S(2)}) copy-start(f32[2,576,768]{2,1,0:T(8,128)} %refs_42_.1) | copy-start | bytes 10616836
  459.9 8.7 %copy-start.1 = (f32[2,576,768]{2,1,0:T(8,128)S(1)}, f32[2,576,768]{2,1,0:T(8,128)}, u32[]{:S(2)}) copy-start(f32[2,576,768]{2,1,0:T(8,128)} %param.20) | copy-start | bytes 10616836
  459.9 9.4 %copy-start.3 = (f32[2,576,768]{2,1,0:T(8,128)S(1)}, f32[2,576,768]{2,1,0:T(8,128)}, u32[]{:S(2)}) copy-start(f32[2,576,768]{2,1,0:T(8,128)} %get-tuple-element.110) | copy-start | bytes 10616836
  469.3 4.4 copy-start.15
  469.3 5.2 %copy-start.16 = (f32[2,64,768]{2,1,0:T(8,128)S(1)}, f32[2,64,768]{2,1,0:T(8,128)}, u32[]{:S(2)}) copy-start(f32[2,64,768]{2,1,0:T(8,128)} %get-tuple-element.105) | copy-start | bytes 1179652
